TPU v7x, 128 devices: a whole 4x4x4 slice. The times are simulated.
128 devices in a mesh: blk: 32 (over z_hi, y, x), head: 4 (over z_lo, core).
Axes of the slice: x: 4, y: 4, z: 4 (z_hi: 2, z_lo: 2; z = z_hi * 2 + z_lo), core: 2. Of those that a mesh axis runs over, the one named last changes fastest.
Arguments:
- tokens: bfloat16 [12288, 1024], P(('blk', 'head')), may hold values from -18 to 18
- block_order: int32 [64], replicated, may hold values from 0 to 63, as said below
- request_lengths: int32 [9], replicated, may hold values from 1 to 9216, 12288 in all
- enc_lengths: int32 [9], replicated, may hold values from 1 to 512, 2048 in all
- w_qkv: bfloat16 [3, 1024, 1024], P(None, None, 'head'), may hold values from -0.1875 to 0.1875
- w_out: bfloat16 [1024, 1024], P('head'), may hold values from -0.1875 to 0.1875
- enc_kv: bfloat16 [2, 2048, 1024], P(None, 'blk', 'head'), may hold values from -18 to 18
- w_cq: bfloat16 [1024, 1024], replicated, may hold values from -0.1875 to 0.1875
- w_co: bfloat16 [1024, 1024], replicated, may hold values from -0.1875 to 0.1875
- w_up: bfloat16 [1024, 4096], replicated, may hold values from -0.1875 to 0.1875
- w_down: bfloat16 [4096, 1024], replicated, may hold values from -0.09375 to 0.09375
- w_next: bfloat16 [3, 1024, 1024], P(None, None, 'head'), may hold values from -0.1875 to 0.1875
Outputs:
- output: float32 [12288, 1024], P(('blk', 'head'))
- cache: bfloat16 [2, 12288, 1024], P(None, 'blk', 'head')
- next_qkv: float32 [3, 12288, 1024], P(None, 'blk', 'head')
Inputs may be any that keep to these rules, and one draw needn't show every extreme that they name: `block_order`: each half-block index appears once, and stored half-blocks 2i and 2i + 1 hold position blocks that add up to 63. `request_lengths`: the lengths sum to 12288. `enc_lengths`: the lengths sum to 2048.
All inputs are finite; a program needn't handle non-finite values.
Results may differ from a plain program's by a relative error of at most 0.024.
Values may be sent and summed in bfloat16 or wider, within the bound.
A program may use at most 128 MiB of HBM per device.

v0:
```python
import functools
import math

import jax
import jax.numpy as jnp
from jax import lax
from jax.experimental import pallas as pl
from jax.experimental.pallas import tpu as pltpu
from jax.sharding import PartitionSpec as P

HEADS = 16


NEGATIVE = -1e30
SCALING = 0.125
EPSILON = 1e-05


def normalize(matrix):
    center = matrix - jnp.mean(matrix, axis=-1, keepdims=True)
    return center * lax.rsqrt(jnp.mean(center * center, axis=-1, keepdims=True) + EPSILON)


def position_of(order_table, indices, halfway):
    slots = jnp.arange(order_table.shape[0], dtype=jnp.int32)
    picked = jnp.sum(
        jnp.where((indices // halfway)[:, None] == slots[None, :], order_table[None, :], 0), axis=1
    )
    return picked * halfway + indices % halfway


def group_of(places, lengths):
    ends = jnp.cumsum(lengths)
    return jnp.sum((places[:, None] >= ends[None, :]).astype(jnp.int32), axis=1)


def online_update(carried, queries, key_rows, value_rows, visible):
    maxima, totals, running = carried
    heads_here = queries.shape[1]
    key_split = key_rows.reshape(key_rows.shape[0], heads_here, -1)
    value_split = value_rows.reshape(value_rows.shape[0], heads_here, -1)
    scores = (
        jnp.einsum("qhd,khd->qhk", queries, key_split, preferred_element_type=jnp.float32) * SCALING
    )
    scores = jnp.where(visible[:, None, :], scores, NEGATIVE)
    updated = jnp.maximum(maxima, jnp.max(scores, axis=2))
    factor = jnp.exp(maxima - updated)
    weights = jnp.exp(scores - updated[:, :, None])
    totals = totals * factor + jnp.sum(weights, axis=2)
    running = running * factor[:, :, None] + jnp.einsum(
        "qhk,khd->qhd",
        weights.astype(jnp.bfloat16),
        value_split,
        preferred_element_type=jnp.float32,
    )
    return (updated, totals, running)


def sweep(
    carried, queries, key_rows, value_rows, key_places, key_groups, query_places, query_groups
):
    length = key_rows.shape[0]
    block_size = math.gcd(length, 2048)
    blocks_count = length // block_size
    key_blocks = key_rows.reshape(blocks_count, block_size, key_rows.shape[1])
    value_blocks = value_rows.reshape(blocks_count, block_size, value_rows.shape[1])
    group_blocks = key_groups.reshape(blocks_count, block_size)
    if key_places is None:
        place_blocks = group_blocks
    else:
        place_blocks = key_places.reshape(blocks_count, block_size)

    def advance(status, element):
        key_block, value_block, place_block, group_block = element
        visible = group_block[None, :] == query_groups[:, None]
        if key_places is None:
            return (online_update(status, queries, key_block, value_block, visible), None)
        visible = visible & (place_block[None, :] <= query_places[:, None])
        updated = online_update(status, queries, key_block, value_block, visible)
        return (updated, None)

    carried, unused = lax.scan(
        advance, carried, (key_blocks, value_blocks, place_blocks, group_blocks)
    )
    return carried


def empty_state(count_q, heads_here, head_width):
    return (
        jnp.full((count_q, heads_here), NEGATIVE, jnp.float32),
        jnp.zeros((count_q, heads_here), jnp.float32),
        jnp.zeros((count_q, heads_here, head_width), jnp.float32),
    )


def finish(carried):
    maxima, totals, running = carried
    return (running / totals[:, :, None]).reshape(running.shape[0], -1).astype(jnp.bfloat16)


def flash_kernel(
    steps_ref, sources_ref, bases_ref, q_ref, low_ref, high_ref, k_hbm, v_hbm, o_ref,
    kbuf, vbuf, sem, qm_sc, m_sc, l_sc, acc_sc, *, max_steps, heads, head_width
):
    half = pl.program_id(0)
    count = steps_ref[half]
    tile = kbuf.shape[1] // 2
    width = kbuf.shape[2]

    def copies(step, slot):
        result = []
        for j in range(2):
            source = pl.multiple_of(sources_ref[(half * max_steps + step) * 2 + j], tile)
            window = pl.ds(j * tile, tile)
            result.append(pltpu.make_async_copy(
                k_hbm.at[pl.ds(source, tile)], kbuf.at[slot, window], sem.at[0, slot, j]))
            result.append(pltpu.make_async_copy(
                v_hbm.at[pl.ds(source, tile)], vbuf.at[slot, window], sem.at[1, slot, j]))
        return result

    for copy in copies(0, 0):
        copy.start()
    column_head = lax.broadcasted_iota(jnp.int32, (1, width), 1) // head_width
    q = q_ref[0]
    for h in range(heads):
        qm_sc[h] = jnp.where(column_head == h, q, jnp.zeros_like(q))
    m_sc[...] = jnp.full(m_sc.shape, NEGATIVE, jnp.float32)
    l_sc[...] = jnp.zeros(l_sc.shape, jnp.float32)
    acc_sc[...] = jnp.zeros(acc_sc.shape, jnp.float32)
    low = low_ref[0]
    high = high_ref[0]

    def body(step, carry):
        slot = step % 2
        for copy in copies(step, slot):
            copy.wait()

        @pl.when(step + 1 < count)
        def _():
            for copy in copies(step + 1, 1 - slot):
                copy.start()

        base = bases_ref[half * max_steps + step]
        places = base + lax.broadcasted_iota(jnp.int32, (1, 2 * tile), 1)
        visible = (places >= low) & (places <= high)
        keys = kbuf[slot]
        values = vbuf[slot]
        for h in range(heads):
            scores = lax.dot_general(
                qm_sc[h], keys, (((1,), (1,)), ((), ())), preferred_element_type=jnp.float32
            ) * SCALING
            scores = jnp.where(visible, scores, NEGATIVE)
            previous = m_sc[h]
            updated = jnp.maximum(previous, jnp.max(scores, axis=1, keepdims=True))
            factor = jnp.exp(previous - updated)
            weights = jnp.exp(scores - updated)
            l_sc[h] = l_sc[h] * factor + jnp.sum(weights, axis=1, keepdims=True)
            acc_sc[h] = acc_sc[h] * factor + jnp.dot(
                weights.astype(jnp.bfloat16), values, preferred_element_type=jnp.float32
            )
            m_sc[h] = updated
        return carry

    lax.fori_loop(0, count, body, 0)
    out = jnp.zeros(acc_sc.shape[1:], jnp.float32)
    for h in range(heads):
        out = jnp.where(column_head == h, acc_sc[h] / l_sc[h], out)
    o_ref[0] = out.astype(o_ref.dtype)


def flash(queries, low, high, keys, values, steps, sources, bases, max_steps, heads):
    halves, tile, width = queries.shape
    head_width = width // heads
    kernel = functools.partial(
        flash_kernel, max_steps=max_steps, heads=heads, head_width=head_width
    )
    row_spec = pl.BlockSpec((1, tile, width), lambda h, *refs: (h, 0, 0))
    bound_spec = pl.BlockSpec((1, tile, 1), lambda h, *refs: (h, 0, 0))
    flops = 4 * halves * max_steps * tile * 2 * tile * width * heads
    return pl.pallas_call(
        kernel,
        out_shape=jax.ShapeDtypeStruct(queries.shape, jnp.bfloat16),
        grid_spec=pltpu.PrefetchScalarGridSpec(
            num_scalar_prefetch=3,
            grid=(halves,),
            in_specs=[
                row_spec,
                bound_spec,
                bound_spec,
                pl.BlockSpec(memory_space=pl.ANY),
                pl.BlockSpec(memory_space=pl.ANY),
            ],
            out_specs=row_spec,
            scratch_shapes=[
                pltpu.VMEM((2, 2 * tile, width), keys.dtype),
                pltpu.VMEM((2, 2 * tile, width), values.dtype),
                pltpu.SemaphoreType.DMA((2, 2, 2)),
                pltpu.VMEM((heads, tile, width), jnp.bfloat16),
                pltpu.VMEM((heads, tile, 1), jnp.float32),
                pltpu.VMEM((heads, tile, 1), jnp.float32),
                pltpu.VMEM((heads, tile, width), jnp.float32),
            ],
        ),
        compiler_params=pltpu.CompilerParams(dimension_semantics=("arbitrary",)),
        cost_estimate=pl.CostEstimate(
            flops=flops,
            transcendentals=halves * max_steps * tile * 2 * tile * heads,
            bytes_accessed=halves * max_steps * 2 * 2 * tile * width * 2,
        ),
    )(steps, sources, bases, queries, low, high, keys, values)


def single_kernel(
    steps_ref, sources_ref, bases_ref, q_ref, low_ref, high_ref, kv_hbm, o_ref,
    buf, sem, m_sc, l_sc, acc_sc, *, max_steps, head_width, pieces
):
    half = pl.program_id(0)
    count = steps_ref[half]
    tile = buf.shape[1] // pieces

    def copies(step, slot):
        result = []
        for j in range(pieces):
            source = pl.multiple_of(sources_ref[(half * max_steps + step) * pieces + j], tile)
            result.append(pltpu.make_async_copy(
                kv_hbm.at[pl.ds(source, tile)], buf.at[slot, pl.ds(j * tile, tile)], sem.at[slot, j]))
        return result

    for copy in copies(0, 0):
        copy.start()
    m_sc[...] = jnp.full(m_sc.shape, NEGATIVE, jnp.float32)
    l_sc[...] = jnp.zeros(l_sc.shape, jnp.float32)
    acc_sc[...] = jnp.zeros(acc_sc.shape, jnp.float32)
    q = q_ref[0]
    low = low_ref[0]
    high = high_ref[0]

    def body(step, carry):
        slot = step % 2
        for copy in copies(step, slot):
            copy.wait()

        @pl.when(step + 1 < count)
        def _():
            for copy in copies(step + 1, 1 - slot):
                copy.start()

        base = bases_ref[half * max_steps + step]
        places = base + lax.broadcasted_iota(jnp.int32, (1, pieces * tile), 1)
        visible = (places >= low) & (places <= high)
        block = buf[slot]
        keys = block[:, :head_width]
        values = block[:, head_width:]
        scores = lax.dot_general(
            q, keys, (((1,), (1,)), ((), ())), preferred_element_type=jnp.float32
        ) * SCALING
        scores = jnp.where(visible, scores, NEGATIVE)
        previous = m_sc[...]
        updated = jnp.maximum(previous, jnp.max(scores, axis=1, keepdims=True))
        factor = jnp.exp(previous - updated)
        weights = jnp.exp(scores - updated)
        l_sc[...] = l_sc[...] * factor + jnp.sum(weights, axis=1, keepdims=True)
        acc_sc[...] = acc_sc[...] * factor + jnp.dot(
            weights.astype(jnp.bfloat16), values, preferred_element_type=jnp.float32
        )
        m_sc[...] = updated
        return carry

    lax.fori_loop(0, count, body, 0)
    o_ref[0] = (acc_sc[...] / l_sc[...]).astype(o_ref.dtype)


def single(queries, low, high, packed, steps, sources, bases, max_steps, pieces):
    halves, tile, head_width = queries.shape
    kernel = functools.partial(
        single_kernel, max_steps=max_steps, head_width=head_width, pieces=pieces
    )
    row_spec = pl.BlockSpec((1, tile, head_width), lambda h, *refs: (h, 0, 0))
    bound_spec = pl.BlockSpec((1, tile, 1), lambda h, *refs: (h, 0, 0))
    return pl.pallas_call(
        kernel,
        out_shape=jax.ShapeDtypeStruct(queries.shape, jnp.bfloat16),
        grid_spec=pltpu.PrefetchScalarGridSpec(
            num_scalar_prefetch=3,
            grid=(halves,),
            in_specs=[row_spec, bound_spec, bound_spec, pl.BlockSpec(memory_space=pl.ANY)],
            out_specs=row_spec,
            scratch_shapes=[
                pltpu.VMEM((2, pieces * tile, packed.shape[1]), packed.dtype),
                pltpu.SemaphoreType.DMA((2, pieces)),
                pltpu.VMEM((tile, 1), jnp.float32),
                pltpu.VMEM((tile, 1), jnp.float32),
                pltpu.VMEM((tile, head_width), jnp.float32),
            ],
        ),
        compiler_params=pltpu.CompilerParams(dimension_semantics=("arbitrary",)),
        cost_estimate=pl.CostEstimate(
            flops=2 * halves * (max_steps // 2) * tile * pieces * tile * head_width * 2,
            transcendentals=halves * (max_steps // 2) * tile * pieces * tile,
            bytes_accessed=halves * (max_steps // 2) * pieces * tile * packed.shape[1] * 2,
        ),
    )(steps, sources, bases, queries, low, high, packed)


def on_device(
    tokens,
    block_order,
    request_lengths,
    enc_lengths,
    w_qkv,
    w_out,
    enc_kv,
    w_cq,
    w_co,
    w_up,
    w_down,
    w_next,
):
    rows_here = tokens.shape[0]
    model_width = tokens.shape[1]
    group_size = lax.axis_size("head")
    cycle_size = lax.axis_size("zy") * lax.axis_size("x")
    block_rows = rows_here * group_size
    halfway = block_rows // 2
    group_width = w_qkv.shape[2]
    head_width = model_width // HEADS
    group_heads = group_width // head_width
    member = lax.axis_index("head")
    ring_size = lax.axis_size("x")
    ring_index = lax.axis_index("x")
    cycle_index = lax.axis_index("zy") * ring_size + ring_index
    encoder = lax.all_gather(enc_kv, ("zy", "x"), axis=1, tiled=True)
    gathered = lax.all_gather(tokens, "head", axis=0, tiled=True)
    projected = jnp.einsum(
        "td,cde->cte", gathered, w_qkv, preferred_element_type=jnp.float32
    ).astype(jnp.bfloat16)
    block_start = cycle_index * block_rows
    query_places = position_of(
        block_order, block_start + jnp.arange(block_rows, dtype=jnp.int32), halfway
    )
    query_groups = group_of(query_places, request_lengths)
    slots = jnp.arange(2 * cycle_size, dtype=jnp.int32)
    holders = jnp.sum(jnp.where(block_order[:, None] == slots[None, :], slots[:, None], 0), axis=0)
    per_head = projected.reshape(3, block_rows, group_heads, head_width).transpose(2, 1, 0, 3)
    per_head = per_head.reshape(group_heads, block_rows, 3 * head_width)
    mine = lax.all_to_all(per_head, "x", 0, 0, tiled=True)
    packed = lax.all_gather(mine[:, :, head_width:], "zy", axis=0, tiled=True)
    packed = packed.reshape(cycle_size * block_rows, 2 * head_width)
    ends = jnp.cumsum(request_lengths).astype(jnp.int32)
    starts = ends - request_lengths
    halves_here = 2 * ring_size
    first_half = lax.axis_index("zy") * halves_here
    pair = lax.dynamic_slice_in_dim(block_order, first_half, halves_here, 0)
    first_request = group_of(pair * halfway, request_lengths)
    low_block = starts[first_request] // halfway
    pieces = 4
    self_steps = (pair - low_block) // pieces + 1
    self_max = (2 * cycle_size + pieces - 1) // pieces
    firsts = low_block[:, None] + pieces * jnp.arange(self_max, dtype=jnp.int32)[None, :]
    self_sources = holders[
        jnp.minimum(firsts[:, :, None] + jnp.arange(pieces, dtype=jnp.int32), 2 * cycle_size - 1)
    ] * halfway
    places_here = (pair[:, None] * halfway + jnp.arange(halfway, dtype=jnp.int32)[None, :])
    groups_here = group_of(places_here.reshape(-1), request_lengths)
    single_out = single(
        mine[:, :, :head_width].reshape(halves_here, halfway, head_width),
        starts[groups_here].reshape(halves_here, halfway, 1),
        places_here.reshape(halves_here, halfway, 1),
        packed,
        self_steps.astype(jnp.int32),
        self_sources.reshape(-1).astype(jnp.int32),
        (firsts * halfway).reshape(-1).astype(jnp.int32),
        self_max,
        pieces,
    )
    returned = lax.all_to_all(
        single_out.reshape(ring_size, block_rows, head_width), "x", 0, 0, tiled=True
    )
    attended = returned.transpose(1, 0, 2).reshape(block_rows, group_width)
    group_blocks = lax.axis_index("zy") * ring_size + jnp.arange(ring_size, dtype=jnp.int32)
    cache_rows = jnp.stack(
        [holders[2 * group_blocks], holders[2 * group_blocks + 1]], axis=1
    )
    cache_parts = jnp.stack(
        [
            jnp.concatenate(
                [
                    lax.dynamic_slice_in_dim(packed, cache_rows[i, 0] * halfway, halfway, 0),
                    lax.dynamic_slice_in_dim(packed, cache_rows[i, 1] * halfway, halfway, 0),
                ],
                axis=0,
            )
            for i in range(ring_size)
        ]
    )
    cache_heads = lax.all_to_all(cache_parts, "x", 0, 0, tiled=True)
    cache = cache_heads.reshape(group_heads, block_rows, 2, head_width).transpose(2, 1, 0, 3)
    cache = cache.reshape(2, block_rows, group_width)
    mixed = lax.psum_scatter(
        jnp.dot(attended, w_out, preferred_element_type=jnp.float32),
        "head",
        scatter_dimension=0,
        tiled=True,
    )
    hidden = normalize(mixed + tokens.astype(jnp.float32))
    hidden_b = hidden.astype(jnp.bfloat16)
    block_hidden = lax.all_gather(hidden_b, "head", axis=0, tiled=True)
    w_cq_group = lax.dynamic_slice_in_dim(w_cq, member * group_width, group_width, 1)
    cross_query = jnp.dot(
        block_hidden, w_cq_group, preferred_element_type=jnp.float32
    ).astype(jnp.bfloat16)
    encoder_rows = encoder.shape[1]
    cross_max = (encoder_rows + halfway - 1 + 2 * halfway - 1) // (2 * halfway)
    padded_encoder = jnp.pad(
        encoder, ((0, 0), (0, cross_max * 2 * halfway + halfway - encoder_rows), (0, 0))
    )
    enc_ends = jnp.cumsum(enc_lengths).astype(jnp.int32)
    enc_starts = enc_ends - enc_lengths
    edge_groups = query_groups.reshape(2, halfway)
    cross_base = (enc_starts[edge_groups[:, 0]] // halfway) * halfway
    cross_steps = (enc_ends[edge_groups[:, -1]] - cross_base + 2 * halfway - 1) // (2 * halfway)
    cross_firsts = jnp.minimum(
        cross_base[:, None] + 2 * halfway * jnp.arange(cross_max, dtype=jnp.int32)[None, :],
        padded_encoder.shape[1] - 2 * halfway,
    )
    cross_sources = jnp.stack([cross_firsts, cross_firsts + halfway], axis=-1)
    crossed_group = flash(
        cross_query.reshape(2, halfway, group_width),
        enc_starts[query_groups].reshape(2, halfway, 1),
        (enc_ends[query_groups] - 1).reshape(2, halfway, 1),
        padded_encoder[0],
        padded_encoder[1],
        cross_steps.astype(jnp.int32),
        cross_sources.reshape(-1).astype(jnp.int32),
        cross_firsts.reshape(-1).astype(jnp.int32),
        cross_max,
        group_heads,
    ).reshape(block_rows, group_width)
    exchanged = lax.all_to_all(
        crossed_group.reshape(group_size, rows_here, group_width), "head", 0, 0, tiled=True
    )
    crossed = exchanged.transpose(1, 0, 2).reshape(rows_here, model_width)
    summed = jnp.dot(crossed, w_co, preferred_element_type=jnp.float32)
    second = normalize(summed + hidden)
    second_b = second.astype(jnp.bfloat16)
    inner = jax.nn.gelu(
        jnp.dot(second_b, w_up, preferred_element_type=jnp.float32), approximate=False
    ).astype(jnp.bfloat16)
    output = normalize(jnp.dot(inner, w_down, preferred_element_type=jnp.float32) + second)
    output_b = output.astype(jnp.bfloat16)
    block_output = lax.all_gather(output_b, "head", axis=0, tiled=True)
    next_qkv = jnp.einsum("td,cde->cte", block_output, w_next, preferred_element_type=jnp.float32)
    return (output, cache, next_qkv)


def solution(mesh):
    ring = 4
    devices = mesh.devices.reshape(mesh.shape["blk"] // ring, ring, mesh.shape["head"])
    fine = jax.sharding.Mesh(devices, ("zy", "x", "head"))
    rows = ("zy", "x", "head")
    blocks = ("zy", "x")
    in_specs = (
        P(rows, None),
        P(),
        P(),
        P(),
        P(None, None, "head"),
        P("head", None),
        P(None, blocks, "head"),
        P(),
        P(),
        P(),
        P(),
        P(None, None, "head"),
    )
    out_specs = (P(rows, None), P(None, blocks, "head"), P(None, blocks, "head"))
    return jax.shard_map(
        on_device, mesh=fine, in_specs=in_specs, out_specs=out_specs, check_vma=False
    )
```

profile of v0, /device:TPU:11, one launch (start us, length us, event | category | flops | bytes accessed | tf_op | source)
XLA Modules:
  0.0 265.0 jit_solution(14681280732016845138)
XLA Ops:
  7.2 9.9 %all_gather.15 = bf16[384,1024]{1,0:T(8,128)(2,1)S(1)} all-gather(bf16[96,1024]{1,0:T(8,128)(2,1)} %param.12), channel_id=1, replica_groups=mesh['zy'=8,'x'=4,'head'=4] {'head'}, dimensions={0}, use_global_device_ids=true | all-gather | bytes 983040 | tf_op jit(solution)/shard_map/all_gather | solution.py:333
  17.1 2.4 convolution_convert_fusion
  19.6 12.4 %all_to_all.20 = bf16[4,384,192]{1,2,0:T(8,128)(2,1)S(1)} all-to-all(bf16[4,384,192]{1,2,0:T(8,128)(2,1)S(1)} %bitcast.104), channel_id=1, replica_groups=mesh['zy'=8,'x'=4,'head'=4] {'x'}, dimensions={0} | all-to-all | bytes 1179648 | tf_op jit(solution)/shard_map/all_to_all | solution.py:346
  36.5 4.4 %fusion.52 = s32[1536]{0:T(1024)S(1)} fusion(s32[]{:T(128)} %bitcast.14, s32[]{:T(128)} %bitcast.15, s32[]{:T(128)} %bitcast.16, s32[]{:T(128)} %bitcast.17, s32[]{:T(128)} %bitcast.18, s32[]{:T(128)} %bitcast.20, s32[]{:T(128)} %bitcast.19, s32[1536]{0:T(1024)S(1)} %convert_reduce_fusion), kind=kLoop, calls=%fused_computation.103 | loop fusion | flops 23040 | bytes 12316 | tf_op jit(solution)/shard_map/gather | solution.py:367
  41.0 1.2 select_select_fusion
  42.2 1.5 reshape.716.low_ref
  45.4 3.3 %gather_fusion.3 = s32[512]{0:T(512)S(1)} fusion(s32[64]{0:T(128)S(1)} %select_reduce_fusion.1, s32[1024]{0:T(1024)S(1)} %pad_clamp_fusion.2), kind=kCustom, calls=%fused_computation.3 | custom fusion | bytes 6144 | tf_op jit(solution)/shard_map/gather | solution.py:360
  53.2 43.3 %all-gather.3.cloned.1.call-done = bf16[32,384,128]{2,1,0:T(8,128)(2,1)} async-done(((bf16[4,384,128]{2,1,0:T(8,128)(2,1)}), bf16[32,384,128]{2,1,0:T(8,128)(2,1)}) %all-gather.3.cloned.1.call-update) | async-done | bytes 3145744 | tf_op jit(solution)/shard_map/all_gather | solution.py:347
  96.5 64.8 %shard_map.139 = bf16[8,192,64]{2,1,0:T(8,128)(2,1)} custom-call(s32[8]{0:T(128)} %get-tuple-element.25.steps_ref, s32[512]{0:T(512)} %broadcast_multiply_fusion.1.sources_ref, s32[128]{0:T(128)} %mul.195.bases_ref, bf16[8,192,64]{2,1,0:T(8,128)(2,1)} %bitcast.110, s32[8,192,1]{2,1,0:T(8,128)} %reshape.716.low_ref, s32[8,192,1]{2,1,0:T(8,128)} %iota_add_fusion.high_ref, ...), custom_call_target="tpu_custom_call" | custom-call | flops 2415919104 | bytes 12582912 | tf_op jit(solution)/shard_map/pallas_call | solution.py:280
  161.4 1.8 copy.61
  163.2 4.2 %all-to-all-start.1 = ((bf16[4,384,64]{1,2,0:T(8,128)(2,1)}), bf16[4,384,64]{1,2,0:T(8,128)(2,1)S(1)}, u32[]{:S(2)}, u32[]{:S(2)}) async-start(bf16[4,384,64]{1,2,0:T(8,128)(2,1)} %copy.61), calls=%async_computation.1 | async-start | bytes 393216 | tf_op jit(solution)/shard_map/all_to_all | solution.py:376
  172.7 1.6 fusion.108
  175.9 8.8 %fusion.60 = (s32[384]{0:T(512)S(1)}, s32[384]{0:T(512)S(1)}) fusion(s32[]{:T(128)} %bitcast.37, s32[]{:T(128)} %bitcast.38, s32[]{:T(128)} %bitcast.39, s32[]{:T(128)} %bitcast.40, s32[]{:T(128)} %bitcast.41, s32[]{:T(128)} %bitcast.43, s32[]{:T(128)} %bitcast.42, s32[384]{0:T(512)S(1)} %convert_reduce_fusion.1, s32[]{:T(128)} %bitcast.34, s32[]{:T(128)} %bitcast.33, ...), kind=kLoop, calls=%fused_computation.158 | loop fusion | flops 8064 | bytes 4664 | tf_op jit(solution)/shard_map/gather | solution.py:430
  184.8 2.6 select_add_fusion
  192.7 3.2 %fusion.11 = (bf16[2496,256]{1,0:T(8,128)(2,1)}, bf16[2496,256]{1,0:T(8,128)(2,1)}) fusion(bf16[2,2048,256]{2,1,0:T(8,128)(2,1)} %all-gather.5.cloned.1.call-done), kind=kLoop, calls=%fused_computation.30 | loop fusion | bytes 4653056 | tf_op jit(solution)/shard_map/squeeze | solution.py:432
  197.8 4.2 %all-to-all-start.3 = ((bf16[4,384,128]{2,1,0:T(8,128)(2,1)}), bf16[4,384,128]{2,1,0:T(8,128)(2,1)S(1)}, u32[]{:S(2)}, u32[]{:S(2)}) async-start(bf16[4,384,128]{2,1,0:T(8,128)(2,1)} %pad_maximum_fusion), calls=%async_computation.4 | async-start | bytes 786432 | tf_op jit(solution)/shard_map/all_to_all | solution.py:396
  205.5 10.3 %all_gather.17 = bf16[384,1024]{1,0:T(8,128)(2,1)S(1)} all-gather(bf16[96,1024]{1,0:T(8,128)(2,1)S(1)} %multiply_convert_fusion.1), channel_id=1, replica_groups=mesh['zy'=8,'x'=4,'head'=4] {'head'}, dimensions={0}, use_global_device_ids=true | all-gather | bytes 983040 | tf_op jit(solution)/shard_map/all_gather | solution.py:407
  215.9 2.1 convolution_convert_fusion.1
  217.9 8.2 %shard_map.140 = bf16[2,192,256]{2,1,0:T(8,128)(2,1)} custom-call(s32[2]{0:T(128)} %get-tuple-element.29.steps_ref, s32[24]{0:T(128)} %reshape.506.sources_ref, s32[12]{0:T(128)} %min.35.bases_ref, bf16[2,192,256]{2,1,0:T(8,128)(2,1)} %bitcast.113, s32[2,192,1]{2,1,0:T(8,128)} %reshape.717.low_ref, s32[2,192,1]{2,1,0:T(8,128)} %sub.86.high_ref, ...), custom_call_target="tpu_custom_call" | custom-call | flops 3623878656 | bytes 4718592 | tf_op jit(solution)/shard_map/pallas_call | solution.py:180
  226.2 4.3 %all-to-all-start.2 = ((bf16[4,96,256]{2,1,0:T(8,128)(2,1)}), bf16[4,96,256]{2,1,0:T(8,128)(2,1)}, u32[]{:S(2)}, u32[]{:S(2)}) async-start(bf16[4,96,256]{2,1,0:T(8,128)(2,1)} %bitcast.112), calls=%async_computation.3 | async-start | bytes 393216 | tf_op jit(solution)/shard_map/all_to_all | solution.py:439
  231.7 3.3 %all-to-all-done.2 = bf16[4,96,256]{2,1,0:T(8,128)(2,1)} async-done(((bf16[4,96,256]{2,1,0:T(8,128)(2,1)}), bf16[4,96,256]{2,1,0:T(8,128)(2,1)}, u32[]{:S(2)}, u32[]{:S(2)}) %all-to-all-start.2) | async-done | bytes 196640 | tf_op jit(solution)/shard_map/all_to_all | solution.py:439
  236.8 10.0 %fusion.107 = (f32[96]{0:T(128)S(1)}, f32[96,1024]{1,0:T(8,128)S(1)}) fusion(f32[96]{0:T(128)S(1)} %add_rsqrt_fusion.1, f32[96,1024]{1,0:T(8,128)S(1)} %get-tuple-element.81, f32[96]{0:T(128)S(1)} %broadcast_multiply_fusion.3, bf16[4096,1024]{1,0:T(8,128)(2,1)} %param.22, bf16[1024,4096]{1,0:T(8,128)(2,1)} %param.21), kind=kOutput, calls=%fused_computation.223 | convolution fusion | flops 1636859776 | bytes 17564800 | tf_op jit(solution)/shard_map/dot_general | solution.py:449
  247.9 8.7 %all_gather.19 = bf16[384,1024]{1,0:T(8,128)(2,1)S(1)} all-gather(bf16[96,1024]{1,0:T(8,128)(2,1)S(1)} %get-tuple-element.23), channel_id=1, replica_groups=mesh['zy'=8,'x'=4,'head'=4] {'head'}, dimensions={0}, use_global_device_ids=true | all-gather | bytes 983040 | tf_op jit(solution)/shard_map/all_gather | solution.py:451
  256.6 1.8 convolution_bitcast_fusion
  (107 shorter events, 27.2 us)
Async XLA Ops:
  7.2 228.8 %copy-start = (bf16[1024,1024]{1,0:T(8,128)(2,1)S(1)}, bf16[1024,1024]{1,0:T(8,128)(2,1)}, u32[]{:S(2)}) copy-start(bf16[1024,1024]{1,0:T(8,128)(2,1)} %param.20) | copy-start | bytes 6291460
  7.2 89.4 %all-gather.3.cloned.1.call-start = ((), (), s32[]{:S(2)}) async-start(), calls=%async_computation.5 | async-start | bytes 3538944 | tf_op jit(solution)/shard_map/all_gather | solution.py:347
  19.6 14.2 %copy-start.4 = (s32[64]{0:T(128)S(1)}, s32[64]{0:T(128)}, u32[]{:S(2)}) copy-start(s32[64]{0:T(128)} %param.13) | copy-start | bytes 772
  32.1 3.4 %copy-start.6 = (s32[9]{0:T(128)S(1)}, s32[9]{0:T(128)}, u32[]{:S(2)}) copy-start(s32[9]{0:T(128)} %param.14) | copy-start | bytes 112
  33.1 159.6 %all-gather.5.cloned.1.call-start = ((), (), s32[]{:S(2)}) async-start(), calls=%async_computation.7 | async-start | bytes 2162688 | tf_op jit(solution)/shard_map/all_gather | solution.py:332
  96.5 75.9 %copy-start.7 = (s32[9]{0:T(128)S(1)}, s32[9]{0:T(128)}, u32[]{:S(2)}) copy-start(s32[9]{0:T(128)} %param.15) | copy-start | bytes 112
  96.5 76.2 %copy-start.3 = (bf16[256,1024]{1,0:T(8,128)(2,1)S(1)}, bf16[256,1024]{1,0:T(8,128)(2,1)}, u32[]{:S(2)}) copy-start(bf16[256,1024]{1,0:T(8,128)(2,1)} %param.17) | copy-start | bytes 1572868
  163.2 9.5 %all-to-all-start.1 = ((bf16[4,384,64]{1,2,0:T(8,128)(2,1)}), bf16[4,384,64]{1,2,0:T(8,128)(2,1)S(1)}, u32[]{:S(2)}, u32[]{:S(2)}) async-start(bf16[4,384,64]{1,2,0:T(8,128)(2,1)} %copy.61), calls=%async_computation.1 | async-start | bytes 393216 | tf_op jit(solution)/shard_map/all_to_all | solution.py:376
  167.4 34.6 %reduce-scatter.2.cloned.1.call-start = ((), (), s32[]{:S(2)}) async-start(), calls=%async_computation.6 | async-start | bytes 1966080 | tf_op jit(solution)/shard_map/reduce_scatter | solution.py:399
  195.9 6.1 %copy-start.2 = (bf16[96,1024]{1,0:T(8,128)(2,1)S(1)}, bf16[96,1024]{1,0:T(8,128)(2,1)}, u32[]{:S(2)}) copy-start(bf16[96,1024]{1,0:T(8,128)(2,1)} %param.12) | copy-start | bytes 589828
  197.8 28.3 %all-to-all-start.3 = ((bf16[4,384,128]{2,1,0:T(8,128)(2,1)}), bf16[4,384,128]{2,1,0:T(8,128)(2,1)S(1)}, u32[]{:S(2)}, u32[]{:S(2)}) async-start(bf16[4,384,128]{2,1,0:T(8,128)(2,1)} %pad_maximum_fusion), calls=%async_computation.4 | async-start | bytes 786432 | tf_op jit(solution)/shard_map/all_to_all | solution.py:396
  226.1 9.8 %copy-start.1 = (f32[96,1024]{1,0:T(8,128)S(1)}, f32[96,1024]{1,0:T(8,128)}, u32[]{:S(2)}) copy-start(f32[96,1024]{1,0:T(8,128)} %reduce-scatter.2.cloned.1.call-done) | copy-start | bytes 1179652
  226.2 8.8 %all-to-all-start.2 = ((bf16[4,96,256]{2,1,0:T(8,128)(2,1)}), bf16[4,96,256]{2,1,0:T(8,128)(2,1)}, u32[]{:S(2)}, u32[]{:S(2)}) async-start(bf16[4,96,256]{2,1,0:T(8,128)(2,1)} %bitcast.112), calls=%async_computation.3 | async-start | bytes 393216 | tf_op jit(solution)/shard_map/all_to_all | solution.py:439
  246.8 9.8 %copy-start.5 = (bf16[3,1024,256]{2,1,0:T(8,128)(2,1)S(1)}, bf16[3,1024,256]{2,1,0:T(8,128)(2,1)}, u32[]{:S(2)}) copy-start(bf16[3,1024,256]{2,1,0:T(8,128)(2,1)} %param.23) | copy-start | bytes 4718596
Sparse Core Ops, SparseCore 0:
  33.2 63.3 all-gather.2
  99.6 68.6 all-gather.4
  174.5 22.9 reduce-scatter.1
where the time goes:
time: 270 us; the launch traced here: 265 us
  Pallas kernels  73 us (27%)
  waiting for transfers between devices  47.3 us (18%)
  blocking collectives  41.3 us (15%)
  other arithmetic  27.1 us (10%)
  local copies, waits for them, and re-layouts  25.7 us (10%)
  between operations  19.1 us (7%)
  matrix products  18.6 us (7%)
  starting transfers between devices  12.9 us (5%)
    pallas_call x1, Pallas kernels, single(): pl.pallas_call(kernel, out_shape=jax.ShapeDtypeStruct(queries.shape, jnp....  64.8 us
    all_gather x1, waiting for transfers between devices, on_device(): packed = lax.all_gather(mine[:, :, head_width:], 'zy', axis=0, tiled=True)  43.3 us
    all_to_all x1, blocking collectives, on_device(): mine = lax.all_to_all(per_head, 'x', 0, 0, tiled=True)  12.4 us
    all_gather x1, blocking collectives, on_device(): block_hidden = lax.all_gather(hidden_b, 'head', axis=0, tiled=True)  10.3 us
    dot_general x1, matrix products, on_device(): jnp.dot(inner, w_down, preferred_element_type=jnp.float32) + second  10 us
    all_gather x1, blocking collectives, on_device(): gathered = lax.all_gather(tokens, 'head', axis=0, tiled=True)  9.88 us
    gather x1, other arithmetic, on_device(): enc_ends[query_groups] - 1  8.84 us
    all_gather x1, blocking collectives, on_device(): block_output = lax.all_gather(output_b, 'head', axis=0, tiled=True)  8.7 us
  transfers between devices with their start and end apart: 6, of which 2 were waited for; matrix products, arithmetic and copies ran while one was open for 20% of the time, Pallas kernels for 28%

commit v1 on v0

--- a/solution.py
+++ b/solution.py
@@ -302,6 +302,63 @@
     )(steps, sources, bases, queries, low, high, packed)
 
 
+def exchange_kernel(src_ref, out_ref, land, send_sem, recv_sem, *, axis, count, gather):
+    me = lax.axis_index(axis)
+    mesh_kind = pl.DeviceIdType.MESH
+    barrier = pltpu.get_barrier_semaphore()
+    for k in range(1, count):
+        pl.semaphore_signal(
+            barrier, inc=1, device_id={axis: lax.rem(me + k, count)}, device_id_type=mesh_kind
+        )
+    pl.semaphore_wait(barrier, count - 1)
+    sends = []
+    for k in range(1, count):
+        peer = lax.rem(me + k, count)
+        copy = pltpu.make_async_remote_copy(
+            src_ref=src_ref if gather else src_ref.at[peer],
+            dst_ref=land.at[me],
+            send_sem=send_sem.at[k],
+            recv_sem=recv_sem.at[me],
+            device_id={axis: peer},
+            device_id_type=mesh_kind,
+        )
+        copy.start()
+        sends.append(copy)
+    land[me] = src_ref[...] if gather else src_ref[me]
+    for copy in sends:
+        copy.wait_send()
+    for k in range(1, count):
+        sender = lax.rem(me + count - k, count)
+        pltpu.make_async_remote_copy(
+            src_ref=src_ref if gather else src_ref.at[sender],
+            dst_ref=land.at[sender],
+            send_sem=send_sem.at[k],
+            recv_sem=recv_sem.at[sender],
+            device_id={axis: sender},
+            device_id_type=mesh_kind,
+        ).wait_recv()
+    out_ref[...] = land[...]
+
+
+def exchange(value, axis, gather, collective):
+    count = lax.axis_size(axis)
+    piece = value.shape if gather else value.shape[1:]
+    shape = (count,) + tuple(piece)
+    kernel = functools.partial(exchange_kernel, axis=axis, count=count, gather=gather)
+    return pl.pallas_call(
+        kernel,
+        out_shape=jax.ShapeDtypeStruct(shape, value.dtype),
+        in_specs=[pl.BlockSpec(memory_space=pltpu.VMEM)],
+        out_specs=pl.BlockSpec(memory_space=pltpu.VMEM),
+        scratch_shapes=[
+            pltpu.VMEM(shape, value.dtype),
+            pltpu.SemaphoreType.DMA((count,)),
+            pltpu.SemaphoreType.DMA((count,)),
+        ],
+        compiler_params=pltpu.CompilerParams(collective_id=collective, has_side_effects=True),
+    )(value)
+
+
 def on_device(
     tokens,
     block_order,
@@ -330,7 +387,7 @@
     ring_index = lax.axis_index("x")
     cycle_index = lax.axis_index("zy") * ring_size + ring_index
     encoder = lax.all_gather(enc_kv, ("zy", "x"), axis=1, tiled=True)
-    gathered = lax.all_gather(tokens, "head", axis=0, tiled=True)
+    gathered = exchange(tokens, "head", True, 0).reshape(block_rows, model_width)
     projected = jnp.einsum(
         "td,cde->cte", gathered, w_qkv, preferred_element_type=jnp.float32
     ).astype(jnp.bfloat16)
@@ -404,7 +461,7 @@
     )
     hidden = normalize(mixed + tokens.astype(jnp.float32))
     hidden_b = hidden.astype(jnp.bfloat16)
-    block_hidden = lax.all_gather(hidden_b, "head", axis=0, tiled=True)
+    block_hidden = exchange(hidden_b, "head", True, 0).reshape(block_rows, model_width)
     w_cq_group = lax.dynamic_slice_in_dim(w_cq, member * group_width, group_width, 1)
     cross_query = jnp.dot(
         block_hidden, w_cq_group, preferred_element_type=jnp.float32
@@ -448,7 +505,7 @@
     ).astype(jnp.bfloat16)
     output = normalize(jnp.dot(inner, w_down, preferred_element_type=jnp.float32) + second)
     output_b = output.astype(jnp.bfloat16)
-    block_output = lax.all_gather(output_b, "head", axis=0, tiled=True)
+    block_output = exchange(output_b, "head", True, 0).reshape(block_rows, model_width)
     next_qkv = jnp.einsum("td,cde->cte", block_output, w_next, preferred_element_type=jnp.float32)
     return (output, cache, next_qkv)
 

time: 270 us -> 280 us (1.037)
  the two profiles are of different devices: /device:TPU:11 before, /device:TPU:91 now
where the time goes in v1:
time: 280 us; the launch traced here: 275 us
  Pallas kernels  99.4 us (36%)
  waiting for transfers between devices  56.9 us (20%)
  other arithmetic  27.9 us (10%)
  local copies, waits for them, and re-layouts  25.6 us (9%)
  matrix products  20.6 us (7%)
  between operations  19.1 us (7%)
  blocking collectives  13.1 us (5%)
  starting transfers between devices  12.8 us (5%)
    pallas_call x1, Pallas kernels, single(): pl.pallas_call(kernel, out_shape=jax.ShapeDtypeStruct(queries.shape, jnp....  46.4 us
    pallas_call x3, Pallas kernels, exchange(): pl.pallas_call(kernel, out_shape=jax.ShapeDtypeStruct(shape, value.dtype)...  39.9 us
    all_gather x1, waiting for transfers between devices, on_device(): packed = lax.all_gather(mine[:, :, head_width:], 'zy', axis=0, tiled=True)  38.7 us
    reduce_scatter x1, waiting for transfers between devices, on_device(): lax.psum_scatter(jnp.dot(attended, w_out, preferred_element_type=jnp.floa...  14.8 us
    pallas_call x1, Pallas kernels, flash(): pl.pallas_call(kernel, out_shape=jax.ShapeDtypeStruct(queries.shape, jnp....  13.1 us
    all_to_all x1, blocking collectives, on_device(): mine = lax.all_to_all(per_head, 'x', 0, 0, tiled=True)  13.1 us
    dot_general x1, matrix products, on_device(): jnp.dot(inner, w_down, preferred_element_type=jnp.float32) + second  9.99 us
    gather x1, other arithmetic, on_device(): enc_ends[query_groups] - 1  8.84 us
  transfers between devices with their start and end apart: 6, of which 3 were waited for; matrix products, arithmetic and copies ran while one was open for 20% of the time, Pallas kernels for 26%

profile of v1, /device:TPU:91, one launch (start us, length us, event | category | flops | bytes accessed | tf_op | source)
XLA Modules:
  0.0 275.4 jit_solution(13374566683578326925)
XLA Ops:
  7.2 13.6 %shard_map.139 = bf16[4,96,1024]{2,1,0:T(8,128)(2,1)} custom-call(bf16[96,1024]{1,0:T(8,128)(2,1)} %src_ref.1), custom_call_target="tpu_custom_call" | custom-call | tf_op jit(solution)/shard_map/pallas_call | solution.py:348
  20.8 2.6 convolution_convert_fusion
  23.5 13.1 %all_to_all.20 = bf16[4,384,192]{1,2,0:T(8,128)(2,1)S(1)} all-to-all(bf16[4,384,192]{1,2,0:T(8,128)(2,1)S(1)} %bitcast.108), channel_id=1, replica_groups=mesh['zy'=8,'x'=4,'head'=4] {'x'}, dimensions={0} | all-to-all | bytes 1179648 | tf_op jit(solution)/shard_map/all_to_all | solution.py:403
  41.0 4.4 %fusion.50 = s32[1536]{0:T(1024)S(1)} fusion(s32[]{:T(128)} %bitcast.15, s32[]{:T(128)} %bitcast.16, s32[]{:T(128)} %bitcast.17, s32[]{:T(128)} %bitcast.18, s32[]{:T(128)} %bitcast.19, s32[]{:T(128)} %bitcast.21, s32[]{:T(128)} %bitcast.20, s32[1536]{0:T(1024)S(1)} %convert_reduce_fusion), kind=kLoop, calls=%fused_computation.101 | loop fusion | flops 23040 | bytes 12316 | tf_op jit(solution)/shard_map/gather | solution.py:424
  49.9 3.3 %gather_fusion.3 = s32[512]{0:T(512)S(1)} fusion(s32[64]{0:T(128)S(1)} %select_reduce_fusion.1, s32[1024]{0:T(1024)S(1)} %pad_clamp_fusion.2), kind=kCustom, calls=%fused_computation.3 | custom fusion | bytes 6144 | tf_op jit(solution)/shard_map/gather | solution.py:417
  57.7 38.7 %all-gather.3.cloned.1.call-done = bf16[32,384,128]{2,1,0:T(8,128)(2,1)} async-done(((bf16[4,384,128]{2,1,0:T(8,128)(2,1)}), bf16[32,384,128]{2,1,0:T(8,128)(2,1)}) %all-gather.3.cloned.1.call-update) | async-done | bytes 3145744 | tf_op jit(solution)/shard_map/all_gather | solution.py:404
  96.4 46.4 %shard_map.140 = bf16[8,192,64]{2,1,0:T(8,128)(2,1)} custom-call(s32[8]{0:T(128)} %get-tuple-element.25.steps_ref, s32[512]{0:T(512)} %broadcast_multiply_fusion.1.sources_ref, s32[128]{0:T(128)} %mul.195.bases_ref, bf16[8,192,64]{2,1,0:T(8,128)(2,1)} %bitcast.116, s32[8,192,1]{2,1,0:T(8,128)} %reshape.728.low_ref, s32[8,192,1]{2,1,0:T(8,128)} %iota_add_fusion.high_ref, ...), custom_call_target="tpu_custom_call" | custom-call | flops 2415919104 | bytes 12582912 | tf_op jit(solution)/shard_map/pallas_call | solution.py:280
  142.8 1.8 copy.61
  144.6 4.2 %all-to-all-start.1 = ((bf16[4,384,64]{1,2,0:T(8,128)(2,1)}), bf16[4,384,64]{1,2,0:T(8,128)(2,1)S(1)}, u32[]{:S(2)}, u32[]{:S(2)}) async-start(bf16[4,384,64]{1,2,0:T(8,128)(2,1)} %copy.61), calls=%async_computation.1 | async-start | bytes 393216 | tf_op jit(solution)/shard_map/all_to_all | solution.py:433
  154.1 1.6 fusion.106
  157.3 8.8 %fusion.58 = (s32[384]{0:T(512)S(1)}, s32[384]{0:T(512)S(1)}) fusion(s32[]{:T(128)} %bitcast.39, s32[]{:T(128)} %bitcast.40, s32[]{:T(128)} %bitcast.41, s32[]{:T(128)} %bitcast.42, s32[]{:T(128)} %bitcast.43, s32[]{:T(128)} %bitcast.45, s32[]{:T(128)} %bitcast.44, s32[384]{0:T(512)S(1)} %convert_reduce_fusion.1, s32[]{:T(128)} %bitcast.36, s32[]{:T(128)} %bitcast.35, ...), kind=kLoop, calls=%fused_computation.156 | loop fusion | flops 8064 | bytes 4664 | tf_op jit(solution)/shard_map/gather | solution.py:487
  166.2 2.6 select_add_fusion
  174.1 3.2 %fusion.11 = (bf16[2496,256]{1,0:T(8,128)(2,1)}, bf16[2496,256]{1,0:T(8,128)(2,1)}) fusion(bf16[2,2048,256]{2,1,0:T(8,128)(2,1)} %all-gather.5.cloned.1.call-done), kind=kLoop, calls=%fused_computation.30 | loop fusion | bytes 4653056 | tf_op jit(solution)/shard_map/squeeze | solution.py:489
  179.2 4.2 %all-to-all-start.3 = ((bf16[4,384,128]{2,1,0:T(8,128)(2,1)}), bf16[4,384,128]{2,1,0:T(8,128)(2,1)S(1)}, u32[]{:S(2)}, u32[]{:S(2)}) async-start(bf16[4,384,128]{2,1,0:T(8,128)(2,1)} %pad_maximum_fusion), calls=%async_computation.4 | async-start | bytes 786432 | tf_op jit(solution)/shard_map/all_to_all | solution.py:453
  183.4 14.8 %reduce-scatter.2.cloned.1.call-done = f32[96,1024]{1,0:T(8,128)} async-done(((f32[384,1024]{1,0:T(8,128)}), f32[96,1024]{1,0:T(8,128)}) %reduce-scatter.2.cloned.1.call-update) | async-done | bytes 393232 | tf_op jit(solution)/shard_map/reduce_scatter | solution.py:456
  200.6 1.8 multiply_convert_fusion.1.src_ref
  202.4 13.1 %shard_map.141 = bf16[4,96,1024]{2,1,0:T(8,128)(2,1)} custom-call(bf16[96,1024]{1,0:T(8,128)(2,1)} %multiply_convert_fusion.1.src_ref), custom_call_target="tpu_custom_call" | custom-call | tf_op jit(solution)/shard_map/pallas_call | solution.py:348
  215.5 2.3 convolution_convert_fusion.1
  217.8 13.1 %shard_map.142 = bf16[2,192,256]{2,1,0:T(8,128)(2,1)} custom-call(s32[2]{0:T(128)} %get-tuple-element.29.steps_ref, s32[24]{0:T(128)} %reshape.515.sources_ref, s32[12]{0:T(128)} %min.35.bases_ref, bf16[2,192,256]{2,1,0:T(8,128)(2,1)} %bitcast.119, s32[2,192,1]{2,1,0:T(8,128)} %reshape.729.low_ref, s32[2,192,1]{2,1,0:T(8,128)} %sub.86.high_ref, ...), custom_call_target="tpu_custom_call" | custom-call | flops 3623878656 | bytes 4718592 | tf_op jit(solution)/shard_map/pallas_call | solution.py:180
  230.9 4.3 %all-to-all-start.2 = ((bf16[4,96,256]{2,1,0:T(8,128)(2,1)}), bf16[4,96,256]{2,1,0:T(8,128)(2,1)}, u32[]{:S(2)}, u32[]{:S(2)}) async-start(bf16[4,96,256]{2,1,0:T(8,128)(2,1)} %bitcast.118), calls=%async_computation.3 | async-start | bytes 393216 | tf_op jit(solution)/shard_map/all_to_all | solution.py:496
  236.4 2.7 all-to-all-done.2
  240.9 10.0 %fusion.105 = (f32[96]{0:T(128)S(1)}, f32[96,1024]{1,0:T(8,128)S(1)}) fusion(f32[96]{0:T(128)S(1)} %add_rsqrt_fusion.1, f32[96,1024]{1,0:T(8,128)S(1)} %get-tuple-element.81, f32[96]{0:T(128)S(1)} %broadcast_multiply_fusion.3, bf16[4096,1024]{1,0:T(8,128)(2,1)} %param.22, bf16[1024,4096]{1,0:T(8,128)(2,1)} %param.21), kind=kOutput, calls=%fused_computation.221 | convolution fusion | flops 1636859776 | bytes 17564800 | tf_op jit(solution)/shard_map/dot_general | solution.py:506
  252.1 13.3 %shard_map.143 = bf16[4,96,1024]{2,1,0:T(8,128)(2,1)} custom-call(bf16[96,1024]{1,0:T(8,128)(2,1)} %get-tuple-element.23.src_ref), custom_call_target="tpu_custom_call" | custom-call | tf_op jit(solution)/shard_map/pallas_call | solution.py:348
  265.4 3.4 %convolution_bitcast_fusion = f32[3,384,256]{2,1,0:T(8,128)} fusion(bf16[384,1024,1]{1,0,2:T(8,128)(2,1)} %bitcast.113, bf16[3,1024,256]{2,1,0:T(8,128)(2,1)} %param.23), kind=kOutput, calls=%fused_computation.27 | convolution fusion | flops 603979776 | bytes 3538944 | tf_op jit(solution)/shard_map/td,cde->cte/dot_general | solution.py:509
  (105 shorter events, 28.9 us)
Async XLA Ops:
  7.2 232.9 %copy-start = (bf16[1024,1024]{1,0:T(8,128)(2,1)S(1)}, bf16[1024,1024]{1,0:T(8,128)(2,1)}, u32[]{:S(2)}) copy-start(bf16[1024,1024]{1,0:T(8,128)(2,1)} %param.20) | copy-start | bytes 6291460
  7.2 89.2 %all-gather.3.cloned.1.call-start = ((), (), s32[]{:S(2)}) async-start(), calls=%async_computation.5 | async-start | bytes 3538944 | tf_op jit(solution)/shard_map/all_gather | solution.py:404
  23.5 14.9 %copy-start.4 = (s32[64]{0:T(128)S(1)}, s32[64]{0:T(128)}, u32[]{:S(2)}) copy-start(s32[64]{0:T(128)} %param.13) | copy-start | bytes 772
  36.6 3.4 %copy-start.5 = (s32[9]{0:T(128)S(1)}, s32[9]{0:T(128)}, u32[]{:S(2)}) copy-start(s32[9]{0:T(128)} %param.14) | copy-start | bytes 112
  37.6 136.5 %all-gather.5.cloned.1.call-start = ((), (), s32[]{:S(2)}) async-start(), calls=%async_computation.7 | async-start | bytes 2162688 | tf_op jit(solution)/shard_map/all_gather | solution.py:389
  96.4 57.4 %copy-start.6 = (s32[9]{0:T(128)S(1)}, s32[9]{0:T(128)}, u32[]{:S(2)}) copy-start(s32[9]{0:T(128)} %param.15) | copy-start | bytes 112
  96.4 57.7 %copy-start.3 = (bf16[256,1024]{1,0:T(8,128)(2,1)S(1)}, bf16[256,1024]{1,0:T(8,128)(2,1)}, u32[]{:S(2)}) copy-start(bf16[256,1024]{1,0:T(8,128)(2,1)} %param.17) | copy-start | bytes 1572868
  144.6 9.5 %all-to-all-start.1 = ((bf16[4,384,64]{1,2,0:T(8,128)(2,1)}), bf16[4,384,64]{1,2,0:T(8,128)(2,1)S(1)}, u32[]{:S(2)}, u32[]{:S(2)}) async-start(bf16[4,384,64]{1,2,0:T(8,128)(2,1)} %copy.61), calls=%async_computation.1 | async-start | bytes 393216 | tf_op jit(solution)/shard_map/all_to_all | solution.py:433
  148.8 49.4 %reduce-scatter.2.cloned.1.call-start = ((), (), s32[]{:S(2)}) async-start(), calls=%async_computation.6 | async-start | bytes 1966080 | tf_op jit(solution)/shard_map/reduce_scatter | solution.py:456
  177.3 20.9 %copy-start.2 = (bf16[96,1024]{1,0:T(8,128)(2,1)S(1)}, bf16[96,1024]{1,0:T(8,128)(2,1)}, u32[]{:S(2)}) copy-start(bf16[96,1024]{1,0:T(8,128)(2,1)} %src_ref.1) | copy-start | bytes 589828
  179.2 51.7 %all-to-all-start.3 = ((bf16[4,384,128]{2,1,0:T(8,128)(2,1)}), bf16[4,384,128]{2,1,0:T(8,128)(2,1)S(1)}, u32[]{:S(2)}, u32[]{:S(2)}) async-start(bf16[4,384,128]{2,1,0:T(8,128)(2,1)} %pad_maximum_fusion), calls=%async_computation.4 | async-start | bytes 786432 | tf_op jit(solution)/shard_map/all_to_all | solution.py:453
  230.9 9.2 %copy-start.1 = (f32[96,1024]{1,0:T(8,128)S(1)}, f32[96,1024]{1,0:T(8,128)}, u32[]{:S(2)}) copy-start(f32[96,1024]{1,0:T(8,128)} %reduce-scatter.2.cloned.1.call-done) | copy-start | bytes 1179652
  230.9 8.2 %all-to-all-start.2 = ((bf16[4,96,256]{2,1,0:T(8,128)(2,1)}), bf16[4,96,256]{2,1,0:T(8,128)(2,1)}, u32[]{:S(2)}, u32[]{:S(2)}) async-start(bf16[4,96,256]{2,1,0:T(8,128)(2,1)} %bitcast.118), calls=%async_computation.3 | async-start | bytes 393216 | tf_op jit(solution)/shard_map/all_to_all | solution.py:496
Sparse Core Ops, SparseCore 0:
  37.7 58.6 all-gather.2
  99.4 69.1 all-gather.4
  171.0 27.1 reduce-scatter.1

commit v2 on v0

--- a/solution.py
+++ b/solution.py
@@ -32,6 +32,17 @@
 def group_of(places, lengths):
     ends = jnp.cumsum(lengths)
     return jnp.sum((places[:, None] >= ends[None, :]).astype(jnp.int32), axis=1)
+
+
+def prefix_below(places, bounds, amounts):
+    return jnp.sum(
+        jnp.where(places[..., None] >= bounds, amounts, 0), axis=-1
+    ).astype(jnp.int32)
+
+
+def lookup(table, indices):
+    slots = jnp.arange(table.shape[0], dtype=jnp.int32)
+    return jnp.sum(jnp.where(indices[..., None] == slots, table, 0), axis=-1).astype(jnp.int32)
 
 
 def online_update(carried, queries, key_rows, value_rows, visible):
@@ -338,7 +349,6 @@
     query_places = position_of(
         block_order, block_start + jnp.arange(block_rows, dtype=jnp.int32), halfway
     )
-    query_groups = group_of(query_places, request_lengths)
     slots = jnp.arange(2 * cycle_size, dtype=jnp.int32)
     holders = jnp.sum(jnp.where(block_order[:, None] == slots[None, :], slots[:, None], 0), axis=0)
     per_head = projected.reshape(3, block_rows, group_heads, head_width).transpose(2, 1, 0, 3)
@@ -351,20 +361,19 @@
     halves_here = 2 * ring_size
     first_half = lax.axis_index("zy") * halves_here
     pair = lax.dynamic_slice_in_dim(block_order, first_half, halves_here, 0)
-    first_request = group_of(pair * halfway, request_lengths)
-    low_block = starts[first_request] // halfway
+    low_block = prefix_below(pair * halfway, ends, request_lengths) // halfway
     pieces = 4
     self_steps = (pair - low_block) // pieces + 1
     self_max = (2 * cycle_size + pieces - 1) // pieces
     firsts = low_block[:, None] + pieces * jnp.arange(self_max, dtype=jnp.int32)[None, :]
-    self_sources = holders[
-        jnp.minimum(firsts[:, :, None] + jnp.arange(pieces, dtype=jnp.int32), 2 * cycle_size - 1)
-    ] * halfway
+    self_sources = lookup(
+        holders,
+        jnp.minimum(firsts[:, :, None] + jnp.arange(pieces, dtype=jnp.int32), 2 * cycle_size - 1),
+    ) * halfway
     places_here = (pair[:, None] * halfway + jnp.arange(halfway, dtype=jnp.int32)[None, :])
-    groups_here = group_of(places_here.reshape(-1), request_lengths)
     single_out = single(
         mine[:, :, :head_width].reshape(halves_here, halfway, head_width),
-        starts[groups_here].reshape(halves_here, halfway, 1),
+        prefix_below(places_here, ends, request_lengths).reshape(halves_here, halfway, 1),
         places_here.reshape(halves_here, halfway, 1),
         packed,
         self_steps.astype(jnp.int32),
@@ -378,8 +387,8 @@
     )
     attended = returned.transpose(1, 0, 2).reshape(block_rows, group_width)
     group_blocks = lax.axis_index("zy") * ring_size + jnp.arange(ring_size, dtype=jnp.int32)
-    cache_rows = jnp.stack(
-        [holders[2 * group_blocks], holders[2 * group_blocks + 1]], axis=1
+    cache_rows = lookup(
+        holders, jnp.stack([2 * group_blocks, 2 * group_blocks + 1], axis=1)
     )
     cache_parts = jnp.stack(
         [
@@ -414,11 +423,12 @@
     padded_encoder = jnp.pad(
         encoder, ((0, 0), (0, cross_max * 2 * halfway + halfway - encoder_rows), (0, 0))
     )
-    enc_ends = jnp.cumsum(enc_lengths).astype(jnp.int32)
-    enc_starts = enc_ends - enc_lengths
-    edge_groups = query_groups.reshape(2, halfway)
-    cross_base = (enc_starts[edge_groups[:, 0]] // halfway) * halfway
-    cross_steps = (enc_ends[edge_groups[:, -1]] - cross_base + 2 * halfway - 1) // (2 * halfway)
+    enc_low = prefix_below(query_places, ends, enc_lengths)
+    enc_high = prefix_below(query_places, starts, enc_lengths) - 1
+    cross_base = (enc_low.reshape(2, halfway)[:, 0] // halfway) * halfway
+    cross_steps = (enc_high.reshape(2, halfway)[:, -1] + 1 - cross_base + 2 * halfway - 1) // (
+        2 * halfway
+    )
     cross_firsts = jnp.minimum(
         cross_base[:, None] + 2 * halfway * jnp.arange(cross_max, dtype=jnp.int32)[None, :],
         padded_encoder.shape[1] - 2 * halfway,
@@ -426,8 +436,8 @@
     cross_sources = jnp.stack([cross_firsts, cross_firsts + halfway], axis=-1)
     crossed_group = flash(
         cross_query.reshape(2, halfway, group_width),
-        enc_starts[query_groups].reshape(2, halfway, 1),
-        (enc_ends[query_groups] - 1).reshape(2, halfway, 1),
+        enc_low.reshape(2, halfway, 1),
+        enc_high.reshape(2, halfway, 1),
         padded_encoder[0],
         padded_encoder[1],
         cross_steps.astype(jnp.int32),

time: 270 us -> 270 us (level)
  the two profiles are of different devices: /device:TPU:11 before, /device:TPU:7 now
where the time goes in v2:
time: 270 us; the launch traced here: 265 us
  waiting for transfers between devices  92.6 us (34%)
  Pallas kernels  55.1 us (20%)
  blocking collectives  39.1 us (14%)
  between operations  19 us (7%)
  matrix products  18.6 us (7%)
  local copies, waits for them, and re-layouts  16.7 us (6%)
  starting transfers between devices  13.6 us (5%)
  other arithmetic  10.5 us (4%)
    all_gather x1, waiting for transfers between devices, on_device(): packed = lax.all_gather(mine[:, :, head_width:], 'zy', axis=0, tiled=True)  57.7 us
    pallas_call x1, Pallas kernels, single(): pl.pallas_call(kernel, out_shape=jax.ShapeDtypeStruct(queries.shape, jnp....  42 us
    reduce_scatter x1, waiting for transfers between devices, on_device(): lax.psum_scatter(jnp.dot(attended, w_out, preferred_element_type=jnp.floa...  19.9 us
    pallas_call x1, Pallas kernels, flash(): pl.pallas_call(kernel, out_shape=jax.ShapeDtypeStruct(queries.shape, jnp....  13.1 us
    all_to_all x1, blocking collectives, on_device(): mine = lax.all_to_all(per_head, 'x', 0, 0, tiled=True)  11.8 us
    dot_general x1, matrix products, on_device(): jnp.dot(inner, w_down, preferred_element_type=jnp.float32) + second  10 us
    all_gather x1, blocking collectives, on_device(): gathered = lax.all_gather(tokens, 'head', axis=0, tiled=True)  9.88 us
    all_gather x1, blocking collectives, on_device(): block_hidden = lax.all_gather(hidden_b, 'head', axis=0, tiled=True)  8.72 us
  transfers between devices with their start and end apart: 6, of which 5 were waited for; matrix products, arithmetic and copies ran while one was open for 10% of the time, Pallas kernels for 21%

profile of v2, /device:TPU:7, one launch (start us, length us, event | category | flops | bytes accessed | tf_op | source)
XLA Modules:
  0.0 265.0 jit_solution(15344889066843600313)
XLA Ops:
  7.2 9.9 %all_gather.15 = bf16[384,1024]{1,0:T(8,128)(2,1)S(1)} all-gather(bf16[96,1024]{1,0:T(8,128)(2,1)} %param.12), channel_id=1, replica_groups=mesh['zy'=8,'x'=4,'head'=4] {'head'}, dimensions={0}, use_global_device_ids=true | all-gather | bytes 983040 | tf_op jit(solution)/shard_map/all_gather | solution.py:344
  17.1 2.4 convolution_convert_fusion
  19.6 11.8 %all_to_all.20 = bf16[4,384,192]{1,2,0:T(8,128)(2,1)S(1)} all-to-all(bf16[4,384,192]{1,2,0:T(8,128)(2,1)S(1)} %bitcast.62), channel_id=1, replica_groups=mesh['zy'=8,'x'=4,'head'=4] {'x'}, dimensions={0} | all-to-all | bytes 1179648 | tf_op jit(solution)/shard_map/all_to_all | solution.py:356
  36.7 1.2 copy.76.low_ref
  40.2 57.7 %all-gather.3.cloned.1.call-done = bf16[32,384,128]{2,1,0:T(8,128)(2,1)} async-done(((bf16[4,384,128]{2,1,0:T(8,128)(2,1)}), bf16[32,384,128]{2,1,0:T(8,128)(2,1)}) %all-gather.3.cloned.1.call-update) | async-done | bytes 3145744 | tf_op jit(solution)/shard_map/all_gather | solution.py:357
  97.8 42.0 %shard_map.139 = bf16[8,192,64]{2,1,0:T(8,128)(2,1)} custom-call(s32[8]{0:T(128)} %get-tuple-element.24.steps_ref, s32[512]{0:T(512)} %mul.192.sources_ref, s32[128]{0:T(128)} %mul.195.bases_ref, bf16[8,192,64]{2,1,0:T(8,128)(2,1)} %bitcast.68, s32[8,192,1]{2,1,0:T(8,128)} %copy.76.low_ref, s32[8,192,1]{2,1,0:T(8,128)} %iota_add_fusion.high_ref, ...), custom_call_target="tpu_custom_call" | custom-call | flops 2415919104 | bytes 12582912 | tf_op jit(solution)/shard_map/pallas_call | solution.py:291
  139.8 1.8 copy.77
  141.6 4.2 %all-to-all-start.1 = ((bf16[4,384,64]{1,2,0:T(8,128)(2,1)}), bf16[4,384,64]{1,2,0:T(8,128)(2,1)S(1)}, u32[]{:S(2)}, u32[]{:S(2)}) async-start(bf16[4,384,64]{1,2,0:T(8,128)(2,1)} %copy.77), calls=%async_computation.1 | async-start | bytes 393216 | tf_op jit(solution)/shard_map/all_to_all | solution.py:385
  146.0 3.4 %all-to-all-done.1 = bf16[4,384,64]{1,2,0:T(8,128)(2,1)S(1)} async-done(((bf16[4,384,64]{1,2,0:T(8,128)(2,1)}), bf16[4,384,64]{1,2,0:T(8,128)(2,1)S(1)}, u32[]{:S(2)}, u32[]{:S(2)}) %all-to-all-start.1) | async-done | bytes 196640 | tf_op jit(solution)/shard_map/all_to_all | solution.py:385
  149.4 1.6 fusion.99
  161.2 7.6 %all-gather.5.cloned.1.call-done = bf16[2,2048,256]{2,1,0:T(8,128)(2,1)} async-done(((bf16[2,64,256]{2,1,0:T(8,128)(2,1)}), bf16[2,2048,256]{2,1,0:T(8,128)(2,1)}) %all-gather.5.cloned.1.call-update) | async-done | bytes 2097168 | tf_op jit(solution)/shard_map/all_gather | solution.py:343
  168.8 3.2 %fusion.11 = (bf16[2496,256]{1,0:T(8,128)(2,1)}, bf16[2496,256]{1,0:T(8,128)(2,1)}) fusion(bf16[2,2048,256]{2,1,0:T(8,128)(2,1)} %all-gather.5.cloned.1.call-done), kind=kLoop, calls=%fused_computation.24 | loop fusion | bytes 4653056 | tf_op jit(solution)/shard_map/squeeze | solution.py:442
  173.9 5.0 %all-to-all-start.3 = ((bf16[4,384,128]{2,1,0:T(8,128)(2,1)}), bf16[4,384,128]{2,1,0:T(8,128)(2,1)S(1)}, u32[]{:S(2)}, u32[]{:S(2)}) async-start(bf16[4,384,128]{2,1,0:T(8,128)(2,1)} %pad_maximum_fusion), calls=%async_computation.4 | async-start | bytes 786432 | tf_op jit(solution)/shard_map/all_to_all | solution.py:405
  178.9 19.9 %reduce-scatter.2.cloned.1.call-done = f32[96,1024]{1,0:T(8,128)} async-done(((f32[384,1024]{1,0:T(8,128)}), f32[96,1024]{1,0:T(8,128)}) %reduce-scatter.2.cloned.1.call-update) | async-done | bytes 393232 | tf_op jit(solution)/shard_map/reduce_scatter | solution.py:408
  198.8 1.1 fusion.51
  199.9 1.2 multiply_reduce_fusion.2
  202.3 8.7 %all_gather.17 = bf16[384,1024]{1,0:T(8,128)(2,1)S(1)} all-gather(bf16[96,1024]{1,0:T(8,128)(2,1)S(1)} %multiply_convert_fusion.1), channel_id=1, replica_groups=mesh['zy'=8,'x'=4,'head'=4] {'head'}, dimensions={0}, use_global_device_ids=true | all-gather | bytes 983040 | tf_op jit(solution)/shard_map/all_gather | solution.py:416
  211.0 2.1 convolution_convert_fusion.1
  213.1 13.1 %shard_map.140 = bf16[2,192,256]{2,1,0:T(8,128)(2,1)} custom-call(s32[2]{0:T(128)} %and_select_fusion.2.steps_ref, s32[24]{0:T(128)} %reshape.398.sources_ref, s32[12]{0:T(128)} %min.32.bases_ref, bf16[2,192,256]{2,1,0:T(8,128)(2,1)} %bitcast.71, s32[2,192,1]{2,1,0:T(8,128)} %reshape.413.low_ref, s32[2,192,1]{2,1,0:T(8,128)} %sub.88.high_ref, ...), custom_call_target="tpu_custom_call" | custom-call | flops 3623878656 | bytes 4718592 | tf_op jit(solution)/shard_map/pallas_call | solution.py:191
  226.2 4.3 %all-to-all-start.2 = ((bf16[4,96,256]{2,1,0:T(8,128)(2,1)}), bf16[4,96,256]{2,1,0:T(8,128)(2,1)}, u32[]{:S(2)}, u32[]{:S(2)}) async-start(bf16[4,96,256]{2,1,0:T(8,128)(2,1)} %bitcast.70), calls=%async_computation.3 | async-start | bytes 393216 | tf_op jit(solution)/shard_map/all_to_all | solution.py:449
  231.8 3.3 %all-to-all-done.2 = bf16[4,96,256]{2,1,0:T(8,128)(2,1)} async-done(((bf16[4,96,256]{2,1,0:T(8,128)(2,1)}), bf16[4,96,256]{2,1,0:T(8,128)(2,1)}, u32[]{:S(2)}, u32[]{:S(2)}) %all-to-all-start.2) | async-done | bytes 196640 | tf_op jit(solution)/shard_map/all_to_all | solution.py:449
  236.9 10.0 %fusion.98 = (f32[96]{0:T(128)S(1)}, f32[96,1024]{1,0:T(8,128)S(1)}) fusion(f32[96]{0:T(128)S(1)} %add_rsqrt_fusion.1, f32[96,1024]{1,0:T(8,128)S(1)} %get-tuple-element.50, f32[96]{0:T(128)S(1)} %broadcast_multiply_fusion.2, bf16[4096,1024]{1,0:T(8,128)(2,1)} %param.22, bf16[1024,4096]{1,0:T(8,128)(2,1)} %param.21), kind=kOutput, calls=%fused_computation.182 | convolution fusion | flops 1636859776 | bytes 17564800 | tf_op jit(solution)/shard_map/dot_general | solution.py:459
  248.0 8.7 %all_gather.19 = bf16[384,1024]{1,0:T(8,128)(2,1)S(1)} all-gather(bf16[96,1024]{1,0:T(8,128)(2,1)S(1)} %get-tuple-element.22), channel_id=1, replica_groups=mesh['zy'=8,'x'=4,'head'=4] {'head'}, dimensions={0}, use_global_device_ids=true | all-gather | bytes 983040 | tf_op jit(solution)/shard_map/all_gather | solution.py:461
  256.7 1.8 convolution_bitcast_fusion
  (90 shorter events, 20.0 us)
Async XLA Ops:
  7.2 228.8 %copy-start = (bf16[1024,1024]{1,0:T(8,128)(2,1)S(1)}, bf16[1024,1024]{1,0:T(8,128)(2,1)}, u32[]{:S(2)}) copy-start(bf16[1024,1024]{1,0:T(8,128)(2,1)} %param.20) | copy-start | bytes 6291460
  7.2 90.7 %all-gather.3.cloned.1.call-start = ((), (), s32[]{:S(2)}) async-start(), calls=%async_computation.5 | async-start | bytes 3538944 | tf_op jit(solution)/shard_map/all_gather | solution.py:357
  19.6 13.6 %copy-start.5 = (s32[9]{0:T(128)S(1)}, s32[9]{0:T(128)}, u32[]{:S(2)}) copy-start(s32[9]{0:T(128)} %param.14) | copy-start | bytes 112
  19.6 13.8 %copy-start.4 = (s32[64]{0:T(128)S(1)}, s32[64]{0:T(128)}, u32[]{:S(2)}) copy-start(s32[64]{0:T(128)} %param.13) | copy-start | bytes 772
  32.4 136.4 %all-gather.5.cloned.1.call-start = ((), (), s32[]{:S(2)}) async-start(), calls=%async_computation.7 | async-start | bytes 2162688 | tf_op jit(solution)/shard_map/all_gather | solution.py:343
  97.8 51.5 %copy-start.3 = (bf16[256,1024]{1,0:T(8,128)(2,1)S(1)}, bf16[256,1024]{1,0:T(8,128)(2,1)}, u32[]{:S(2)}) copy-start(bf16[256,1024]{1,0:T(8,128)(2,1)} %param.17) | copy-start | bytes 1572868
  141.6 7.7 %all-to-all-start.1 = ((bf16[4,384,64]{1,2,0:T(8,128)(2,1)}), bf16[4,384,64]{1,2,0:T(8,128)(2,1)S(1)}, u32[]{:S(2)}, u32[]{:S(2)}) async-start(bf16[4,384,64]{1,2,0:T(8,128)(2,1)} %copy.77), calls=%async_computation.1 | async-start | bytes 393216 | tf_op jit(solution)/shard_map/all_to_all | solution.py:385
  145.9 52.9 %reduce-scatter.2.cloned.1.call-start = ((), (), s32[]{:S(2)}) async-start(), calls=%async_computation.6 | async-start | bytes 1966080 | tf_op jit(solution)/shard_map/reduce_scatter | solution.py:408
  149.4 7.3 %copy-start.6 = (s32[9]{0:T(128)S(1)}, s32[9]{0:T(128)}, u32[]{:S(2)}) copy-start(s32[9]{0:T(128)} %param.15) | copy-start | bytes 112
  172.0 26.7 %copy-start.2 = (bf16[96,1024]{1,0:T(8,128)(2,1)S(1)}, bf16[96,1024]{1,0:T(8,128)(2,1)}, u32[]{:S(2)}) copy-start(bf16[96,1024]{1,0:T(8,128)(2,1)} %param.12) | copy-start | bytes 589828
  173.9 52.3 %all-to-all-start.3 = ((bf16[4,384,128]{2,1,0:T(8,128)(2,1)}), bf16[4,384,128]{2,1,0:T(8,128)(2,1)S(1)}, u32[]{:S(2)}, u32[]{:S(2)}) async-start(bf16[4,384,128]{2,1,0:T(8,128)(2,1)} %pad_maximum_fusion), calls=%async_computation.4 | async-start | bytes 786432 | tf_op jit(solution)/shard_map/all_to_all | solution.py:405
  226.2 9.8 %copy-start.1 = (f32[96,1024]{1,0:T(8,128)S(1)}, f32[96,1024]{1,0:T(8,128)}, u32[]{:S(2)}) copy-start(f32[96,1024]{1,0:T(8,128)} %reduce-scatter.2.cloned.1.call-done) | copy-start | bytes 1179652
  226.2 8.8 %all-to-all-start.2 = ((bf16[4,96,256]{2,1,0:T(8,128)(2,1)}), bf16[4,96,256]{2,1,0:T(8,128)(2,1)}, u32[]{:S(2)}, u32[]{:S(2)}) async-start(bf16[4,96,256]{2,1,0:T(8,128)(2,1)} %bitcast.70), calls=%async_computation.3 | async-start | bytes 393216 | tf_op jit(solution)/shard_map/all_to_all | solution.py:449
  246.9 9.8 %copy-start.7 = (bf16[3,1024,256]{2,1,0:T(8,128)(2,1)S(1)}, bf16[3,1024,256]{2,1,0:T(8,128)(2,1)}, u32[]{:S(2)}) copy-start(bf16[3,1024,256]{2,1,0:T(8,128)(2,1)} %param.23) | copy-start | bytes 4718596
Sparse Core Ops, SparseCore 0:
  32.5 65.2 all-gather.2
  100.9 67.9 all-gather.4
  171.2 27.4 reduce-scatter.1

commit v3 on v2

--- a/solution.py
+++ b/solution.py
@@ -222,12 +222,17 @@
 
 
 def single_kernel(
-    steps_ref, sources_ref, bases_ref, q_ref, low_ref, high_ref, kv_hbm, o_ref,
-    buf, sem, m_sc, l_sc, acc_sc, *, max_steps, head_width, pieces
+    steps_ref, sources_ref, bases_ref, q_ref, low_ref, high_ref, m_ref, l_ref, acc_ref, kv_hbm,
+    *rest, max_steps, pieces, first, last
 ):
+    if last:
+        o_ref, buf, sem, m_sc, l_sc, acc_sc = rest
+    else:
+        m_out, l_out, acc_out, buf, sem, m_sc, l_sc, acc_sc = rest
     half = pl.program_id(0)
     count = steps_ref[half]
     tile = buf.shape[1] // pieces
+    head_width = q_ref.shape[2]
 
     def copies(step, slot):
         result = []
@@ -237,14 +242,25 @@
                 kv_hbm.at[pl.ds(source, tile)], buf.at[slot, pl.ds(j * tile, tile)], sem.at[slot, j]))
         return result
 
-    for copy in copies(0, 0):
-        copy.start()
-    m_sc[...] = jnp.full(m_sc.shape, NEGATIVE, jnp.float32)
-    l_sc[...] = jnp.zeros(l_sc.shape, jnp.float32)
-    acc_sc[...] = jnp.zeros(acc_sc.shape, jnp.float32)
+    @pl.when(count > 0)
+    def _():
+        for copy in copies(0, 0):
+            copy.start()
+
+    if first:
+        m_sc[...] = jnp.full(m_sc.shape, NEGATIVE, jnp.float32)
+        l_sc[...] = jnp.zeros(l_sc.shape, jnp.float32)
+        acc_sc[...] = jnp.zeros(acc_sc.shape, jnp.float32)
+    else:
+        m_sc[...] = m_ref[0]
+        l_sc[...] = l_ref[0]
+        acc_sc[...] = acc_ref[0]
     q = q_ref[0]
     low = low_ref[0]
     high = high_ref[0]
+    lane = lax.broadcasted_iota(jnp.int32, (1, pieces * tile), 1)
+    piece = lane // tile
+    offset = lane - piece * tile
 
     def body(step, carry):
         slot = step % 2
@@ -256,8 +272,11 @@
             for copy in copies(step + 1, 1 - slot):
                 copy.start()
 
-        base = bases_ref[half * max_steps + step]
-        places = base + lax.broadcasted_iota(jnp.int32, (1, pieces * tile), 1)
+        row = (half * max_steps + step) * pieces
+        base = jnp.zeros((1, pieces * tile), jnp.int32)
+        for j in range(pieces):
+            base = jnp.where(piece == j, bases_ref[row + j], base)
+        places = base + offset
         visible = (places >= low) & (places <= high)
         block = buf[slot]
         keys = block[:, :head_width]
@@ -278,24 +297,42 @@
         return carry
 
     lax.fori_loop(0, count, body, 0)
-    o_ref[0] = (acc_sc[...] / l_sc[...]).astype(o_ref.dtype)
-
-
-def single(queries, low, high, packed, steps, sources, bases, max_steps, pieces):
+    if last:
+        o_ref[0] = (acc_sc[...] / l_sc[...]).astype(o_ref.dtype)
+    else:
+        m_out[0] = m_sc[...]
+        l_out[0] = l_sc[...]
+        acc_out[0] = acc_sc[...]
+
+
+def single(queries, low, high, state, packed, steps, sources, bases, max_steps, pieces, first, last):
     halves, tile, head_width = queries.shape
     kernel = functools.partial(
-        single_kernel, max_steps=max_steps, head_width=head_width, pieces=pieces
+        single_kernel, max_steps=max_steps, pieces=pieces, first=first, last=last
     )
     row_spec = pl.BlockSpec((1, tile, head_width), lambda h, *refs: (h, 0, 0))
     bound_spec = pl.BlockSpec((1, tile, 1), lambda h, *refs: (h, 0, 0))
+    state_shapes = (
+        jax.ShapeDtypeStruct((halves, tile, 1), jnp.float32),
+        jax.ShapeDtypeStruct((halves, tile, 1), jnp.float32),
+        jax.ShapeDtypeStruct((halves, tile, head_width), jnp.float32),
+    )
+    state_specs = [bound_spec, bound_spec, row_spec]
+    if last:
+        out_shape = jax.ShapeDtypeStruct(queries.shape, jnp.bfloat16)
+        out_specs = row_spec
+    else:
+        out_shape = state_shapes
+        out_specs = state_specs
     return pl.pallas_call(
         kernel,
-        out_shape=jax.ShapeDtypeStruct(queries.shape, jnp.bfloat16),
+        out_shape=out_shape,
         grid_spec=pltpu.PrefetchScalarGridSpec(
             num_scalar_prefetch=3,
             grid=(halves,),
-            in_specs=[row_spec, bound_spec, bound_spec, pl.BlockSpec(memory_space=pl.ANY)],
-            out_specs=row_spec,
+            in_specs=[row_spec, bound_spec, bound_spec] + state_specs
+            + [pl.BlockSpec(memory_space=pl.ANY)],
+            out_specs=out_specs,
             scratch_shapes=[
                 pltpu.VMEM((2, pieces * tile, packed.shape[1]), packed.dtype),
                 pltpu.SemaphoreType.DMA((2, pieces)),
@@ -306,11 +343,11 @@
         ),
         compiler_params=pltpu.CompilerParams(dimension_semantics=("arbitrary",)),
         cost_estimate=pl.CostEstimate(
-            flops=2 * halves * (max_steps // 2) * tile * pieces * tile * head_width * 2,
-            transcendentals=halves * (max_steps // 2) * tile * pieces * tile,
-            bytes_accessed=halves * (max_steps // 2) * pieces * tile * packed.shape[1] * 2,
+            flops=2 * halves * (max_steps // 4) * tile * pieces * tile * head_width * 2,
+            transcendentals=halves * (max_steps // 4) * tile * pieces * tile,
+            bytes_accessed=halves * (max_steps // 4) * pieces * tile * packed.shape[1] * 2,
         ),
-    )(steps, sources, bases, queries, low, high, packed)
+    )(steps, sources, bases, queries, low, high, *state, packed)
 
 
 def on_device(
@@ -354,8 +391,9 @@
     per_head = projected.reshape(3, block_rows, group_heads, head_width).transpose(2, 1, 0, 3)
     per_head = per_head.reshape(group_heads, block_rows, 3 * head_width)
     mine = lax.all_to_all(per_head, "x", 0, 0, tiled=True)
-    packed = lax.all_gather(mine[:, :, head_width:], "zy", axis=0, tiled=True)
-    packed = packed.reshape(cycle_size * block_rows, 2 * head_width)
+    parts = mine[:, :, head_width:].reshape(ring_size, 2, halfway, 2 * head_width)
+    even = lax.all_gather(parts[:, 0], "zy", axis=0, tiled=True).reshape(-1, 2 * head_width)
+    odd = lax.all_gather(parts[:, 1], "zy", axis=0, tiled=True).reshape(-1, 2 * head_width)
     ends = jnp.cumsum(request_lengths).astype(jnp.int32)
     starts = ends - request_lengths
     halves_here = 2 * ring_size
@@ -363,24 +401,40 @@
     pair = lax.dynamic_slice_in_dim(block_order, first_half, halves_here, 0)
     low_block = prefix_below(pair * halfway, ends, request_lengths) // halfway
     pieces = 4
-    self_steps = (pair - low_block) // pieces + 1
-    self_max = (2 * cycle_size + pieces - 1) // pieces
-    firsts = low_block[:, None] + pieces * jnp.arange(self_max, dtype=jnp.int32)[None, :]
-    self_sources = lookup(
-        holders,
-        jnp.minimum(firsts[:, :, None] + jnp.arange(pieces, dtype=jnp.int32), 2 * cycle_size - 1),
-    ) * halfway
+    candidates = jnp.arange(2 * cycle_size, dtype=jnp.int32)
+    in_range = (candidates[None, :] >= low_block[:, None]) & (candidates[None, :] <= pair[:, None])
+    pass_max = (2 * cycle_size + pieces - 1) // pieces
+    slots_all = jnp.arange(pass_max * pieces, dtype=jnp.int32)
+    plans = []
+    for parity in range(2):
+        chosen = in_range & ((holders % 2) == parity)[None, :]
+        rank = jnp.cumsum(chosen.astype(jnp.int32), axis=1) - 1
+        count = jnp.sum(chosen.astype(jnp.int32), axis=1)
+        picked = chosen[:, None, :] & (rank[:, None, :] == slots_all[None, :, None])
+        listed = jnp.sum(jnp.where(picked, candidates, 0), axis=-1)
+        listed = jnp.where(slots_all[None, :] >= count[:, None], 2 * cycle_size, listed)
+        rows = jnp.sum(jnp.where(picked, (holders // 2) * halfway, 0), axis=-1)
+        plans.append(
+            (
+                ((count + pieces - 1) // pieces).astype(jnp.int32),
+                rows.reshape(-1).astype(jnp.int32),
+                (listed * halfway).reshape(-1).astype(jnp.int32),
+            )
+        )
     places_here = (pair[:, None] * halfway + jnp.arange(halfway, dtype=jnp.int32)[None, :])
+    self_queries = mine[:, :, :head_width].reshape(halves_here, halfway, head_width)
+    self_low = prefix_below(places_here, ends, request_lengths).reshape(halves_here, halfway, 1)
+    self_high = places_here.reshape(halves_here, halfway, 1)
+    blank = (
+        jnp.zeros((halves_here, halfway, 1), jnp.float32),
+        jnp.zeros((halves_here, halfway, 1), jnp.float32),
+        jnp.zeros((halves_here, halfway, head_width), jnp.float32),
+    )
+    state = single(
+        self_queries, self_low, self_high, blank, even, *plans[0], pass_max, pieces, True, False
+    )
     single_out = single(
-        mine[:, :, :head_width].reshape(halves_here, halfway, head_width),
-        prefix_below(places_here, ends, request_lengths).reshape(halves_here, halfway, 1),
-        places_here.reshape(halves_here, halfway, 1),
-        packed,
-        self_steps.astype(jnp.int32),
-        self_sources.reshape(-1).astype(jnp.int32),
-        (firsts * halfway).reshape(-1).astype(jnp.int32),
-        self_max,
-        pieces,
+        self_queries, self_low, self_high, state, odd, *plans[1], pass_max, pieces, False, True
     )
     returned = lax.all_to_all(
         single_out.reshape(ring_size, block_rows, head_width), "x", 0, 0, tiled=True
@@ -390,15 +444,17 @@
     cache_rows = lookup(
         holders, jnp.stack([2 * group_blocks, 2 * group_blocks + 1], axis=1)
     )
+    def cache_piece(holder):
+        start = (holder // 2) * halfway
+        return jnp.where(
+            holder % 2 == 0,
+            lax.dynamic_slice_in_dim(even, start, halfway, 0),
+            lax.dynamic_slice_in_dim(odd, start, halfway, 0),
+        )
+
     cache_parts = jnp.stack(
         [
-            jnp.concatenate(
-                [
-                    lax.dynamic_slice_in_dim(packed, cache_rows[i, 0] * halfway, halfway, 0),
-                    lax.dynamic_slice_in_dim(packed, cache_rows[i, 1] * halfway, halfway, 0),
-                ],
-                axis=0,
-            )
+            jnp.concatenate([cache_piece(cache_rows[i, 0]), cache_piece(cache_rows[i, 1])], axis=0)
             for i in range(ring_size)
         ]
     )

time: 270 us -> 306 us (1.13)
  the two profiles are of different devices: /device:TPU:7 before, /device:TPU:27 now
where the time goes in v3:
time: 306 us; the launch traced here: 301 us
  waiting for transfers between devices  106 us (35%)
  Pallas kernels  56.9 us (19%)
  blocking collectives  39.8 us (13%)
  between operations  34.5 us (11%)
  local copies, waits for them, and re-layouts  18.9 us (6%)
  matrix products  18.5 us (6%)
  starting transfers between devices  13.3 us (4%)
  other arithmetic  13 us (4%)
    pallas_call x2, Pallas kernels, single(): pl.pallas_call(kernel, out_shape=out_shape, grid_spec=pltpu.PrefetchScala...  45.5 us
    all_gather x1, waiting for transfers between devices, on_device(): lax.all_gather(parts[:, 0], 'zy', axis=0, tiled=True)  40.1 us
    all_gather x1, waiting for transfers between devices, on_device(): lax.all_gather(parts[:, 1], 'zy', axis=0, tiled=True)  27.2 us
    reduce_scatter x1, waiting for transfers between devices, on_device(): lax.psum_scatter(jnp.dot(attended, w_out, preferred_element_type=jnp.floa...  23.7 us
    all_to_all x1, blocking collectives, on_device(): mine = lax.all_to_all(per_head, 'x', 0, 0, tiled=True)  12.4 us
    pallas_call x1, Pallas kernels, flash(): pl.pallas_call(kernel, out_shape=jax.ShapeDtypeStruct(queries.shape, jnp....  11.5 us
    dot_general x1, matrix products, on_device(): jnp.dot(inner, w_down, preferred_element_type=jnp.float32) + second  10 us
    all_gather x1, blocking collectives, on_device(): gathered = lax.all_gather(tokens, 'head', axis=0, tiled=True)  9.88 us
  transfers between devices with their start and end apart: 7, of which 6 were waited for; matrix products, arithmetic and copies ran while one was open for 11% of the time, Pallas kernels for 19%

profile of v3, /device:TPU:27, one launch (start us, length us, event | category | flops | bytes accessed | tf_op | source)
XLA Modules:
  0.0 300.9 jit_solution(3806223863905396921)
XLA Ops:
  7.2 9.9 %all_gather.18 = bf16[384,1024]{1,0:T(8,128)(2,1)S(1)} all-gather(bf16[96,1024]{1,0:T(8,128)(2,1)} %param.12), channel_id=1, replica_groups=mesh['zy'=8,'x'=4,'head'=4] {'head'}, dimensions={0}, use_global_device_ids=true | all-gather | bytes 983040 | tf_op jit(solution)/shard_map/all_gather | solution.py:381
  17.1 2.4 convolution_convert_fusion
  19.6 12.4 %all_to_all.20 = bf16[4,384,192]{1,2,0:T(8,128)(2,1)S(1)} all-to-all(bf16[4,384,192]{1,2,0:T(8,128)(2,1)S(1)} %bitcast.64), channel_id=1, replica_groups=mesh['zy'=8,'x'=4,'head'=4] {'x'}, dimensions={0} | all-to-all | bytes 1179648 | tf_op jit(solution)/shard_map/all_to_all | solution.py:393
  44.0 40.1 %all-gather.8.cloned.1.call-done = bf16[32,1,192,128]{3,2,1,0:T(8,128)(2,1)} async-done(((bf16[4,1,192,128]{3,2,1,0:T(8,128)(2,1)}), bf16[32,1,192,128]{3,2,1,0:T(8,128)(2,1)}) %all-gather.8.cloned.1.call-update) | async-done | bytes 1572880 | tf_op jit(solution)/shard_map/all_gather | solution.py:395
  86.1 23.6 %shard_map.139 = (f32[8,192,1]{2,1,0:T(8,128)}, f32[8,192,1]{2,1,0:T(8,128)}, f32[8,192,64]{2,1,0:T(8,128)}) custom-call(s32[8]{0:T(128)} %and_select_fusion.steps_ref, s32[512]{0:T(512)} %reshape.556.sources_ref, s32[512]{0:T(512)} %mul.159.bases_ref, bf16[8,192,64]{2,1,0:T(8,128)(2,1)} %bitcast.71, s32[8,192,1]{2,1,0:T(8,128)} %copy.64.low_ref, ...), custom_call_target="tpu_custom_call" | custom-call | flops 1207959552 | bytes 6291456 | tf_op jit(solution)/shard_map/pallas_call | solution.py:327
  109.7 27.2 %all-gather.10.cloned.1.call-done = bf16[32,1,192,128]{3,2,1,0:T(8,128)(2,1)} async-done(((bf16[4,1,192,128]{3,2,1,0:T(8,128)(2,1)}), bf16[32,1,192,128]{3,2,1,0:T(8,128)(2,1)}) %all-gather.10.cloned.1.call-update) | async-done | bytes 1572880 | tf_op jit(solution)/shard_map/all_gather | solution.py:396
  137.0 21.8 %shard_map.140 = bf16[8,192,64]{2,1,0:T(8,128)(2,1)} custom-call(s32[8]{0:T(128)} %and_select_fusion.2.steps_ref, s32[512]{0:T(512)} %reshape.551.sources_ref, s32[512]{0:T(512)} %mul.157.bases_ref, bf16[8,192,64]{2,1,0:T(8,128)(2,1)} %bitcast.72, s32[8,192,1]{2,1,0:T(8,128)} %copy.64.low_ref, s32[8,192,1]{2,1,0:T(8,128)} %iota_add_fusion.high_ref, ...), custom_call_target="tpu_custom_call" | custom-call | flops 1207959552 | bytes 6291456 | tf_op jit(solution)/shard_map/pallas_call | solution.py:327
  158.8 1.8 copy.65
  160.6 4.2 %all-to-all-start.1 = ((bf16[4,384,64]{1,2,0:T(8,128)(2,1)}), bf16[4,384,64]{1,2,0:T(8,128)(2,1)S(1)}, u32[]{:S(2)}, u32[]{:S(2)}) async-start(bf16[4,384,64]{1,2,0:T(8,128)(2,1)} %copy.65), calls=%async_computation.1 | async-start | bytes 393216 | tf_op jit(solution)/shard_map/all_to_all | solution.py:439
  164.9 4.0 %all-to-all-done.1 = bf16[4,384,64]{1,2,0:T(8,128)(2,1)S(1)} async-done(((bf16[4,384,64]{1,2,0:T(8,128)(2,1)}), bf16[4,384,64]{1,2,0:T(8,128)(2,1)S(1)}, u32[]{:S(2)}, u32[]{:S(2)}) %all-to-all-start.1) | async-done | bytes 196640 | tf_op jit(solution)/shard_map/all_to_all | solution.py:439
  168.9 1.6 fusion.109
  196.4 1.2 dynamic-slice_select_fusion.7
  198.6 4.6 %all-to-all-start.3 = ((bf16[4,384,128]{2,1,0:T(8,128)(2,1)}), bf16[4,384,128]{2,1,0:T(8,128)(2,1)S(1)}, u32[]{:S(2)}, u32[]{:S(2)}) async-start(bf16[4,384,128]{2,1,0:T(8,128)(2,1)} %pad_maximum_fusion), calls=%async_computation.4 | async-start | bytes 786432 | tf_op jit(solution)/shard_map/all_to_all | solution.py:461
  203.2 6.3 %all-gather.6.cloned.1.call-done = bf16[2,2048,256]{2,1,0:T(8,128)(2,1)} async-done(((bf16[2,64,256]{2,1,0:T(8,128)(2,1)}), bf16[2,2048,256]{2,1,0:T(8,128)(2,1)}) %all-gather.6.cloned.1.call-update) | async-done | bytes 2097168 | tf_op jit(solution)/shard_map/all_gather | solution.py:380
  209.5 3.1 %fusion.11 = (bf16[2496,256]{1,0:T(8,128)(2,1)}, bf16[2496,256]{1,0:T(8,128)(2,1)}) fusion(bf16[2,2048,256]{2,1,0:T(8,128)(2,1)} %all-gather.6.cloned.1.call-done), kind=kLoop, calls=%fused_computation.24 | loop fusion | bytes 4653056 | tf_op jit(solution)/shard_map/squeeze | solution.py:498
  212.6 23.7 %reduce-scatter.2.cloned.1.call-done = f32[96,1024]{1,0:T(8,128)} async-done(((f32[384,1024]{1,0:T(8,128)}), f32[96,1024]{1,0:T(8,128)}) %reduce-scatter.2.cloned.1.call-update) | async-done | bytes 393232 | tf_op jit(solution)/shard_map/reduce_scatter | solution.py:464
  239.8 8.7 %all_gather.21 = bf16[384,1024]{1,0:T(8,128)(2,1)S(1)} all-gather(bf16[96,1024]{1,0:T(8,128)(2,1)S(1)} %multiply_convert_fusion.1), channel_id=1, replica_groups=mesh['zy'=8,'x'=4,'head'=4] {'head'}, dimensions={0}, use_global_device_ids=true | all-gather | bytes 983040 | tf_op jit(solution)/shard_map/all_gather | solution.py:472
  248.6 2.1 convolution_convert_fusion.1
  250.7 11.5 %shard_map.141 = bf16[2,192,256]{2,1,0:T(8,128)(2,1)} custom-call(s32[2]{0:T(128)} %and_select_fusion.5.steps_ref, s32[24]{0:T(128)} %reshape.550.sources_ref, s32[12]{0:T(128)} %min.22.bases_ref, bf16[2,192,256]{2,1,0:T(8,128)(2,1)} %bitcast.75, s32[2,192,1]{2,1,0:T(8,128)} %reshape.573.low_ref, s32[2,192,1]{2,1,0:T(8,128)} %sub.149.high_ref, ...), custom_call_target="tpu_custom_call" | custom-call | flops 3623878656 | bytes 4718592 | tf_op jit(solution)/shard_map/pallas_call | solution.py:191
  262.1 4.3 %all-to-all-start.2 = ((bf16[4,96,256]{2,1,0:T(8,128)(2,1)}), bf16[4,96,256]{2,1,0:T(8,128)(2,1)}, u32[]{:S(2)}, u32[]{:S(2)}) async-start(bf16[4,96,256]{2,1,0:T(8,128)(2,1)} %bitcast.74), calls=%async_computation.3 | async-start | bytes 393216 | tf_op jit(solution)/shard_map/all_to_all | solution.py:505
  267.7 3.3 %all-to-all-done.2 = bf16[4,96,256]{2,1,0:T(8,128)(2,1)} async-done(((bf16[4,96,256]{2,1,0:T(8,128)(2,1)}), bf16[4,96,256]{2,1,0:T(8,128)(2,1)}, u32[]{:S(2)}, u32[]{:S(2)}) %all-to-all-start.2) | async-done | bytes 196640 | tf_op jit(solution)/shard_map/all_to_all | solution.py:505
  272.8 10.0 %fusion.108 = (f32[96]{0:T(128)S(1)}, f32[96,1024]{1,0:T(8,128)S(1)}) fusion(f32[96]{0:T(128)S(1)} %add_rsqrt_fusion.1, f32[96,1024]{1,0:T(8,128)S(1)} %get-tuple-element.67, f32[96]{0:T(128)S(1)} %broadcast_multiply_fusion.1, bf16[4096,1024]{1,0:T(8,128)(2,1)} %param.22, bf16[1024,4096]{1,0:T(8,128)(2,1)} %param.21), kind=kOutput, calls=%fused_computation.210 | convolution fusion | flops 1636859776 | bytes 17564800 | tf_op jit(solution)/shard_map/dot_general | solution.py:515
  283.9 8.7 %all_gather.23 = bf16[384,1024]{1,0:T(8,128)(2,1)S(1)} all-gather(bf16[96,1024]{1,0:T(8,128)(2,1)S(1)} %get-tuple-element.29), channel_id=1, replica_groups=mesh['zy'=8,'x'=4,'head'=4] {'head'}, dimensions={0}, use_global_device_ids=true | all-gather | bytes 983040 | tf_op jit(solution)/shard_map/all_gather | solution.py:517
  292.6 1.8 convolution_bitcast_fusion
  (107 shorter events, 27.8 us)
Async XLA Ops:
  7.2 264.8 %copy-start = (bf16[1024,1024]{1,0:T(8,128)(2,1)S(1)}, bf16[1024,1024]{1,0:T(8,128)(2,1)}, u32[]{:S(2)}) copy-start(bf16[1024,1024]{1,0:T(8,128)(2,1)} %param.20) | copy-start | bytes 6291460
  7.2 77.0 %all-gather.8.cloned.1.call-start = ((), (), s32[]{:S(2)}) async-start(), calls=%async_computation.7 | async-start | bytes 1769472 | tf_op jit(solution)/shard_map/all_gather | solution.py:395
  32.1 2.6 copy-start.4
  32.1 2.8 copy-start.5
  33.1 103.8 %all-gather.10.cloned.1.call-start = ((), (), s32[]{:S(2)}) async-start(), calls=%async_computation.8 | async-start | bytes 1769472 | tf_op jit(solution)/shard_map/all_gather | solution.py:396
  33.9 175.6 %all-gather.6.cloned.1.call-start = ((), (), s32[]{:S(2)}) async-start(), calls=%async_computation.6 | async-start | bytes 2162688 | tf_op jit(solution)/shard_map/all_gather | solution.py:380
  137.0 31.9 %copy-start.3 = (bf16[256,1024]{1,0:T(8,128)(2,1)S(1)}, bf16[256,1024]{1,0:T(8,128)(2,1)}, u32[]{:S(2)}) copy-start(bf16[256,1024]{1,0:T(8,128)(2,1)} %param.17) | copy-start | bytes 1572868
  160.6 8.2 %all-to-all-start.1 = ((bf16[4,384,64]{1,2,0:T(8,128)(2,1)}), bf16[4,384,64]{1,2,0:T(8,128)(2,1)S(1)}, u32[]{:S(2)}, u32[]{:S(2)}) async-start(bf16[4,384,64]{1,2,0:T(8,128)(2,1)} %copy.65), calls=%async_computation.1 | async-start | bytes 393216 | tf_op jit(solution)/shard_map/all_to_all | solution.py:439
  164.9 71.5 %reduce-scatter.2.cloned.1.call-start = ((), (), s32[]{:S(2)}) async-start(), calls=%async_computation.5 | async-start | bytes 1966080 | tf_op jit(solution)/shard_map/reduce_scatter | solution.py:464
  168.9 1.6 copy-start.6
  198.6 63.6 %all-to-all-start.3 = ((bf16[4,384,128]{2,1,0:T(8,128)(2,1)}), bf16[4,384,128]{2,1,0:T(8,128)(2,1)S(1)}, u32[]{:S(2)}, u32[]{:S(2)}) async-start(bf16[4,384,128]{2,1,0:T(8,128)(2,1)} %pad_maximum_fusion), calls=%async_computation.4 | async-start | bytes 786432 | tf_op jit(solution)/shard_map/all_to_all | solution.py:461
  203.2 33.2 %copy-start.2 = (bf16[96,1024]{1,0:T(8,128)(2,1)S(1)}, bf16[96,1024]{1,0:T(8,128)(2,1)}, u32[]{:S(2)}) copy-start(bf16[96,1024]{1,0:T(8,128)(2,1)} %param.12) | copy-start | bytes 589828
  262.1 9.8 %copy-start.1 = (f32[96,1024]{1,0:T(8,128)S(1)}, f32[96,1024]{1,0:T(8,128)}, u32[]{:S(2)}) copy-start(f32[96,1024]{1,0:T(8,128)} %reduce-scatter.2.cloned.1.call-done) | copy-start | bytes 1179652
  262.1 8.8 %all-to-all-start.2 = ((bf16[4,96,256]{2,1,0:T(8,128)(2,1)}), bf16[4,96,256]{2,1,0:T(8,128)(2,1)}, u32[]{:S(2)}, u32[]{:S(2)}) async-start(bf16[4,96,256]{2,1,0:T(8,128)(2,1)} %bitcast.74), calls=%async_computation.3 | async-start | bytes 393216 | tf_op jit(solution)/shard_map/all_to_all | solution.py:505
  282.8 9.8 %copy-start.7 = (bf16[3,1024,256]{2,1,0:T(8,128)(2,1)S(1)}, bf16[3,1024,256]{2,1,0:T(8,128)(2,1)}, u32[]{:S(2)}) copy-start(bf16[3,1024,256]{2,1,0:T(8,128)(2,1)} %param.23) | copy-start | bytes 4718596
Sparse Core Ops, SparseCore 0:
  33.3 50.8 all-gather.7
  87.0 49.8 all-gather.9
  140.0 69.4 all-gather.5
  211.7 24.5 reduce-scatter.1

commit v4 on v2

--- a/solution.py
+++ b/solution.py
@@ -222,7 +222,7 @@
 
 
 def single_kernel(
-    steps_ref, sources_ref, bases_ref, q_ref, low_ref, high_ref, kv_hbm, o_ref,
+    steps_ref, sources_ref, bases_ref, limits_ref, q_ref, low_ref, high_ref, kv_hbm, o_ref,
     buf, sem, m_sc, l_sc, acc_sc, *, max_steps, head_width, pieces
 ):
     half = pl.program_id(0)
@@ -257,31 +257,44 @@
                 copy.start()
 
         base = bases_ref[half * max_steps + step]
-        places = base + lax.broadcasted_iota(jnp.int32, (1, pieces * tile), 1)
-        visible = (places >= low) & (places <= high)
-        block = buf[slot]
-        keys = block[:, :head_width]
-        values = block[:, head_width:]
-        scores = lax.dot_general(
-            q, keys, (((1,), (1,)), ((), ())), preferred_element_type=jnp.float32
-        ) * SCALING
-        scores = jnp.where(visible, scores, NEGATIVE)
-        previous = m_sc[...]
-        updated = jnp.maximum(previous, jnp.max(scores, axis=1, keepdims=True))
-        factor = jnp.exp(previous - updated)
-        weights = jnp.exp(scores - updated)
-        l_sc[...] = l_sc[...] * factor + jnp.sum(weights, axis=1, keepdims=True)
-        acc_sc[...] = acc_sc[...] * factor + jnp.dot(
-            weights.astype(jnp.bfloat16), values, preferred_element_type=jnp.float32
-        )
-        m_sc[...] = updated
+        keys = buf[slot, :, :head_width]
+        values = buf[slot, :, head_width:]
+
+        def update(masked):
+            scores = lax.dot_general(
+                q, keys, (((1,), (1,)), ((), ())), preferred_element_type=jnp.float32
+            ) * SCALING
+            if masked:
+                places = base + lax.broadcasted_iota(jnp.int32, (1, pieces * tile), 1)
+                visible = (places >= low) & (places <= high)
+                scores = jnp.where(visible, scores, NEGATIVE)
+            previous = m_sc[...]
+            updated = jnp.maximum(previous, jnp.max(scores, axis=1, keepdims=True))
+            factor = jnp.exp(previous - updated)
+            weights = jnp.exp(scores - updated)
+            l_sc[...] = l_sc[...] * factor + jnp.sum(weights, axis=1, keepdims=True)
+            acc_sc[...] = acc_sc[...] * factor + jnp.dot(
+                weights.astype(jnp.bfloat16), values, preferred_element_type=jnp.float32
+            )
+            m_sc[...] = updated
+
+        full = (base >= limits_ref[2 * half]) & (base + pieces * tile - 1 <= limits_ref[2 * half + 1])
+
+        @pl.when(full)
+        def _():
+            update(False)
+
+        @pl.when(jnp.logical_not(full))
+        def _():
+            update(True)
+
         return carry
 
     lax.fori_loop(0, count, body, 0)
     o_ref[0] = (acc_sc[...] / l_sc[...]).astype(o_ref.dtype)
 
 
-def single(queries, low, high, packed, steps, sources, bases, max_steps, pieces):
+def single(queries, low, high, packed, steps, sources, bases, limits, max_steps, pieces):
     halves, tile, head_width = queries.shape
     kernel = functools.partial(
         single_kernel, max_steps=max_steps, head_width=head_width, pieces=pieces
@@ -292,7 +305,7 @@
         kernel,
         out_shape=jax.ShapeDtypeStruct(queries.shape, jnp.bfloat16),
         grid_spec=pltpu.PrefetchScalarGridSpec(
-            num_scalar_prefetch=3,
+            num_scalar_prefetch=4,
             grid=(halves,),
             in_specs=[row_spec, bound_spec, bound_spec, pl.BlockSpec(memory_space=pl.ANY)],
             out_specs=row_spec,
@@ -310,7 +323,7 @@
             transcendentals=halves * (max_steps // 2) * tile * pieces * tile,
             bytes_accessed=halves * (max_steps // 2) * pieces * tile * packed.shape[1] * 2,
         ),
-    )(steps, sources, bases, queries, low, high, packed)
+    )(steps, sources, bases, limits, queries, low, high, packed)
 
 
 def on_device(
@@ -371,14 +384,17 @@
         jnp.minimum(firsts[:, :, None] + jnp.arange(pieces, dtype=jnp.int32), 2 * cycle_size - 1),
     ) * halfway
     places_here = (pair[:, None] * halfway + jnp.arange(halfway, dtype=jnp.int32)[None, :])
+    self_low = prefix_below(places_here, ends, request_lengths).reshape(halves_here, halfway)
+    limits = jnp.stack([self_low[:, -1], places_here[:, 0]], axis=1).reshape(-1)
     single_out = single(
         mine[:, :, :head_width].reshape(halves_here, halfway, head_width),
-        prefix_below(places_here, ends, request_lengths).reshape(halves_here, halfway, 1),
+        self_low.reshape(halves_here, halfway, 1),
         places_here.reshape(halves_here, halfway, 1),
         packed,
         self_steps.astype(jnp.int32),
         self_sources.reshape(-1).astype(jnp.int32),
         (firsts * halfway).reshape(-1).astype(jnp.int32),
+        limits.astype(jnp.int32),
         self_max,
         pieces,
     )

time: 270 us -> 271 us (level)
  the two profiles are of different devices: /device:TPU:7 before, /device:TPU:1 now
where the time goes in v4:
time: 271 us; the launch traced here: 266 us
  waiting for transfers between devices  103 us (38%)
  Pallas kernels  43.6 us (16%)
  blocking collectives  41.5 us (15%)
  between operations  19 us (7%)
  matrix products  18.6 us (7%)
  local copies, waits for them, and re-layouts  17.5 us (6%)
  starting transfers between devices  11.8 us (4%)
  other arithmetic  10.5 us (4%)
    all_gather x1, waiting for transfers between devices, on_device(): packed = lax.all_gather(mine[:, :, head_width:], 'zy', axis=0, tiled=True)  55.3 us
    pallas_call x1, Pallas kernels, single(): pl.pallas_call(kernel, out_shape=jax.ShapeDtypeStruct(queries.shape, jnp....  33.8 us
    reduce_scatter x1, waiting for transfers between devices, on_device(): lax.psum_scatter(jnp.dot(attended, w_out, preferred_element_type=jnp.floa...  22.4 us
    all_gather x1, waiting for transfers between devices, on_device(): encoder = lax.all_gather(enc_kv, ('zy', 'x'), axis=1, tiled=True)  16.2 us
    all_to_all x1, blocking collectives, on_device(): mine = lax.all_to_all(per_head, 'x', 0, 0, tiled=True)  13.4 us
    all_gather x1, blocking collectives, on_device(): gathered = lax.all_gather(tokens, 'head', axis=0, tiled=True)  10.7 us
    dot_general x1, matrix products, on_device(): jnp.dot(inner, w_down, preferred_element_type=jnp.float32) + second  10 us
    pallas_call x1, Pallas kernels, flash(): pl.pallas_call(kernel, out_shape=jax.ShapeDtypeStruct(queries.shape, jnp....  9.82 us
  transfers between devices with their start and end apart: 6, of which 5 were waited for; matrix products, arithmetic and copies ran while one was open for 11% of the time, Pallas kernels for 16%

profile of v4, /device:TPU:1, one launch (start us, length us, event | category | flops | bytes accessed | tf_op | source)
XLA Modules:
  0.0 265.6 jit_solution(15789698268995822632)
XLA Ops:
  7.2 10.7 %all_gather.15 = bf16[384,1024]{1,0:T(8,128)(2,1)S(1)} all-gather(bf16[96,1024]{1,0:T(8,128)(2,1)} %param.12), channel_id=1, replica_groups=mesh['zy'=8,'x'=4,'head'=4] {'head'}, dimensions={0}, use_global_device_ids=true | all-gather | bytes 983040 | tf_op jit(solution)/shard_map/all_gather | solution.py:357
  17.9 2.4 convolution_convert_fusion
  20.5 13.4 %all_to_all.20 = bf16[4,384,192]{1,2,0:T(8,128)(2,1)S(1)} all-to-all(bf16[4,384,192]{1,2,0:T(8,128)(2,1)S(1)} %bitcast.62), channel_id=1, replica_groups=mesh['zy'=8,'x'=4,'head'=4] {'x'}, dimensions={0} | all-to-all | bytes 1179648 | tf_op jit(solution)/shard_map/all_to_all | solution.py:369
  40.0 1.2 copy.79.low_ref
  43.4 55.3 %all-gather.3.cloned.1.call-done = bf16[32,384,128]{2,1,0:T(8,128)(2,1)} async-done(((bf16[4,384,128]{2,1,0:T(8,128)(2,1)}), bf16[32,384,128]{2,1,0:T(8,128)(2,1)}) %all-gather.3.cloned.1.call-update) | async-done | bytes 3145744 | tf_op jit(solution)/shard_map/all_gather | solution.py:370
  98.8 33.8 %shard_map.139 = bf16[8,192,64]{2,1,0:T(8,128)(2,1)} custom-call(s32[8]{0:T(128)} %get-tuple-element.24.steps_ref, s32[512]{0:T(512)} %mul.192.sources_ref, s32[128]{0:T(128)} %mul.195.bases_ref, s32[16]{0:T(128)} %reshape.402.limits_ref, bf16[8,192,64]{2,1,0:T(8,128)(2,1)} %bitcast.68, s32[8,192,1]{2,1,0:T(8,128)} %copy.79.low_ref, ...), custom_call_target="tpu_custom_call" | custom-call | flops 2415919104 | bytes 12582912 | tf_op jit(solution)/shard_map/pallas_call | solution.py:304
  132.6 1.8 copy.80
  134.4 4.0 %all-to-all-start.1 = ((bf16[4,384,64]{1,2,0:T(8,128)(2,1)}), bf16[4,384,64]{1,2,0:T(8,128)(2,1)S(1)}, u32[]{:S(2)}, u32[]{:S(2)}) async-start(bf16[4,384,64]{1,2,0:T(8,128)(2,1)} %copy.80), calls=%async_computation.1 | async-start | bytes 393216 | tf_op jit(solution)/shard_map/all_to_all | solution.py:401
  138.5 5.2 %all-to-all-done.1 = bf16[4,384,64]{1,2,0:T(8,128)(2,1)S(1)} async-done(((bf16[4,384,64]{1,2,0:T(8,128)(2,1)}), bf16[4,384,64]{1,2,0:T(8,128)(2,1)S(1)}, u32[]{:S(2)}, u32[]{:S(2)}) %all-to-all-start.1) | async-done | bytes 196640 | tf_op jit(solution)/shard_map/all_to_all | solution.py:401
  143.7 1.6 fusion.99
  155.5 16.2 %all-gather.5.cloned.1.call-done = bf16[2,2048,256]{2,1,0:T(8,128)(2,1)} async-done(((bf16[2,64,256]{2,1,0:T(8,128)(2,1)}), bf16[2,2048,256]{2,1,0:T(8,128)(2,1)}) %all-gather.5.cloned.1.call-update) | async-done | bytes 2097168 | tf_op jit(solution)/shard_map/all_gather | solution.py:356
  171.7 3.2 %fusion.11 = (bf16[2496,256]{1,0:T(8,128)(2,1)}, bf16[2496,256]{1,0:T(8,128)(2,1)}) fusion(bf16[2,2048,256]{2,1,0:T(8,128)(2,1)} %all-gather.5.cloned.1.call-done), kind=kLoop, calls=%fused_computation.24 | loop fusion | bytes 4653056 | tf_op jit(solution)/shard_map/squeeze | solution.py:458
  176.8 3.5 %all-to-all-start.3 = ((bf16[4,384,128]{2,1,0:T(8,128)(2,1)}), bf16[4,384,128]{2,1,0:T(8,128)(2,1)S(1)}, u32[]{:S(2)}, u32[]{:S(2)}) async-start(bf16[4,384,128]{2,1,0:T(8,128)(2,1)} %pad_maximum_fusion), calls=%async_computation.4 | async-start | bytes 786432 | tf_op jit(solution)/shard_map/all_to_all | solution.py:421
  180.3 22.4 %reduce-scatter.2.cloned.1.call-done = f32[96,1024]{1,0:T(8,128)} async-done(((f32[384,1024]{1,0:T(8,128)}), f32[96,1024]{1,0:T(8,128)}) %reduce-scatter.2.cloned.1.call-update) | async-done | bytes 393232 | tf_op jit(solution)/shard_map/reduce_scatter | solution.py:424
  202.7 1.1 fusion.51
  203.8 1.2 multiply_reduce_fusion.2
  206.1 8.7 %all_gather.17 = bf16[384,1024]{1,0:T(8,128)(2,1)S(1)} all-gather(bf16[96,1024]{1,0:T(8,128)(2,1)S(1)} %multiply_convert_fusion.1), channel_id=1, replica_groups=mesh['zy'=8,'x'=4,'head'=4] {'head'}, dimensions={0}, use_global_device_ids=true | all-gather | bytes 983040 | tf_op jit(solution)/shard_map/all_gather | solution.py:432
  214.9 2.1 convolution_convert_fusion.1
  217.0 9.8 %shard_map.140 = bf16[2,192,256]{2,1,0:T(8,128)(2,1)} custom-call(s32[2]{0:T(128)} %and_select_fusion.2.steps_ref, s32[24]{0:T(128)} %reshape.401.sources_ref, s32[12]{0:T(128)} %min.32.bases_ref, bf16[2,192,256]{2,1,0:T(8,128)(2,1)} %bitcast.71, s32[2,192,1]{2,1,0:T(8,128)} %reshape.417.low_ref, s32[2,192,1]{2,1,0:T(8,128)} %sub.88.high_ref, ...), custom_call_target="tpu_custom_call" | custom-call | flops 3623878656 | bytes 4718592 | tf_op jit(solution)/shard_map/pallas_call | solution.py:191
  226.8 4.3 %all-to-all-start.2 = ((bf16[4,96,256]{2,1,0:T(8,128)(2,1)}), bf16[4,96,256]{2,1,0:T(8,128)(2,1)}, u32[]{:S(2)}, u32[]{:S(2)}) async-start(bf16[4,96,256]{2,1,0:T(8,128)(2,1)} %bitcast.70), calls=%async_computation.3 | async-start | bytes 393216 | tf_op jit(solution)/shard_map/all_to_all | solution.py:465
  232.3 3.3 %all-to-all-done.2 = bf16[4,96,256]{2,1,0:T(8,128)(2,1)} async-done(((bf16[4,96,256]{2,1,0:T(8,128)(2,1)}), bf16[4,96,256]{2,1,0:T(8,128)(2,1)}, u32[]{:S(2)}, u32[]{:S(2)}) %all-to-all-start.2) | async-done | bytes 196640 | tf_op jit(solution)/shard_map/all_to_all | solution.py:465
  237.4 10.0 %fusion.98 = (f32[96]{0:T(128)S(1)}, f32[96,1024]{1,0:T(8,128)S(1)}) fusion(f32[96]{0:T(128)S(1)} %add_rsqrt_fusion.1, f32[96,1024]{1,0:T(8,128)S(1)} %get-tuple-element.50, f32[96]{0:T(128)S(1)} %broadcast_multiply_fusion.2, bf16[4096,1024]{1,0:T(8,128)(2,1)} %param.22, bf16[1024,4096]{1,0:T(8,128)(2,1)} %param.21), kind=kOutput, calls=%fused_computation.183 | convolution fusion | flops 1636859776 | bytes 17564800 | tf_op jit(solution)/shard_map/dot_general | solution.py:475
  248.6 8.7 %all_gather.19 = bf16[384,1024]{1,0:T(8,128)(2,1)S(1)} all-gather(bf16[96,1024]{1,0:T(8,128)(2,1)S(1)} %get-tuple-element.22), channel_id=1, replica_groups=mesh['zy'=8,'x'=4,'head'=4] {'head'}, dimensions={0}, use_global_device_ids=true | all-gather | bytes 983040 | tf_op jit(solution)/shard_map/all_gather | solution.py:477
  257.3 1.8 convolution_bitcast_fusion
  (94 shorter events, 20.9 us)
Async XLA Ops:
  7.2 229.4 %copy-start = (bf16[1024,1024]{1,0:T(8,128)(2,1)S(1)}, bf16[1024,1024]{1,0:T(8,128)(2,1)}, u32[]{:S(2)}) copy-start(bf16[1024,1024]{1,0:T(8,128)(2,1)} %param.20) | copy-start | bytes 6291460
  7.2 91.6 %all-gather.3.cloned.1.call-start = ((), (), s32[]{:S(2)}) async-start(), calls=%async_computation.5 | async-start | bytes 3538944 | tf_op jit(solution)/shard_map/all_gather | solution.py:370
  20.4 15.2 %copy-start.5 = (s32[9]{0:T(128)S(1)}, s32[9]{0:T(128)}, u32[]{:S(2)}) copy-start(s32[9]{0:T(128)} %param.14) | copy-start | bytes 112
  20.5 15.3 %copy-start.4 = (s32[64]{0:T(128)S(1)}, s32[64]{0:T(128)}, u32[]{:S(2)}) copy-start(s32[64]{0:T(128)} %param.13) | copy-start | bytes 772
  34.8 136.9 %all-gather.5.cloned.1.call-start = ((), (), s32[]{:S(2)}) async-start(), calls=%async_computation.7 | async-start | bytes 2162688 | tf_op jit(solution)/shard_map/all_gather | solution.py:356
  98.7 44.9 %copy-start.3 = (bf16[256,1024]{1,0:T(8,128)(2,1)S(1)}, bf16[256,1024]{1,0:T(8,128)(2,1)}, u32[]{:S(2)}) copy-start(bf16[256,1024]{1,0:T(8,128)(2,1)} %param.17) | copy-start | bytes 1572868
  134.4 9.3 %all-to-all-start.1 = ((bf16[4,384,64]{1,2,0:T(8,128)(2,1)}), bf16[4,384,64]{1,2,0:T(8,128)(2,1)S(1)}, u32[]{:S(2)}, u32[]{:S(2)}) async-start(bf16[4,384,64]{1,2,0:T(8,128)(2,1)} %copy.80), calls=%async_computation.1 | async-start | bytes 393216 | tf_op jit(solution)/shard_map/all_to_all | solution.py:401
  138.4 64.3 %reduce-scatter.2.cloned.1.call-start = ((), (), s32[]{:S(2)}) async-start(), calls=%async_computation.6 | async-start | bytes 1966080 | tf_op jit(solution)/shard_map/reduce_scatter | solution.py:424
  143.7 7.3 %copy-start.6 = (s32[9]{0:T(128)S(1)}, s32[9]{0:T(128)}, u32[]{:S(2)}) copy-start(s32[9]{0:T(128)} %param.15) | copy-start | bytes 112
  174.9 27.7 %copy-start.2 = (bf16[96,1024]{1,0:T(8,128)(2,1)S(1)}, bf16[96,1024]{1,0:T(8,128)(2,1)}, u32[]{:S(2)}) copy-start(bf16[96,1024]{1,0:T(8,128)(2,1)} %param.12) | copy-start | bytes 589828
  176.8 50.0 %all-to-all-start.3 = ((bf16[4,384,128]{2,1,0:T(8,128)(2,1)}), bf16[4,384,128]{2,1,0:T(8,128)(2,1)S(1)}, u32[]{:S(2)}, u32[]{:S(2)}) async-start(bf16[4,384,128]{2,1,0:T(8,128)(2,1)} %pad_maximum_fusion), calls=%async_computation.4 | async-start | bytes 786432 | tf_op jit(solution)/shard_map/all_to_all | solution.py:421
  226.8 9.8 %copy-start.1 = (f32[96,1024]{1,0:T(8,128)S(1)}, f32[96,1024]{1,0:T(8,128)}, u32[]{:S(2)}) copy-start(f32[96,1024]{1,0:T(8,128)} %reduce-scatter.2.cloned.1.call-done) | copy-start | bytes 1179652
  226.8 8.8 %all-to-all-start.2 = ((bf16[4,96,256]{2,1,0:T(8,128)(2,1)}), bf16[4,96,256]{2,1,0:T(8,128)(2,1)}, u32[]{:S(2)}, u32[]{:S(2)}) async-start(bf16[4,96,256]{2,1,0:T(8,128)(2,1)} %bitcast.70), calls=%async_computation.3 | async-start | bytes 393216 | tf_op jit(solution)/shard_map/all_to_all | solution.py:465
  247.5 9.8 %copy-start.7 = (bf16[3,1024,256]{2,1,0:T(8,128)(2,1)S(1)}, bf16[3,1024,256]{2,1,0:T(8,128)(2,1)}, u32[]{:S(2)}) copy-start(bf16[3,1024,256]{2,1,0:T(8,128)(2,1)} %param.23) | copy-start | bytes 4718596
Sparse Core Ops, SparseCore 0:
  35.0 63.7 all-gather.2
  101.8 69.9 all-gather.4
  174.1 28.4 reduce-scatter.1

commit v5 on v4

--- a/solution.py
+++ b/solution.py
@@ -354,6 +354,9 @@
     ring_index = lax.axis_index("x")
     cycle_index = lax.axis_index("zy") * ring_size + ring_index
     encoder = lax.all_gather(enc_kv, ("zy", "x"), axis=1, tiled=True)
+    full_out = lax.all_to_all(
+        jnp.broadcast_to(w_out[None], (group_size,) + w_out.shape), "head", 0, 0, tiled=True
+    ).reshape(model_width, model_width)
     gathered = lax.all_gather(tokens, "head", axis=0, tiled=True)
     projected = jnp.einsum(
         "td,cde->cte", gathered, w_qkv, preferred_element_type=jnp.float32
@@ -398,10 +401,15 @@
         self_max,
         pieces,
     )
-    returned = lax.all_to_all(
-        single_out.reshape(ring_size, block_rows, head_width), "x", 0, 0, tiled=True
-    )
-    attended = returned.transpose(1, 0, 2).reshape(block_rows, group_width)
+    owners = lax.all_to_all(
+        single_out.reshape(ring_size * group_size, rows_here, head_width),
+        ("x", "head"),
+        0,
+        0,
+        tiled=True,
+    )
+    attended_rows = owners.reshape(ring_size, group_size, rows_here, head_width)
+    attended_rows = attended_rows.transpose(2, 1, 0, 3).reshape(rows_here, model_width)
     group_blocks = lax.axis_index("zy") * ring_size + jnp.arange(ring_size, dtype=jnp.int32)
     cache_rows = lookup(
         holders, jnp.stack([2 * group_blocks, 2 * group_blocks + 1], axis=1)
@@ -421,12 +429,7 @@
     cache_heads = lax.all_to_all(cache_parts, "x", 0, 0, tiled=True)
     cache = cache_heads.reshape(group_heads, block_rows, 2, head_width).transpose(2, 1, 0, 3)
     cache = cache.reshape(2, block_rows, group_width)
-    mixed = lax.psum_scatter(
-        jnp.dot(attended, w_out, preferred_element_type=jnp.float32),
-        "head",
-        scatter_dimension=0,
-        tiled=True,
-    )
+    mixed = jnp.dot(attended_rows, full_out, preferred_element_type=jnp.float32)
     hidden = normalize(mixed + tokens.astype(jnp.float32))
     hidden_b = hidden.astype(jnp.bfloat16)
     block_hidden = lax.all_gather(hidden_b, "head", axis=0, tiled=True)

time: 271 us -> 281 us (1.037)
  the two profiles are of different devices: /device:TPU:1 before, /device:TPU:11 now
where the time goes in v5:
time: 281 us; the launch traced here: 276 us
  waiting for transfers between devices  76.7 us (27%)
  Pallas kernels  76.6 us (27%)
  blocking collectives  39.8 us (14%)
  between operations  19.4 us (7%)
  matrix products  19.1 us (7%)
  starting transfers between devices  18.8 us (7%)
  local copies, waits for them, and re-layouts  18.2 us (6%)
  other arithmetic  7.39 us (3%)
    pallas_call x1, Pallas kernels, single(): pl.pallas_call(kernel, out_shape=jax.ShapeDtypeStruct(queries.shape, jnp....  68.4 us
    all_gather x1, waiting for transfers between devices, on_device(): packed = lax.all_gather(mine[:, :, head_width:], 'zy', axis=0, tiled=True)  54.4 us
    all_to_all x1, waiting for transfers between devices, on_device(): lax.all_to_all(jnp.broadcast_to(w_out[None], (group_size,) + w_out.shape)...  18.3 us
    all_to_all x1, blocking collectives, on_device(): mine = lax.all_to_all(per_head, 'x', 0, 0, tiled=True)  12.4 us
    dot_general x1, matrix products, on_device(): jnp.dot(inner, w_down, preferred_element_type=jnp.float32) + second  10 us
    all_gather x1, blocking collectives, on_device(): gathered = lax.all_gather(tokens, 'head', axis=0, tiled=True)  9.88 us
    all_gather x1, blocking collectives, on_device(): block_hidden = lax.all_gather(hidden_b, 'head', axis=0, tiled=True)  8.73 us
    all_gather x1, blocking collectives, on_device(): block_output = lax.all_gather(output_b, 'head', axis=0, tiled=True)  8.7 us
  transfers between devices with their start and end apart: 6, of which 3 were waited for; matrix products, arithmetic and copies ran while one was open for 10% of the time, Pallas kernels for 28%

profile of v5, /device:TPU:11, one launch (start us, length us, event | category | flops | bytes accessed | tf_op | source)
XLA Modules:
  0.0 275.9 jit_solution(3817619166484642543)
XLA Ops:
  7.2 9.9 %all_gather.15 = bf16[384,1024]{1,0:T(8,128)(2,1)S(1)} all-gather(bf16[96,1024]{1,0:T(8,128)(2,1)} %param.12), channel_id=1, replica_groups=mesh['zy'=8,'x'=4,'head'=4] {'head'}, dimensions={0}, use_global_device_ids=true | all-gather | bytes 983040 | tf_op jit(solution)/shard_map/all_gather | solution.py:360
  17.1 2.4 convolution_convert_fusion
  19.6 12.4 %all_to_all.25 = bf16[4,384,192]{1,2,0:T(8,128)(2,1)S(1)} all-to-all(bf16[4,384,192]{1,2,0:T(8,128)(2,1)S(1)} %bitcast.64), channel_id=1, replica_groups=mesh['zy'=8,'x'=4,'head'=4] {'x'}, dimensions={0} | all-to-all | bytes 1179648 | tf_op jit(solution)/shard_map/all_to_all | solution.py:372
  38.2 1.2 copy.81.low_ref
  40.2 1.0 iota_add_fusion.high_ref
  42.2 54.4 %all-gather.3.cloned.1.call-done = bf16[32,384,128]{2,1,0:T(8,128)(2,1)} async-done(((bf16[4,384,128]{2,1,0:T(8,128)(2,1)}), bf16[32,384,128]{2,1,0:T(8,128)(2,1)}) %all-gather.3.cloned.1.call-update) | async-done | bytes 3145744 | tf_op jit(solution)/shard_map/all_gather | solution.py:373
  96.6 68.4 %shard_map.139 = bf16[8,192,64]{2,1,0:T(8,128)(2,1)} custom-call(s32[8]{0:T(128)} %get-tuple-element.24.steps_ref, s32[512]{0:T(512)} %mul.192.sources_ref, s32[128]{0:T(128)} %mul.195.bases_ref, s32[16]{0:T(128)} %reshape.409.limits_ref, bf16[8,192,64]{2,1,0:T(8,128)(2,1)} %bitcast.72, s32[8,192,1]{2,1,0:T(8,128)} %copy.81.low_ref, ...), custom_call_target="tpu_custom_call" | custom-call | flops 2415919104 | bytes 12582912 | tf_op jit(solution)/shard_map/pallas_call | solution.py:304
  165.1 1.9 copy.82
  167.0 6.1 %all-to-all-start.1 = ((bf16[16,96,64]{1,2,0:T(8,128)(2,1)}), bf16[16,96,64]{1,2,0:T(8,128)(2,1)S(1)}, u32[]{:S(2)}, u32[]{:S(2)}) async-start(bf16[16,96,64]{1,2,0:T(8,128)(2,1)} %copy.82), calls=%async_computation.1 | async-start | bytes 524288 | tf_op jit(solution)/shard_map/all_to_all | solution.py:404
  181.4 1.7 broadcast_in_dim.116
  183.1 4.8 %all-to-all-start.2 = ((bf16[4,256,1024]{2,1,0:T(8,128)(2,1)}), bf16[4,256,1024]{2,1,0:T(8,128)(2,1)}, u32[]{:S(2)}, u32[]{:S(2)}) async-start(bf16[4,256,1024]{2,1,0:T(8,128)(2,1)} %broadcast_in_dim.116), calls=%async_computation.2 | async-start | bytes 4194304 | tf_op jit(solution)/shard_map/all_to_all | solution.py:357
  189.4 3.2 %fusion.11 = (bf16[2496,256]{1,0:T(8,128)(2,1)}, bf16[2496,256]{1,0:T(8,128)(2,1)}) fusion(bf16[2,2048,256]{2,1,0:T(8,128)(2,1)} %all-gather.5.cloned.1.call-done), kind=kLoop, calls=%fused_computation.24 | loop fusion | bytes 4653056 | tf_op jit(solution)/shard_map/squeeze | solution.py:461
  192.6 1.0 constant_dynamic-slice_fusion.7
  194.5 18.3 %all-to-all-done.2 = bf16[4,256,1024]{2,1,0:T(8,128)(2,1)} async-done(((bf16[4,256,1024]{2,1,0:T(8,128)(2,1)}), bf16[4,256,1024]{2,1,0:T(8,128)(2,1)}, u32[]{:S(2)}, u32[]{:S(2)}) %all-to-all-start.2) | async-done | bytes 2097184 | tf_op jit(solution)/shard_map/all_to_all | solution.py:357
  212.8 4.2 %all-to-all-start.4 = ((bf16[4,384,128]{2,1,0:T(8,128)(2,1)}), bf16[4,384,128]{2,1,0:T(8,128)(2,1)S(1)}, u32[]{:S(2)}, u32[]{:S(2)}) async-start(bf16[4,384,128]{2,1,0:T(8,128)(2,1)} %pad_maximum_fusion), calls=%async_computation.4 | async-start | bytes 786432 | tf_op jit(solution)/shard_map/all_to_all | solution.py:429
  217.0 2.2 fusion.96
  219.6 8.7 %all_gather.17 = bf16[384,1024]{1,0:T(8,128)(2,1)S(1)} all-gather(bf16[96,1024]{1,0:T(8,128)(2,1)S(1)} %multiply_convert_fusion.1), channel_id=1, replica_groups=mesh['zy'=8,'x'=4,'head'=4] {'head'}, dimensions={0}, use_global_device_ids=true | all-gather | bytes 983040 | tf_op jit(solution)/shard_map/all_gather | solution.py:435
  228.3 2.1 convolution_convert_fusion.1
  230.4 8.2 %shard_map.140 = bf16[2,192,256]{2,1,0:T(8,128)(2,1)} custom-call(s32[2]{0:T(128)} %and_select_fusion.2.steps_ref, s32[24]{0:T(128)} %reshape.408.sources_ref, s32[12]{0:T(128)} %min.32.bases_ref, bf16[2,192,256]{2,1,0:T(8,128)(2,1)} %bitcast.75, s32[2,192,1]{2,1,0:T(8,128)} %reshape.426.low_ref, s32[2,192,1]{2,1,0:T(8,128)} %sub.88.high_ref, ...), custom_call_target="tpu_custom_call" | custom-call | flops 3623878656 | bytes 4718592 | tf_op jit(solution)/shard_map/pallas_call | solution.py:191
  238.6 3.5 %all-to-all-start.3 = ((bf16[4,96,256]{2,1,0:T(8,128)(2,1)}), bf16[4,96,256]{2,1,0:T(8,128)(2,1)S(1)}, u32[]{:S(2)}, u32[]{:S(2)}) async-start(bf16[4,96,256]{2,1,0:T(8,128)(2,1)} %bitcast.74), calls=%async_computation.3 | async-start | bytes 393216 | tf_op jit(solution)/shard_map/all_to_all | solution.py:468
  243.4 3.3 %all-to-all-done.3 = bf16[4,96,256]{2,1,0:T(8,128)(2,1)S(1)} async-done(((bf16[4,96,256]{2,1,0:T(8,128)(2,1)}), bf16[4,96,256]{2,1,0:T(8,128)(2,1)S(1)}, u32[]{:S(2)}, u32[]{:S(2)}) %all-to-all-start.3) | async-done | bytes 196640 | tf_op jit(solution)/shard_map/all_to_all | solution.py:468
  247.5 10.0 %fusion.98 = (f32[96]{0:T(128)S(1)}, f32[96,1024]{1,0:T(8,128)S(1)}) fusion(f32[96]{0:T(128)S(1)} %add_rsqrt_fusion.1, f32[96,1024]{1,0:T(8,128)S(1)} %get-tuple-element.52, f32[96]{0:T(128)S(1)} %broadcast_multiply_fusion.2, bf16[4096,1024]{1,0:T(8,128)(2,1)} %param.22, bf16[1024,4096]{1,0:T(8,128)(2,1)} %param.21), kind=kOutput, calls=%fused_computation.183 | convolution fusion | flops 1636859776 | bytes 17564800 | tf_op jit(solution)/shard_map/dot_general | solution.py:478
  258.6 8.7 %all_gather.19 = bf16[384,1024]{1,0:T(8,128)(2,1)S(1)} all-gather(bf16[96,1024]{1,0:T(8,128)(2,1)S(1)} %get-tuple-element.22), channel_id=1, replica_groups=mesh['zy'=8,'x'=4,'head'=4] {'head'}, dimensions={0}, use_global_device_ids=true | all-gather | bytes 983040 | tf_op jit(solution)/shard_map/all_gather | solution.py:480
  267.3 1.8 convolution_bitcast_fusion
  (92 shorter events, 17.0 us)
Async XLA Ops:
  7.2 239.5 %copy-start = (bf16[1024,1024]{1,0:T(8,128)(2,1)S(1)}, bf16[1024,1024]{1,0:T(8,128)(2,1)}, u32[]{:S(2)}) copy-start(bf16[1024,1024]{1,0:T(8,128)(2,1)} %param.20) | copy-start | bytes 6291460
  7.2 89.4 %all-gather.3.cloned.1.call-start = ((), (), s32[]{:S(2)}) async-start(), calls=%async_computation.5 | async-start | bytes 3538944 | tf_op jit(solution)/shard_map/all_gather | solution.py:373
  19.6 14.2 %copy-start.3 = (s32[64]{0:T(128)S(1)}, s32[64]{0:T(128)}, u32[]{:S(2)}) copy-start(s32[64]{0:T(128)} %param.13) | copy-start | bytes 772
  19.6 14.5 %copy-start.4 = (s32[9]{0:T(128)S(1)}, s32[9]{0:T(128)}, u32[]{:S(2)}) copy-start(s32[9]{0:T(128)} %param.14) | copy-start | bytes 112
  32.1 7.5 %copy-start.5 = (s32[9]{0:T(128)S(1)}, s32[9]{0:T(128)}, u32[]{:S(2)}) copy-start(s32[9]{0:T(128)} %param.15) | copy-start | bytes 112
  33.1 156.3 %all-gather.5.cloned.1.call-start = ((), (), s32[]{:S(2)}) async-start(), calls=%async_computation.6 | async-start | bytes 2162688 | tf_op jit(solution)/shard_map/all_gather | solution.py:356
  165.1 16.4 %copy-start.2 = (bf16[256,1024]{1,0:T(8,128)(2,1)S(1)}, bf16[256,1024]{1,0:T(8,128)(2,1)}, u32[]{:S(2)}) copy-start(bf16[256,1024]{1,0:T(8,128)(2,1)} %param.17) | copy-start | bytes 1572868
  167.0 14.4 %all-to-all-start.1 = ((bf16[16,96,64]{1,2,0:T(8,128)(2,1)}), bf16[16,96,64]{1,2,0:T(8,128)(2,1)S(1)}, u32[]{:S(2)}, u32[]{:S(2)}) async-start(bf16[16,96,64]{1,2,0:T(8,128)(2,1)} %copy.82), calls=%async_computation.1 | async-start | bytes 524288 | tf_op jit(solution)/shard_map/all_to_all | solution.py:404
  183.1 29.7 %all-to-all-start.2 = ((bf16[4,256,1024]{2,1,0:T(8,128)(2,1)}), bf16[4,256,1024]{2,1,0:T(8,128)(2,1)}, u32[]{:S(2)}, u32[]{:S(2)}) async-start(bf16[4,256,1024]{2,1,0:T(8,128)(2,1)} %broadcast_in_dim.116), calls=%async_computation.2 | async-start | bytes 4194304 | tf_op jit(solution)/shard_map/all_to_all | solution.py:357
  193.6 23.5 %copy-start.1 = (bf16[96,1024]{1,0:T(8,128)(2,1)S(1)}, bf16[96,1024]{1,0:T(8,128)(2,1)}, u32[]{:S(2)}) copy-start(bf16[96,1024]{1,0:T(8,128)(2,1)} %param.12) | copy-start | bytes 589828
  212.8 25.8 %all-to-all-start.4 = ((bf16[4,384,128]{2,1,0:T(8,128)(2,1)}), bf16[4,384,128]{2,1,0:T(8,128)(2,1)S(1)}, u32[]{:S(2)}, u32[]{:S(2)}) async-start(bf16[4,384,128]{2,1,0:T(8,128)(2,1)} %pad_maximum_fusion), calls=%async_computation.4 | async-start | bytes 786432 | tf_op jit(solution)/shard_map/all_to_all | solution.py:429
  238.6 8.1 %all-to-all-start.3 = ((bf16[4,96,256]{2,1,0:T(8,128)(2,1)}), bf16[4,96,256]{2,1,0:T(8,128)(2,1)S(1)}, u32[]{:S(2)}, u32[]{:S(2)}) async-start(bf16[4,96,256]{2,1,0:T(8,128)(2,1)} %bitcast.74), calls=%async_computation.3 | async-start | bytes 393216 | tf_op jit(solution)/shard_map/all_to_all | solution.py:468
  257.5 9.8 %copy-start.6 = (bf16[3,1024,256]{2,1,0:T(8,128)(2,1)S(1)}, bf16[3,1024,256]{2,1,0:T(8,128)(2,1)}, u32[]{:S(2)}) copy-start(bf16[3,1024,256]{2,1,0:T(8,128)(2,1)} %param.23) | copy-start | bytes 4718596
Sparse Core Ops, SparseCore 0:
  33.2 63.3 all-gather.2
  99.6 76.8 all-gather.4

commit v6 on v5

--- a/solution.py
+++ b/solution.py
@@ -353,7 +353,6 @@
     ring_size = lax.axis_size("x")
     ring_index = lax.axis_index("x")
     cycle_index = lax.axis_index("zy") * ring_size + ring_index
-    encoder = lax.all_gather(enc_kv, ("zy", "x"), axis=1, tiled=True)
     full_out = lax.all_to_all(
         jnp.broadcast_to(w_out[None], (group_size,) + w_out.shape), "head", 0, 0, tiled=True
     ).reshape(model_width, model_width)
@@ -372,6 +371,8 @@
     mine = lax.all_to_all(per_head, "x", 0, 0, tiled=True)
     packed = lax.all_gather(mine[:, :, head_width:], "zy", axis=0, tiled=True)
     packed = packed.reshape(cycle_size * block_rows, 2 * head_width)
+    full_out, packed, late_kv = lax.optimization_barrier((full_out, packed, enc_kv))
+    encoder = lax.all_gather(late_kv, ("zy", "x"), axis=1, tiled=True)
     ends = jnp.cumsum(request_lengths).astype(jnp.int32)
     starts = ends - request_lengths
     halves_here = 2 * ring_size

time: 281 us -> 240 us (0.85)
  waiting for transfers between devices: 76.7 us -> 51.4 us
  Pallas kernels: 76.6 us -> 57.5 us
    all_gather x1, waiting for transfers between devices: 54.4 us -> 28.4 us  [on_device(): packed = lax.all_gather(mine[:, :, head_width:], 'zy', axis=0, tiled=True)]
    pallas_call x1, Pallas kernels: 68.4 us -> 49.3 us  [single(): pl.pallas_call(kernel, out_shape=jax.ShapeDtypeStruct(queries.shape, jnp....]
    all_to_all x1, waiting for transfers between devices: 0.01 us -> 4.41 us  [on_device(): lax.all_to_all(single_out.reshape(ring_size * group_size, rows_here, head...]
    all_to_all x1, waiting for transfers between devices: 18.3 us -> 15.3 us  [on_device(): lax.all_to_all(jnp.broadcast_to(w_out[None], (group_size,) + w_out.shape)...]
  transfers between devices with their start and end apart: 6 -> 6, of which waited for: 3 -> 4; matrix products, arithmetic and copies ran while one was open for 10% -> 12% of each run, Pallas kernels for 28% -> 24%
where the time goes in v6:
time: 240 us; the launch traced here: 236 us
  Pallas kernels  57.5 us (24%)
  waiting for transfers between devices  51.4 us (21%)
  blocking collectives  39.8 us (17%)
  local copies, waits for them, and re-layouts  20.9 us (9%)
  starting transfers between devices  20.5 us (9%)
  between operations  19.4 us (8%)
  matrix products  19.1 us (8%)
  other arithmetic  7.37 us (3%)
    pallas_call x1, Pallas kernels, single(): pl.pallas_call(kernel, out_shape=jax.ShapeDtypeStruct(queries.shape, jnp....  49.3 us
    all_gather x1, waiting for transfers between devices, on_device(): packed = lax.all_gather(mine[:, :, head_width:], 'zy', axis=0, tiled=True)  28.4 us
    all_to_all x1, waiting for transfers between devices, on_device(): lax.all_to_all(jnp.broadcast_to(w_out[None], (group_size,) + w_out.shape)...  15.3 us
    all_to_all x1, blocking collectives, on_device(): mine = lax.all_to_all(per_head, 'x', 0, 0, tiled=True)  12.4 us
    dot_general x1, matrix products, on_device(): jnp.dot(inner, w_down, preferred_element_type=jnp.float32) + second  10 us
    all_gather x1, blocking collectives, on_device(): gathered = lax.all_gather(tokens, 'head', axis=0, tiled=True)  9.88 us
    all_gather x1, blocking collectives, on_device(): block_hidden = lax.all_gather(hidden_b, 'head', axis=0, tiled=True)  8.72 us
    all_gather x1, blocking collectives, on_device(): block_output = lax.all_gather(output_b, 'head', axis=0, tiled=True)  8.7 us
  transfers between devices with their start and end apart: 6, of which 4 were waited for; matrix products, arithmetic and copies ran while one was open for 12% of the time, Pallas kernels for 24%

profile of v6, /device:TPU:11, one launch (start us, length us, event | category | flops | bytes accessed | tf_op | source)
XLA Modules:
  0.0 236.0 jit_solution(7499697678209029012)
XLA Ops:
  7.2 9.9 %all_gather.15 = bf16[384,1024]{1,0:T(8,128)(2,1)S(1)} all-gather(bf16[96,1024]{1,0:T(8,128)(2,1)} %param.12), channel_id=1, replica_groups=mesh['zy'=8,'x'=4,'head'=4] {'head'}, dimensions={0}, use_global_device_ids=true | all-gather | bytes 983040 | tf_op jit(solution)/shard_map/all_gather | solution.py:359
  17.1 2.4 %convolution_convert_fusion = bf16[3,256,384]{2,1,0:T(8,128)(2,1)S(1)} fusion(bf16[3,1024,256]{2,1,0:T(8,128)(2,1)} %param.16, bf16[384,1024]{1,0:T(8,128)(2,1)S(1)} %all_gather.15), kind=kOutput, calls=%fused_computation.22 | convolution fusion | flops 604274688 | bytes 2949120 | tf_op jit(solution)/shard_map/td,cde->cte/dot_general | solution.py:360
  19.6 12.4 %all_to_all.25 = bf16[4,384,192]{1,2,0:T(8,128)(2,1)S(1)} all-to-all(bf16[4,384,192]{1,2,0:T(8,128)(2,1)S(1)} %bitcast.64), channel_id=1, replica_groups=mesh['zy'=8,'x'=4,'head'=4] {'x'}, dimensions={0} | all-to-all | bytes 1179648 | tf_op jit(solution)/shard_map/all_to_all | solution.py:371
  33.1 2.7 %broadcast_in_dim.116 = bf16[4,256,1024]{2,1,0:T(8,128)(2,1)} broadcast(bf16[256,1024]{1,0:T(8,128)(2,1)} %param.17), dimensions={1,2} | broadcast | bytes 2621440 | tf_op jit(solution)/shard_map/broadcast_in_dim | solution.py:357
  35.7 6.1 %all-to-all-start.1 = ((bf16[4,256,1024]{2,1,0:T(8,128)(2,1)}), bf16[4,256,1024]{2,1,0:T(8,128)(2,1)}, u32[]{:S(2)}, u32[]{:S(2)}) async-start(bf16[4,256,1024]{2,1,0:T(8,128)(2,1)} %broadcast_in_dim.116), calls=%async_computation.1 | async-start | bytes 4194304 | tf_op jit(solution)/shard_map/all_to_all | solution.py:356
  54.5 1.2 copy.81.low_ref
  55.7 15.3 %all-to-all-done.1 = bf16[4,256,1024]{2,1,0:T(8,128)(2,1)} async-done(((bf16[4,256,1024]{2,1,0:T(8,128)(2,1)}), bf16[4,256,1024]{2,1,0:T(8,128)(2,1)}, u32[]{:S(2)}, u32[]{:S(2)}) %all-to-all-start.1) | async-done | bytes 2097184 | tf_op jit(solution)/shard_map/all_to_all | solution.py:356
  71.0 28.4 %all-gather.3.cloned.1.call-done = bf16[32,384,128]{2,1,0:T(8,128)(2,1)} async-done(((bf16[4,384,128]{2,1,0:T(8,128)(2,1)}), bf16[32,384,128]{2,1,0:T(8,128)(2,1)}) %all-gather.3.cloned.1.call-update) | async-done | bytes 3145744 | tf_op jit(solution)/shard_map/all_gather | solution.py:372
  104.0 49.3 %shard_map.139 = bf16[8,192,64]{2,1,0:T(8,128)(2,1)} custom-call(s32[8]{0:T(128)} %get-tuple-element.30.steps_ref, s32[512]{0:T(512)} %mul.192.sources_ref, s32[128]{0:T(128)} %mul.195.bases_ref, s32[16]{0:T(128)} %reshape.409.limits_ref, bf16[8,192,64]{2,1,0:T(8,128)(2,1)} %bitcast.72, s32[8,192,1]{2,1,0:T(8,128)} %copy.81.low_ref, ...), custom_call_target="tpu_custom_call" | custom-call | flops 2415919104 | bytes 12582912 | tf_op jit(solution)/shard_map/pallas_call | solution.py:304
  153.3 1.9 copy.82
  155.2 6.1 %all-to-all-start.2 = ((bf16[16,96,64]{1,2,0:T(8,128)(2,1)}), bf16[16,96,64]{1,2,0:T(8,128)(2,1)S(1)}, u32[]{:S(2)}, u32[]{:S(2)}) async-start(bf16[16,96,64]{1,2,0:T(8,128)(2,1)} %copy.82), calls=%async_computation.2 | async-start | bytes 524288 | tf_op jit(solution)/shard_map/all_to_all | solution.py:405
  161.3 1.0 constant_dynamic-slice_fusion.7
  163.2 4.4 %all-to-all-done.2 = bf16[16,96,64]{1,2,0:T(8,128)(2,1)S(1)} async-done(((bf16[16,96,64]{1,2,0:T(8,128)(2,1)}), bf16[16,96,64]{1,2,0:T(8,128)(2,1)S(1)}, u32[]{:S(2)}, u32[]{:S(2)}) %all-to-all-start.2) | async-done | bytes 196640 | tf_op jit(solution)/shard_map/all_to_all | solution.py:405
  167.6 4.8 %all-to-all-start.4 = ((bf16[4,384,128]{2,1,0:T(8,128)(2,1)}), bf16[4,384,128]{2,1,0:T(8,128)(2,1)S(1)}, u32[]{:S(2)}, u32[]{:S(2)}) async-start(bf16[4,384,128]{2,1,0:T(8,128)(2,1)} %pad_maximum_fusion), calls=%async_computation.4 | async-start | bytes 786432 | tf_op jit(solution)/shard_map/all_to_all | solution.py:430
  172.4 2.2 fusion.96
  174.9 8.7 %all_gather.17 = bf16[384,1024]{1,0:T(8,128)(2,1)S(1)} all-gather(bf16[96,1024]{1,0:T(8,128)(2,1)S(1)} %multiply_convert_fusion.1), channel_id=1, replica_groups=mesh['zy'=8,'x'=4,'head'=4] {'head'}, dimensions={0}, use_global_device_ids=true | all-gather | bytes 983040 | tf_op jit(solution)/shard_map/all_gather | solution.py:436
  183.7 2.1 convolution_convert_fusion.1
  185.8 3.2 %fusion.11 = (bf16[2496,256]{1,0:T(8,128)(2,1)}, bf16[2496,256]{1,0:T(8,128)(2,1)}) fusion(bf16[2,2048,256]{2,1,0:T(8,128)(2,1)} %all-gather.5.cloned.1.call-done), kind=kLoop, calls=%fused_computation.24 | loop fusion | bytes 4653056 | tf_op jit(solution)/shard_map/squeeze | solution.py:462
  188.9 8.2 %shard_map.140 = bf16[2,192,256]{2,1,0:T(8,128)(2,1)} custom-call(s32[2]{0:T(128)} %and_select_fusion.2.steps_ref, s32[24]{0:T(128)} %reshape.408.sources_ref, s32[12]{0:T(128)} %min.32.bases_ref, bf16[2,192,256]{2,1,0:T(8,128)(2,1)} %bitcast.75, s32[2,192,1]{2,1,0:T(8,128)} %reshape.426.low_ref, s32[2,192,1]{2,1,0:T(8,128)} %sub.88.high_ref, ...), custom_call_target="tpu_custom_call" | custom-call | flops 3623878656 | bytes 4718592 | tf_op jit(solution)/shard_map/pallas_call | solution.py:191
  197.1 3.5 %all-to-all-start.3 = ((bf16[4,96,256]{2,1,0:T(8,128)(2,1)}), bf16[4,96,256]{2,1,0:T(8,128)(2,1)S(1)}, u32[]{:S(2)}, u32[]{:S(2)}) async-start(bf16[4,96,256]{2,1,0:T(8,128)(2,1)} %bitcast.74), calls=%async_computation.3 | async-start | bytes 393216 | tf_op jit(solution)/shard_map/all_to_all | solution.py:469
  201.9 3.2 %all-to-all-done.3 = bf16[4,96,256]{2,1,0:T(8,128)(2,1)S(1)} async-done(((bf16[4,96,256]{2,1,0:T(8,128)(2,1)}), bf16[4,96,256]{2,1,0:T(8,128)(2,1)S(1)}, u32[]{:S(2)}, u32[]{:S(2)}) %all-to-all-start.3) | async-done | bytes 196640 | tf_op jit(solution)/shard_map/all_to_all | solution.py:469
  207.5 10.0 %fusion.98 = (f32[96]{0:T(128)S(1)}, f32[96,1024]{1,0:T(8,128)S(1)}) fusion(f32[96]{0:T(128)S(1)} %add_rsqrt_fusion.1, f32[96,1024]{1,0:T(8,128)S(1)} %get-tuple-element.58, f32[96]{0:T(128)S(1)} %broadcast_multiply_fusion.2, bf16[4096,1024]{1,0:T(8,128)(2,1)} %param.22, bf16[1024,4096]{1,0:T(8,128)(2,1)} %param.21), kind=kOutput, calls=%fused_computation.183 | convolution fusion | flops 1636859776 | bytes 17564800 | tf_op jit(solution)/shard_map/dot_general | solution.py:479
  218.7 8.7 %all_gather.19 = bf16[384,1024]{1,0:T(8,128)(2,1)S(1)} all-gather(bf16[96,1024]{1,0:T(8,128)(2,1)S(1)} %get-tuple-element.28), channel_id=1, replica_groups=mesh['zy'=8,'x'=4,'head'=4] {'head'}, dimensions={0}, use_global_device_ids=true | all-gather | bytes 983040 | tf_op jit(solution)/shard_map/all_gather | solution.py:481
  227.4 1.8 convolution_bitcast_fusion
  (92 shorter events, 19.0 us)
Async XLA Ops:
  7.2 199.6 %copy-start = (bf16[1024,1024]{1,0:T(8,128)(2,1)S(1)}, bf16[1024,1024]{1,0:T(8,128)(2,1)}, u32[]{:S(2)}) copy-start(bf16[1024,1024]{1,0:T(8,128)(2,1)} %param.20) | copy-start | bytes 6291460
  7.2 92.2 %all-gather.3.cloned.1.call-start = ((), (), s32[]{:S(2)}) async-start(), calls=%async_computation.5 | async-start | bytes 3538944 | tf_op jit(solution)/shard_map/all_gather | solution.py:372
  35.7 6.1 %copy-start.4 = (s32[9]{0:T(128)S(1)}, s32[9]{0:T(128)}, u32[]{:S(2)}) copy-start(s32[9]{0:T(128)} %param.14) | copy-start | bytes 112
  35.7 6.3 %copy-start.3 = (s32[64]{0:T(128)S(1)}, s32[64]{0:T(128)}, u32[]{:S(2)}) copy-start(s32[64]{0:T(128)} %param.13) | copy-start | bytes 772
  35.7 6.8 %copy-start.5 = (s32[9]{0:T(128)S(1)}, s32[9]{0:T(128)}, u32[]{:S(2)}) copy-start(s32[9]{0:T(128)} %param.15) | copy-start | bytes 112
  35.7 35.3 %all-to-all-start.1 = ((bf16[4,256,1024]{2,1,0:T(8,128)(2,1)}), bf16[4,256,1024]{2,1,0:T(8,128)(2,1)}, u32[]{:S(2)}, u32[]{:S(2)}) async-start(bf16[4,256,1024]{2,1,0:T(8,128)(2,1)} %broadcast_in_dim.116), calls=%async_computation.1 | async-start | bytes 4194304 | tf_op jit(solution)/shard_map/all_to_all | solution.py:356
  41.8 143.9 %all-gather.5.cloned.1.call-start = ((), (), s32[]{:S(2)}) async-start(), calls=%async_computation.6 | async-start | bytes 2162688 | tf_op jit(solution)/shard_map/all_gather | solution.py:375
  155.2 12.4 %all-to-all-start.2 = ((bf16[16,96,64]{1,2,0:T(8,128)(2,1)}), bf16[16,96,64]{1,2,0:T(8,128)(2,1)S(1)}, u32[]{:S(2)}, u32[]{:S(2)}) async-start(bf16[16,96,64]{1,2,0:T(8,128)(2,1)} %copy.82), calls=%async_computation.2 | async-start | bytes 524288 | tf_op jit(solution)/shard_map/all_to_all | solution.py:405
  162.3 10.1 %copy-start.2 = (bf16[96,1024]{1,0:T(8,128)(2,1)S(1)}, bf16[96,1024]{1,0:T(8,128)(2,1)}, u32[]{:S(2)}) copy-start(bf16[96,1024]{1,0:T(8,128)(2,1)} %param.12) | copy-start | bytes 589828
  167.6 29.5 %all-to-all-start.4 = ((bf16[4,384,128]{2,1,0:T(8,128)(2,1)}), bf16[4,384,128]{2,1,0:T(8,128)(2,1)S(1)}, u32[]{:S(2)}, u32[]{:S(2)}) async-start(bf16[4,384,128]{2,1,0:T(8,128)(2,1)} %pad_maximum_fusion), calls=%async_computation.4 | async-start | bytes 786432 | tf_op jit(solution)/shard_map/all_to_all | solution.py:430
  197.1 8.0 %all-to-all-start.3 = ((bf16[4,96,256]{2,1,0:T(8,128)(2,1)}), bf16[4,96,256]{2,1,0:T(8,128)(2,1)S(1)}, u32[]{:S(2)}, u32[]{:S(2)}) async-start(bf16[4,96,256]{2,1,0:T(8,128)(2,1)} %bitcast.74), calls=%async_computation.3 | async-start | bytes 393216 | tf_op jit(solution)/shard_map/all_to_all | solution.py:469
  205.1 0.7 copy-start.1
  217.5 9.8 %copy-start.6 = (bf16[3,1024,256]{2,1,0:T(8,128)(2,1)S(1)}, bf16[3,1024,256]{2,1,0:T(8,128)(2,1)}, u32[]{:S(2)}) copy-start(bf16[3,1024,256]{2,1,0:T(8,128)(2,1)} %param.23) | copy-start | bytes 4718596
Sparse Core Ops, SparseCore 0:
  33.2 66.1 all-gather.2
  102.4 71.6 all-gather.4

commit v7 on v6

--- a/solution.py
+++ b/solution.py
@@ -433,11 +433,14 @@
     mixed = jnp.dot(attended_rows, full_out, preferred_element_type=jnp.float32)
     hidden = normalize(mixed + tokens.astype(jnp.float32))
     hidden_b = hidden.astype(jnp.bfloat16)
-    block_hidden = lax.all_gather(hidden_b, "head", axis=0, tiled=True)
-    w_cq_group = lax.dynamic_slice_in_dim(w_cq, member * group_width, group_width, 1)
-    cross_query = jnp.dot(
-        block_hidden, w_cq_group, preferred_element_type=jnp.float32
-    ).astype(jnp.bfloat16)
+    own_query = jnp.dot(hidden_b, w_cq, preferred_element_type=jnp.float32).astype(jnp.bfloat16)
+    cross_query = lax.all_to_all(
+        own_query.reshape(rows_here, group_size, group_width).transpose(1, 0, 2),
+        "head",
+        0,
+        0,
+        tiled=True,
+    ).reshape(block_rows, group_width)
     encoder_rows = encoder.shape[1]
     cross_max = (encoder_rows + halfway - 1 + 2 * halfway - 1) // (2 * halfway)
     padded_encoder = jnp.pad(

time: 240 us -> 243 us (1.012)
  the two profiles are of different devices: /device:TPU:11 before, /device:TPU:71 now
where the time goes in v7:
time: 243 us; the launch traced here: 239 us
  Pallas kernels  60.9 us (25%)
  waiting for transfers between devices  55.6 us (23%)
  blocking collectives  30.1 us (12%)
  starting transfers between devices  26.7 us (11%)
  local copies, waits for them, and re-layouts  21.7 us (9%)
  between operations  19.4 us (8%)
  matrix products  17.6 us (7%)
  other arithmetic  7.26 us (3%)
    pallas_call x1, Pallas kernels, single(): pl.pallas_call(kernel, out_shape=jax.ShapeDtypeStruct(queries.shape, jnp....  49.4 us
    all_gather x1, waiting for transfers between devices, on_device(): packed = lax.all_gather(mine[:, :, head_width:], 'zy', axis=0, tiled=True)  27.1 us
    all_to_all x1, waiting for transfers between devices, on_device(): lax.all_to_all(jnp.broadcast_to(w_out[None], (group_size,) + w_out.shape)...  18.7 us
    all_to_all x1, blocking collectives, on_device(): mine = lax.all_to_all(per_head, 'x', 0, 0, tiled=True)  11.8 us
    pallas_call x1, Pallas kernels, flash(): pl.pallas_call(kernel, out_shape=jax.ShapeDtypeStruct(queries.shape, jnp....  11.5 us
    dot_general x1, matrix products, on_device(): jnp.dot(inner, w_down, preferred_element_type=jnp.float32) + second  10 us
    all_gather x1, blocking collectives, on_device(): gathered = lax.all_gather(tokens, 'head', axis=0, tiled=True)  9.59 us
    all_gather x1, blocking collectives, on_device(): block_output = lax.all_gather(output_b, 'head', axis=0, tiled=True)  8.7 us
  transfers between devices with their start and end apart: 7, of which 5 were waited for; matrix products, arithmetic and copies ran while one was open for 12% of the time, Pallas kernels for 25%

profile of v7, /device:TPU:71, one launch (start us, length us, event | category | flops | bytes accessed | tf_op | source)
XLA Modules:
  0.0 239.3 jit_solution(15824451269612190561)
XLA Ops:
  7.2 9.6 %all_gather.12 = bf16[384,1024]{1,0:T(8,128)(2,1)S(1)} all-gather(bf16[96,1024]{1,0:T(8,128)(2,1)} %param.12), channel_id=1, replica_groups=mesh['zy'=8,'x'=4,'head'=4] {'head'}, dimensions={0}, use_global_device_ids=true | all-gather | bytes 983040 | tf_op jit(solution)/shard_map/all_gather | solution.py:359
  16.8 2.4 %convolution_convert_fusion = bf16[3,256,384]{2,1,0:T(8,128)(2,1)S(1)} fusion(bf16[3,1024,256]{2,1,0:T(8,128)(2,1)} %param.16, bf16[384,1024]{1,0:T(8,128)(2,1)S(1)} %all_gather.12), kind=kOutput, calls=%fused_computation.22 | convolution fusion | flops 604274688 | bytes 2949120 | tf_op jit(solution)/shard_map/td,cde->cte/dot_general | solution.py:360
  19.3 11.8 %all_to_all.30 = bf16[4,384,192]{1,2,0:T(8,128)(2,1)S(1)} all-to-all(bf16[4,384,192]{1,2,0:T(8,128)(2,1)S(1)} %bitcast.71), channel_id=1, replica_groups=mesh['zy'=8,'x'=4,'head'=4] {'x'}, dimensions={0} | all-to-all | bytes 1179648 | tf_op jit(solution)/shard_map/all_to_all | solution.py:371
  32.1 2.7 %broadcast_in_dim.116 = bf16[4,256,1024]{2,1,0:T(8,128)(2,1)} broadcast(bf16[256,1024]{1,0:T(8,128)(2,1)} %param.17), dimensions={1,2} | broadcast | bytes 2621440 | tf_op jit(solution)/shard_map/broadcast_in_dim | solution.py:357
  34.8 6.1 %all-to-all-start.1 = ((bf16[4,256,1024]{2,1,0:T(8,128)(2,1)}), bf16[4,256,1024]{2,1,0:T(8,128)(2,1)}, u32[]{:S(2)}, u32[]{:S(2)}) async-start(bf16[4,256,1024]{2,1,0:T(8,128)(2,1)} %broadcast_in_dim.116), calls=%async_computation.1 | async-start | bytes 4194304 | tf_op jit(solution)/shard_map/all_to_all | solution.py:356
  51.3 18.7 %all-to-all-done.1 = bf16[4,256,1024]{2,1,0:T(8,128)(2,1)} async-done(((bf16[4,256,1024]{2,1,0:T(8,128)(2,1)}), bf16[4,256,1024]{2,1,0:T(8,128)(2,1)}, u32[]{:S(2)}, u32[]{:S(2)}) %all-to-all-start.1) | async-done | bytes 2097184 | tf_op jit(solution)/shard_map/all_to_all | solution.py:356
  70.0 27.1 %all-gather.3.cloned.1.call-done = bf16[32,384,128]{2,1,0:T(8,128)(2,1)} async-done(((bf16[4,384,128]{2,1,0:T(8,128)(2,1)}), bf16[32,384,128]{2,1,0:T(8,128)(2,1)}) %all-gather.3.cloned.1.call-update) | async-done | bytes 3145744 | tf_op jit(solution)/shard_map/all_gather | solution.py:372
  99.4 1.2 copy.86.low_ref
  105.1 49.4 %shard_map.139 = bf16[8,192,64]{2,1,0:T(8,128)(2,1)} custom-call(s32[8]{0:T(128)} %get-tuple-element.30.steps_ref, s32[512]{0:T(512)} %mul.189.sources_ref, s32[128]{0:T(128)} %mul.192.bases_ref, s32[16]{0:T(128)} %reshape.409.limits_ref, bf16[8,192,64]{2,1,0:T(8,128)(2,1)} %bitcast.80, s32[8,192,1]{2,1,0:T(8,128)} %copy.86.low_ref, ...), custom_call_target="tpu_custom_call" | custom-call | flops 2415919104 | bytes 12582912 | tf_op jit(solution)/shard_map/pallas_call | solution.py:304
  154.6 1.9 copy.87
  156.4 7.0 %all-to-all-start.2 = ((bf16[16,96,64]{1,2,0:T(8,128)(2,1)}), bf16[16,96,64]{1,2,0:T(8,128)(2,1)S(1)}, u32[]{:S(2)}, u32[]{:S(2)}) async-start(bf16[16,96,64]{1,2,0:T(8,128)(2,1)} %copy.87), calls=%async_computation.2 | async-start | bytes 524288 | tf_op jit(solution)/shard_map/all_to_all | solution.py:405
  163.5 1.1 constant_dynamic-slice_fusion.7
  165.4 5.2 %all-to-all-done.2 = bf16[16,96,64]{1,2,0:T(8,128)(2,1)S(1)} async-done(((bf16[16,96,64]{1,2,0:T(8,128)(2,1)}), bf16[16,96,64]{1,2,0:T(8,128)(2,1)S(1)}, u32[]{:S(2)}, u32[]{:S(2)}) %all-to-all-start.2) | async-done | bytes 196640 | tf_op jit(solution)/shard_map/all_to_all | solution.py:405
  170.7 2.3 fusion.96
  174.5 4.6 %all-to-all-start.3 = ((bf16[4,96,256]{2,1,0:T(8,128)(2,1)}), bf16[4,96,256]{2,1,0:T(8,128)(2,1)S(1)}, u32[]{:S(2)}, u32[]{:S(2)}) async-start(bf16[4,96,256]{2,1,0:T(8,128)(2,1)} %bitcast.70), calls=%async_computation.3 | async-start | bytes 393216 | tf_op jit(solution)/shard_map/all_to_all | solution.py:437
  179.1 3.2 %fusion.11 = (bf16[2496,256]{1,0:T(8,128)(2,1)}, bf16[2496,256]{1,0:T(8,128)(2,1)}) fusion(bf16[2,2048,256]{2,1,0:T(8,128)(2,1)} %all-gather.5.cloned.1.call-done), kind=kLoop, calls=%fused_computation.24 | loop fusion | bytes 4653056 | tf_op jit(solution)/shard_map/squeeze | solution.py:465
  182.2 1.3 all-to-all-done.3
  183.5 4.4 %all-to-all-start.5 = ((bf16[4,384,128]{2,1,0:T(8,128)(2,1)}), bf16[4,384,128]{2,1,0:T(8,128)(2,1)S(1)}, u32[]{:S(2)}, u32[]{:S(2)}) async-start(bf16[4,384,128]{2,1,0:T(8,128)(2,1)} %pad_maximum_fusion), calls=%async_computation.5 | async-start | bytes 786432 | tf_op jit(solution)/shard_map/all_to_all | solution.py:430
  188.0 11.5 %shard_map.140 = bf16[2,192,256]{2,1,0:T(8,128)(2,1)} custom-call(s32[2]{0:T(128)} %and_select_fusion.2.steps_ref, s32[24]{0:T(128)} %reshape.408.sources_ref, s32[12]{0:T(128)} %min.32.bases_ref, bf16[2,192,256]{2,1,0:T(8,128)(2,1)} %bitcast.82, s32[2,192,1]{2,1,0:T(8,128)} %reshape.426.low_ref, s32[2,192,1]{2,1,0:T(8,128)} %sub.88.high_ref, ...), custom_call_target="tpu_custom_call" | custom-call | flops 3623878656 | bytes 4718592 | tf_op jit(solution)/shard_map/pallas_call | solution.py:191
  199.5 4.5 %all-to-all-start.4 = ((bf16[4,96,256]{2,1,0:T(8,128)(2,1)}), bf16[4,96,256]{2,1,0:T(8,128)(2,1)S(1)}, u32[]{:S(2)}, u32[]{:S(2)}) async-start(bf16[4,96,256]{2,1,0:T(8,128)(2,1)} %bitcast.83), calls=%async_computation.4 | async-start | bytes 393216 | tf_op jit(solution)/shard_map/all_to_all | solution.py:472
  205.2 3.3 %all-to-all-done.4 = bf16[4,96,256]{2,1,0:T(8,128)(2,1)S(1)} async-done(((bf16[4,96,256]{2,1,0:T(8,128)(2,1)}), bf16[4,96,256]{2,1,0:T(8,128)(2,1)S(1)}, u32[]{:S(2)}, u32[]{:S(2)}) %all-to-all-start.4) | async-done | bytes 196640 | tf_op jit(solution)/shard_map/all_to_all | solution.py:472
  210.9 10.0 %fusion.98 = (f32[96]{0:T(128)S(1)}, f32[96,1024]{1,0:T(8,128)S(1)}) fusion(f32[96]{0:T(128)S(1)} %add_rsqrt_fusion.1, f32[96,1024]{1,0:T(8,128)S(1)} %get-tuple-element.58, f32[96]{0:T(128)S(1)} %broadcast_multiply_fusion.2, bf16[4096,1024]{1,0:T(8,128)(2,1)} %param.22, bf16[1024,4096]{1,0:T(8,128)(2,1)} %param.21), kind=kOutput, calls=%fused_computation.184 | convolution fusion | flops 1636859776 | bytes 17564800 | tf_op jit(solution)/shard_map/dot_general | solution.py:482
  222.0 8.7 %all_gather.15 = bf16[384,1024]{1,0:T(8,128)(2,1)S(1)} all-gather(bf16[96,1024]{1,0:T(8,128)(2,1)S(1)} %get-tuple-element.28), channel_id=1, replica_groups=mesh['zy'=8,'x'=4,'head'=4] {'head'}, dimensions={0}, use_global_device_ids=true | all-gather | bytes 983040 | tf_op jit(solution)/shard_map/all_gather | solution.py:484
  230.7 1.8 convolution_bitcast_fusion
  (97 shorter events, 20.1 us)
Async XLA Ops:
  7.2 202.9 %copy-start = (bf16[1024,1024]{1,0:T(8,128)(2,1)S(1)}, bf16[1024,1024]{1,0:T(8,128)(2,1)}, u32[]{:S(2)}) copy-start(bf16[1024,1024]{1,0:T(8,128)(2,1)} %param.20) | copy-start | bytes 6291460
  7.2 89.9 %all-gather.3.cloned.1.call-start = ((), (), s32[]{:S(2)}) async-start(), calls=%async_computation.6 | async-start | bytes 3538944 | tf_op jit(solution)/shard_map/all_gather | solution.py:372
  34.8 6.1 %copy-start.5 = (s32[64]{0:T(128)S(1)}, s32[64]{0:T(128)}, u32[]{:S(2)}) copy-start(s32[64]{0:T(128)} %param.13) | copy-start | bytes 772
  34.8 12.2 %copy-start.6 = (s32[9]{0:T(128)S(1)}, s32[9]{0:T(128)}, u32[]{:S(2)}) copy-start(s32[9]{0:T(128)} %param.14) | copy-start | bytes 112
  34.8 12.5 %copy-start.7 = (s32[9]{0:T(128)S(1)}, s32[9]{0:T(128)}, u32[]{:S(2)}) copy-start(s32[9]{0:T(128)} %param.15) | copy-start | bytes 112
  34.8 35.3 %all-to-all-start.1 = ((bf16[4,256,1024]{2,1,0:T(8,128)(2,1)}), bf16[4,256,1024]{2,1,0:T(8,128)(2,1)}, u32[]{:S(2)}, u32[]{:S(2)}) async-start(bf16[4,256,1024]{2,1,0:T(8,128)(2,1)} %broadcast_in_dim.116), calls=%async_computation.1 | async-start | bytes 4194304 | tf_op jit(solution)/shard_map/all_to_all | solution.py:356
  40.9 138.2 %all-gather.5.cloned.1.call-start = ((), (), s32[]{:S(2)}) async-start(), calls=%async_computation.7 | async-start | bytes 2162688 | tf_op jit(solution)/shard_map/all_gather | solution.py:375
  156.4 14.2 %all-to-all-start.2 = ((bf16[16,96,64]{1,2,0:T(8,128)(2,1)}), bf16[16,96,64]{1,2,0:T(8,128)(2,1)S(1)}, u32[]{:S(2)}, u32[]{:S(2)}) async-start(bf16[16,96,64]{1,2,0:T(8,128)(2,1)} %copy.87), calls=%async_computation.2 | async-start | bytes 524288 | tf_op jit(solution)/shard_map/all_to_all | solution.py:405
  163.5 7.1 %copy-start.3 = (bf16[96,1024]{1,0:T(8,128)(2,1)S(1)}, bf16[96,1024]{1,0:T(8,128)(2,1)}, u32[]{:S(2)}) copy-start(bf16[96,1024]{1,0:T(8,128)(2,1)} %param.12) | copy-start | bytes 589828
  170.6 2.6 %copy-start.1 = (bf16[1024,1024]{1,0:T(8,128)(2,1)S(1)}, bf16[1024,1024]{1,0:T(8,128)(2,1)}, u32[]{:S(2)}) copy-start(bf16[1024,1024]{1,0:T(8,128)(2,1)} %param.19) | copy-start | bytes 6291460
  174.5 9.1 %all-to-all-start.3 = ((bf16[4,96,256]{2,1,0:T(8,128)(2,1)}), bf16[4,96,256]{2,1,0:T(8,128)(2,1)S(1)}, u32[]{:S(2)}, u32[]{:S(2)}) async-start(bf16[4,96,256]{2,1,0:T(8,128)(2,1)} %bitcast.70), calls=%async_computation.3 | async-start | bytes 393216 | tf_op jit(solution)/shard_map/all_to_all | solution.py:437
  183.5 4.5 %copy-start.4 = (bf16[4,96,256]{2,1,0:T(8,128)(2,1)}, bf16[4,96,256]{2,1,0:T(8,128)(2,1)S(1)}, u32[]{:S(2)}) copy-start(bf16[4,96,256]{2,1,0:T(8,128)(2,1)S(1)} %all-to-all-done.3) | copy-start | bytes 589828
  183.5 15.9 %all-to-all-start.5 = ((bf16[4,384,128]{2,1,0:T(8,128)(2,1)}), bf16[4,384,128]{2,1,0:T(8,128)(2,1)S(1)}, u32[]{:S(2)}, u32[]{:S(2)}) async-start(bf16[4,384,128]{2,1,0:T(8,128)(2,1)} %pad_maximum_fusion), calls=%async_computation.5 | async-start | bytes 786432 | tf_op jit(solution)/shard_map/all_to_all | solution.py:430
  199.5 9.0 %all-to-all-start.4 = ((bf16[4,96,256]{2,1,0:T(8,128)(2,1)}), bf16[4,96,256]{2,1,0:T(8,128)(2,1)S(1)}, u32[]{:S(2)}, u32[]{:S(2)}) async-start(bf16[4,96,256]{2,1,0:T(8,128)(2,1)} %bitcast.83), calls=%async_computation.4 | async-start | bytes 393216 | tf_op jit(solution)/shard_map/all_to_all | solution.py:472
  208.4 0.7 copy-start.2
  220.9 9.8 %copy-start.8 = (bf16[3,1024,256]{2,1,0:T(8,128)(2,1)S(1)}, bf16[3,1024,256]{2,1,0:T(8,128)(2,1)}, u32[]{:S(2)}) copy-start(bf16[3,1024,256]{2,1,0:T(8,128)(2,1)} %param.23) | copy-start | bytes 4718596
Sparse Core Ops, SparseCore 0:
  32.2 64.8 all-gather.2
  100.1 70.6 all-gather.4

commit v8 on v7

--- a/solution.py
+++ b/solution.py
@@ -379,7 +379,7 @@
     first_half = lax.axis_index("zy") * halves_here
     pair = lax.dynamic_slice_in_dim(block_order, first_half, halves_here, 0)
     low_block = prefix_below(pair * halfway, ends, request_lengths) // halfway
-    pieces = 4
+    pieces = 8
     self_steps = (pair - low_block) // pieces + 1
     self_max = (2 * cycle_size + pieces - 1) // pieces
     firsts = low_block[:, None] + pieces * jnp.arange(self_max, dtype=jnp.int32)[None, :]

time: 243 us -> 236 us (0.971)
  the two profiles are of different devices: /device:TPU:71 before, /device:TPU:1 now
where the time goes in v8:
time: 236 us; the launch traced here: 231 us
  waiting for transfers between devices  66.2 us (28%)
  Pallas kernels  41.6 us (18%)
  blocking collectives  32.8 us (14%)
  starting transfers between devices  24.4 us (10%)
  local copies, waits for them, and re-layouts  21.5 us (9%)
  between operations  19.4 us (8%)
  matrix products  17.6 us (7%)
  other arithmetic  7.84 us (3%)
    pallas_call x1, Pallas kernels, single(): pl.pallas_call(kernel, out_shape=jax.ShapeDtypeStruct(queries.shape, jnp....  33.4 us
    all_gather x1, waiting for transfers between devices, on_device(): packed = lax.all_gather(mine[:, :, head_width:], 'zy', axis=0, tiled=True)  28.8 us
    all_to_all x1, waiting for transfers between devices, on_device(): lax.all_to_all(jnp.broadcast_to(w_out[None], (group_size,) + w_out.shape)...  18.7 us
    all_to_all x1, blocking collectives, on_device(): mine = lax.all_to_all(per_head, 'x', 0, 0, tiled=True)  13.4 us
    all_gather x1, blocking collectives, on_device(): gathered = lax.all_gather(tokens, 'head', axis=0, tiled=True)  10.7 us
    dot_general x1, matrix products, on_device(): jnp.dot(inner, w_down, preferred_element_type=jnp.float32) + second  10 us
    all_gather x1, waiting for transfers between devices, on_device(): encoder = lax.all_gather(late_kv, ('zy', 'x'), axis=1, tiled=True)  9.88 us
    all_gather x1, blocking collectives, on_device(): block_output = lax.all_gather(output_b, 'head', axis=0, tiled=True)  8.7 us
  transfers between devices with their start and end apart: 7, of which 5 were waited for; matrix products, arithmetic and copies ran while one was open for 12% of the time, Pallas kernels for 18%

profile of v8, /device:TPU:1, one launch (start us, length us, event | category | flops | bytes accessed | tf_op | source)
XLA Modules:
  0.0 231.3 jit_solution(12891123828181076569)
XLA Ops:
  7.2 10.7 %all_gather.12 = bf16[384,1024]{1,0:T(8,128)(2,1)S(1)} all-gather(bf16[96,1024]{1,0:T(8,128)(2,1)} %param.12), channel_id=1, replica_groups=mesh['zy'=8,'x'=4,'head'=4] {'head'}, dimensions={0}, use_global_device_ids=true | all-gather | bytes 983040 | tf_op jit(solution)/shard_map/all_gather | solution.py:359
  17.9 2.4 %convolution_convert_fusion = bf16[3,256,384]{2,1,0:T(8,128)(2,1)S(1)} fusion(bf16[3,1024,256]{2,1,0:T(8,128)(2,1)} %param.16, bf16[384,1024]{1,0:T(8,128)(2,1)S(1)} %all_gather.12), kind=kOutput, calls=%fused_computation.22 | convolution fusion | flops 604274688 | bytes 2949120 | tf_op jit(solution)/shard_map/td,cde->cte/dot_general | solution.py:360
  20.4 13.4 %all_to_all.30 = bf16[4,384,192]{1,2,0:T(8,128)(2,1)S(1)} all-to-all(bf16[4,384,192]{1,2,0:T(8,128)(2,1)S(1)} %bitcast.71), channel_id=1, replica_groups=mesh['zy'=8,'x'=4,'head'=4] {'x'}, dimensions={0} | all-to-all | bytes 1179648 | tf_op jit(solution)/shard_map/all_to_all | solution.py:371
  34.8 2.7 %broadcast_in_dim.116 = bf16[4,256,1024]{2,1,0:T(8,128)(2,1)} broadcast(bf16[256,1024]{1,0:T(8,128)(2,1)} %param.17), dimensions={1,2} | broadcast | bytes 2621440 | tf_op jit(solution)/shard_map/broadcast_in_dim | solution.py:357
  37.5 6.1 %all-to-all-start.1 = ((bf16[4,256,1024]{2,1,0:T(8,128)(2,1)}), bf16[4,256,1024]{2,1,0:T(8,128)(2,1)}, u32[]{:S(2)}, u32[]{:S(2)}) async-start(bf16[4,256,1024]{2,1,0:T(8,128)(2,1)} %broadcast_in_dim.116), calls=%async_computation.1 | async-start | bytes 4194304 | tf_op jit(solution)/shard_map/all_to_all | solution.py:356
  54.0 18.7 %all-to-all-done.1 = bf16[4,256,1024]{2,1,0:T(8,128)(2,1)} async-done(((bf16[4,256,1024]{2,1,0:T(8,128)(2,1)}), bf16[4,256,1024]{2,1,0:T(8,128)(2,1)}, u32[]{:S(2)}, u32[]{:S(2)}) %all-to-all-start.1) | async-done | bytes 2097184 | tf_op jit(solution)/shard_map/all_to_all | solution.py:356
  72.7 28.8 %all-gather.3.cloned.1.call-done = bf16[32,384,128]{2,1,0:T(8,128)(2,1)} async-done(((bf16[4,384,128]{2,1,0:T(8,128)(2,1)}), bf16[32,384,128]{2,1,0:T(8,128)(2,1)}) %all-gather.3.cloned.1.call-update) | async-done | bytes 3145744 | tf_op jit(solution)/shard_map/all_gather | solution.py:372
  101.6 1.2 select_reduce_fusion
  104.2 1.2 copy.68.low_ref
  110.0 33.4 %shard_map.139 = bf16[8,192,64]{2,1,0:T(8,128)(2,1)} custom-call(s32[8]{0:T(128)} %get-tuple-element.27.steps_ref, s32[512]{0:T(512)} %mul.189.sources_ref, s32[64]{0:T(128)} %mul.192.bases_ref, s32[16]{0:T(128)} %reshape.409.limits_ref, bf16[8,192,64]{2,1,0:T(8,128)(2,1)} %bitcast.80, s32[8,192,1]{2,1,0:T(8,128)} %copy.68.low_ref, ...), custom_call_target="tpu_custom_call" | custom-call | flops 2415919104 | bytes 12582912 | tf_op jit(solution)/shard_map/pallas_call | solution.py:304
  143.4 1.9 copy.69
  145.2 5.4 %all-to-all-start.2 = ((bf16[16,96,64]{1,2,0:T(8,128)(2,1)}), bf16[16,96,64]{1,2,0:T(8,128)(2,1)S(1)}, u32[]{:S(2)}, u32[]{:S(2)}) async-start(bf16[16,96,64]{1,2,0:T(8,128)(2,1)} %copy.69), calls=%async_computation.2 | async-start | bytes 524288 | tf_op jit(solution)/shard_map/all_to_all | solution.py:405
  152.5 5.5 %all-to-all-done.2 = bf16[16,96,64]{1,2,0:T(8,128)(2,1)S(1)} async-done(((bf16[16,96,64]{1,2,0:T(8,128)(2,1)}), bf16[16,96,64]{1,2,0:T(8,128)(2,1)S(1)}, u32[]{:S(2)}, u32[]{:S(2)}) %all-to-all-start.2) | async-done | bytes 196640 | tf_op jit(solution)/shard_map/all_to_all | solution.py:405
  158.1 2.3 %fusion.96 = (f32[96]{0:T(128)S(1)}, f32[96,1024]{1,0:T(8,128)S(1)}) fusion(bf16[96,1024]{1,0:T(8,128)(2,1)S(1)} %copy-done.3, bf16[96,1024]{0,1:T(8,128)(2,1)S(1)} %bitcast.74, bf16[1024,1024]{1,0:T(8,128)(2,1)} %bitcast.9), kind=kOutput, calls=%fused_computation.182 | convolution fusion | flops 201621408 | bytes 2883968 | tf_op jit(solution)/shard_map/dot_general | solution.py:433
  161.8 3.7 %all-to-all-start.3 = ((bf16[4,96,256]{2,1,0:T(8,128)(2,1)}), bf16[4,96,256]{2,1,0:T(8,128)(2,1)S(1)}, u32[]{:S(2)}, u32[]{:S(2)}) async-start(bf16[4,96,256]{2,1,0:T(8,128)(2,1)} %bitcast.70), calls=%async_computation.3 | async-start | bytes 393216 | tf_op jit(solution)/shard_map/all_to_all | solution.py:437
  165.6 9.9 %all-gather.5.cloned.1.call-done = bf16[2,2048,256]{2,1,0:T(8,128)(2,1)} async-done(((bf16[2,64,256]{2,1,0:T(8,128)(2,1)}), bf16[2,2048,256]{2,1,0:T(8,128)(2,1)}) %all-gather.5.cloned.1.call-update) | async-done | bytes 2097168 | tf_op jit(solution)/shard_map/all_gather | solution.py:375
  175.5 3.2 %fusion.11 = (bf16[2496,256]{1,0:T(8,128)(2,1)}, bf16[2496,256]{1,0:T(8,128)(2,1)}) fusion(bf16[2,2048,256]{2,1,0:T(8,128)(2,1)} %all-gather.5.cloned.1.call-done), kind=kLoop, calls=%fused_computation.24 | loop fusion | bytes 4653056 | tf_op jit(solution)/shard_map/squeeze | solution.py:465
  178.6 4.0 %all-to-all-start.5 = ((bf16[4,384,128]{2,1,0:T(8,128)(2,1)}), bf16[4,384,128]{2,1,0:T(8,128)(2,1)S(1)}, u32[]{:S(2)}, u32[]{:S(2)}) async-start(bf16[4,384,128]{2,1,0:T(8,128)(2,1)} %pad_maximum_fusion), calls=%async_computation.5 | async-start | bytes 786432 | tf_op jit(solution)/shard_map/all_to_all | solution.py:430
  182.6 8.2 %shard_map.140 = bf16[2,192,256]{2,1,0:T(8,128)(2,1)} custom-call(s32[2]{0:T(128)} %and_select_fusion.2.steps_ref, s32[24]{0:T(128)} %reshape.408.sources_ref, s32[12]{0:T(128)} %min.32.bases_ref, bf16[2,192,256]{2,1,0:T(8,128)(2,1)} %bitcast.82, s32[2,192,1]{2,1,0:T(8,128)} %reshape.426.low_ref, s32[2,192,1]{2,1,0:T(8,128)} %sub.88.high_ref, ...), custom_call_target="tpu_custom_call" | custom-call | flops 3623878656 | bytes 4718592 | tf_op jit(solution)/shard_map/pallas_call | solution.py:191
  190.8 5.2 %all-to-all-start.4 = ((bf16[4,96,256]{2,1,0:T(8,128)(2,1)}), bf16[4,96,256]{2,1,0:T(8,128)(2,1)S(1)}, u32[]{:S(2)}, u32[]{:S(2)}) async-start(bf16[4,96,256]{2,1,0:T(8,128)(2,1)} %bitcast.83), calls=%async_computation.4 | async-start | bytes 393216 | tf_op jit(solution)/shard_map/all_to_all | solution.py:472
  197.2 3.3 %all-to-all-done.4 = bf16[4,96,256]{2,1,0:T(8,128)(2,1)S(1)} async-done(((bf16[4,96,256]{2,1,0:T(8,128)(2,1)}), bf16[4,96,256]{2,1,0:T(8,128)(2,1)S(1)}, u32[]{:S(2)}, u32[]{:S(2)}) %all-to-all-start.4) | async-done | bytes 196640 | tf_op jit(solution)/shard_map/all_to_all | solution.py:472
  202.9 10.0 %fusion.98 = (f32[96]{0:T(128)S(1)}, f32[96,1024]{1,0:T(8,128)S(1)}) fusion(f32[96]{0:T(128)S(1)} %add_rsqrt_fusion.1, f32[96,1024]{1,0:T(8,128)S(1)} %get-tuple-element.55, f32[96]{0:T(128)S(1)} %broadcast_multiply_fusion.3, bf16[4096,1024]{1,0:T(8,128)(2,1)} %param.22, bf16[1024,4096]{1,0:T(8,128)(2,1)} %param.21), kind=kOutput, calls=%fused_computation.184 | convolution fusion | flops 1636859776 | bytes 17564800 | tf_op jit(solution)/shard_map/dot_general | solution.py:482
  214.0 8.7 %all_gather.15 = bf16[384,1024]{1,0:T(8,128)(2,1)S(1)} all-gather(bf16[96,1024]{1,0:T(8,128)(2,1)S(1)} %get-tuple-element.25), channel_id=1, replica_groups=mesh['zy'=8,'x'=4,'head'=4] {'head'}, dimensions={0}, use_global_device_ids=true | all-gather | bytes 983040 | tf_op jit(solution)/shard_map/all_gather | solution.py:484
  222.7 1.8 convolution_bitcast_fusion
  (96 shorter events, 20.4 us)
Async XLA Ops:
  7.2 194.9 %copy-start = (bf16[1024,1024]{1,0:T(8,128)(2,1)S(1)}, bf16[1024,1024]{1,0:T(8,128)(2,1)}, u32[]{:S(2)}) copy-start(bf16[1024,1024]{1,0:T(8,128)(2,1)} %param.20) | copy-start | bytes 6291460
  7.2 94.3 %all-gather.3.cloned.1.call-start = ((), (), s32[]{:S(2)}) async-start(), calls=%async_computation.6 | async-start | bytes 3538944 | tf_op jit(solution)/shard_map/all_gather | solution.py:372
  37.5 6.1 %copy-start.5 = (s32[64]{0:T(128)S(1)}, s32[64]{0:T(128)}, u32[]{:S(2)}) copy-start(s32[64]{0:T(128)} %param.13) | copy-start | bytes 772
  37.5 12.2 %copy-start.6 = (s32[9]{0:T(128)S(1)}, s32[9]{0:T(128)}, u32[]{:S(2)}) copy-start(s32[9]{0:T(128)} %param.14) | copy-start | bytes 112
  37.5 12.5 %copy-start.7 = (s32[9]{0:T(128)S(1)}, s32[9]{0:T(128)}, u32[]{:S(2)}) copy-start(s32[9]{0:T(128)} %param.15) | copy-start | bytes 112
  37.5 35.3 %all-to-all-start.1 = ((bf16[4,256,1024]{2,1,0:T(8,128)(2,1)}), bf16[4,256,1024]{2,1,0:T(8,128)(2,1)}, u32[]{:S(2)}, u32[]{:S(2)}) async-start(bf16[4,256,1024]{2,1,0:T(8,128)(2,1)} %broadcast_in_dim.116), calls=%async_computation.1 | async-start | bytes 4194304 | tf_op jit(solution)/shard_map/all_to_all | solution.py:356
  43.6 131.9 %all-gather.5.cloned.1.call-start = ((), (), s32[]{:S(2)}) async-start(), calls=%async_computation.7 | async-start | bytes 2162688 | tf_op jit(solution)/shard_map/all_gather | solution.py:375
  145.2 12.8 %all-to-all-start.2 = ((bf16[16,96,64]{1,2,0:T(8,128)(2,1)}), bf16[16,96,64]{1,2,0:T(8,128)(2,1)S(1)}, u32[]{:S(2)}, u32[]{:S(2)}) async-start(bf16[16,96,64]{1,2,0:T(8,128)(2,1)} %copy.69), calls=%async_computation.2 | async-start | bytes 524288 | tf_op jit(solution)/shard_map/all_to_all | solution.py:405
  150.6 7.4 %copy-start.3 = (bf16[96,1024]{1,0:T(8,128)(2,1)S(1)}, bf16[96,1024]{1,0:T(8,128)(2,1)}, u32[]{:S(2)}) copy-start(bf16[96,1024]{1,0:T(8,128)(2,1)} %param.12) | copy-start | bytes 589828
  158.0 2.6 %copy-start.1 = (bf16[1024,1024]{1,0:T(8,128)(2,1)S(1)}, bf16[1024,1024]{1,0:T(8,128)(2,1)}, u32[]{:S(2)}) copy-start(bf16[1024,1024]{1,0:T(8,128)(2,1)} %param.19) | copy-start | bytes 6291460
  161.8 16.8 %all-to-all-start.3 = ((bf16[4,96,256]{2,1,0:T(8,128)(2,1)}), bf16[4,96,256]{2,1,0:T(8,128)(2,1)S(1)}, u32[]{:S(2)}, u32[]{:S(2)}) async-start(bf16[4,96,256]{2,1,0:T(8,128)(2,1)} %bitcast.70), calls=%async_computation.3 | async-start | bytes 393216 | tf_op jit(solution)/shard_map/all_to_all | solution.py:437
  178.6 4.0 %copy-start.4 = (bf16[4,96,256]{2,1,0:T(8,128)(2,1)}, bf16[4,96,256]{2,1,0:T(8,128)(2,1)S(1)}, u32[]{:S(2)}) copy-start(bf16[4,96,256]{2,1,0:T(8,128)(2,1)S(1)} %all-to-all-done.3) | copy-start | bytes 589828
  178.6 12.2 %all-to-all-start.5 = ((bf16[4,384,128]{2,1,0:T(8,128)(2,1)}), bf16[4,384,128]{2,1,0:T(8,128)(2,1)S(1)}, u32[]{:S(2)}, u32[]{:S(2)}) async-start(bf16[4,384,128]{2,1,0:T(8,128)(2,1)} %pad_maximum_fusion), calls=%async_computation.5 | async-start | bytes 786432 | tf_op jit(solution)/shard_map/all_to_all | solution.py:430
  190.8 9.7 %all-to-all-start.4 = ((bf16[4,96,256]{2,1,0:T(8,128)(2,1)}), bf16[4,96,256]{2,1,0:T(8,128)(2,1)S(1)}, u32[]{:S(2)}, u32[]{:S(2)}) async-start(bf16[4,96,256]{2,1,0:T(8,128)(2,1)} %bitcast.83), calls=%async_computation.4 | async-start | bytes 393216 | tf_op jit(solution)/shard_map/all_to_all | solution.py:472
  200.5 0.7 copy-start.2
  212.9 9.8 %copy-start.8 = (bf16[3,1024,256]{2,1,0:T(8,128)(2,1)S(1)}, bf16[3,1024,256]{2,1,0:T(8,128)(2,1)}, u32[]{:S(2)}) copy-start(bf16[3,1024,256]{2,1,0:T(8,128)(2,1)} %param.23) | copy-start | bytes 4718596
Sparse Core Ops, SparseCore 0:
  34.9 66.5 all-gather.2
  104.5 70.8 all-gather.4

commit v9 on v8

--- a/solution.py
+++ b/solution.py
@@ -356,6 +356,9 @@
     full_out = lax.all_to_all(
         jnp.broadcast_to(w_out[None], (group_size,) + w_out.shape), "head", 0, 0, tiled=True
     ).reshape(model_width, model_width)
+    enc_all = lax.all_to_all(
+        jnp.broadcast_to(enc_kv[None], (cycle_size,) + enc_kv.shape), ("zy", "x"), 0, 0, tiled=True
+    )
     gathered = lax.all_gather(tokens, "head", axis=0, tiled=True)
     projected = jnp.einsum(
         "td,cde->cte", gathered, w_qkv, preferred_element_type=jnp.float32
@@ -371,8 +374,10 @@
     mine = lax.all_to_all(per_head, "x", 0, 0, tiled=True)
     packed = lax.all_gather(mine[:, :, head_width:], "zy", axis=0, tiled=True)
     packed = packed.reshape(cycle_size * block_rows, 2 * head_width)
-    full_out, packed, late_kv = lax.optimization_barrier((full_out, packed, enc_kv))
-    encoder = lax.all_gather(late_kv, ("zy", "x"), axis=1, tiled=True)
+    full_out, packed, enc_all = lax.optimization_barrier((full_out, packed, enc_all))
+    encoder = enc_all.transpose(1, 0, 2, 3).reshape(
+        2, cycle_size * enc_kv.shape[1], enc_kv.shape[2]
+    )
     ends = jnp.cumsum(request_lengths).astype(jnp.int32)
     starts = ends - request_lengths
     halves_here = 2 * ring_size

time: 236 us -> 248 us (1.051)
  the two profiles are of different devices: /device:TPU:1 before, /device:TPU:93 now
where the time goes in v9:
time: 248 us; the launch traced here: 245 us
  Pallas kernels  56.1 us (23%)
  waiting for transfers between devices  55.4 us (22%)
  starting transfers between devices  37.3 us (15%)
  blocking collectives  29.8 us (12%)
  local copies, waits for them, and re-layouts  21.5 us (9%)
  between operations  19.5 us (8%)
  matrix products  17.6 us (7%)
  other arithmetic  7.75 us (3%)
    pallas_call x1, Pallas kernels, single(): pl.pallas_call(kernel, out_shape=jax.ShapeDtypeStruct(queries.shape, jnp....  44.6 us
    all_to_all x1, waiting for transfers between devices, on_device(): lax.all_to_all(jnp.broadcast_to(w_out[None], (group_size,) + w_out.shape)...  18.8 us
    all_to_all x1, waiting for transfers between devices, on_device(): lax.all_to_all(jnp.broadcast_to(enc_kv[None], (cycle_size,) + enc_kv.shap...  18.6 us
    pallas_call x1, Pallas kernels, flash(): pl.pallas_call(kernel, out_shape=jax.ShapeDtypeStruct(queries.shape, jnp....  11.5 us
    all_to_all x1, blocking collectives, on_device(): mine = lax.all_to_all(per_head, 'x', 0, 0, tiled=True)  11.5 us
    dot_general x1, matrix products, on_device(): jnp.dot(inner, w_down, preferred_element_type=jnp.float32) + second  10 us
    all_gather x1, waiting for transfers between devices, on_device(): packed = lax.all_gather(mine[:, :, head_width:], 'zy', axis=0, tiled=True)  9.98 us
    all_gather x1, blocking collectives, on_device(): gathered = lax.all_gather(tokens, 'head', axis=0, tiled=True)  9.59 us
  transfers between devices with their start and end apart: 7, of which 6 were waited for; matrix products, arithmetic and copies ran while one was open for 10% of the time, Pallas kernels for 5%

profile of v9, /device:TPU:93, one launch (start us, length us, event | category | flops | bytes accessed | tf_op | source)
XLA Modules:
  0.0 245.0 jit_solution(13854144877502464492)
XLA Ops:
  7.2 9.6 %all_gather.9 = bf16[384,1024]{1,0:T(8,128)(2,1)S(1)} all-gather(bf16[96,1024]{1,0:T(8,128)(2,1)} %param.12), channel_id=1, replica_groups=mesh['zy'=8,'x'=4,'head'=4] {'head'}, dimensions={0}, use_global_device_ids=true | all-gather | bytes 983040 | tf_op jit(solution)/shard_map/all_gather | solution.py:362
  16.8 2.4 convolution_convert_fusion
  19.3 11.5 %all_to_all.35 = bf16[4,384,192]{1,2,0:T(8,128)(2,1)S(1)} all-to-all(bf16[4,384,192]{1,2,0:T(8,128)(2,1)S(1)} %bitcast.74), channel_id=1, replica_groups=mesh['zy'=8,'x'=4,'head'=4] {'x'}, dimensions={0} | all-to-all | bytes 1179648 | tf_op jit(solution)/shard_map/all_to_all | solution.py:374
  31.8 2.7 %broadcast_in_dim.122 = bf16[4,256,1024]{2,1,0:T(8,128)(2,1)} broadcast(bf16[256,1024]{1,0:T(8,128)(2,1)} %param.17), dimensions={1,2} | broadcast | bytes 2621440 | tf_op jit(solution)/shard_map/broadcast_in_dim | solution.py:357
  34.5 6.0 %all-to-all-start.1 = ((bf16[4,256,1024]{2,1,0:T(8,128)(2,1)}), bf16[4,256,1024]{2,1,0:T(8,128)(2,1)}, u32[]{:S(2)}, u32[]{:S(2)}) async-start(bf16[4,256,1024]{2,1,0:T(8,128)(2,1)} %broadcast_in_dim.122), calls=%async_computation.1 | async-start | bytes 4194304 | tf_op jit(solution)/shard_map/all_to_all | solution.py:356
  50.8 18.8 %all-to-all-done.1 = bf16[4,256,1024]{2,1,0:T(8,128)(2,1)} async-done(((bf16[4,256,1024]{2,1,0:T(8,128)(2,1)}), bf16[4,256,1024]{2,1,0:T(8,128)(2,1)}, u32[]{:S(2)}, u32[]{:S(2)}) %all-to-all-start.1) | async-done | bytes 2097184 | tf_op jit(solution)/shard_map/all_to_all | solution.py:356
  71.3 9.4 %all-to-all-start.2 = ((bf16[32,2,64,256]{3,2,1,0:T(8,128)(2,1)}), bf16[32,2,64,256]{3,2,1,0:T(8,128)(2,1)}, u32[]{:S(2)}, u32[]{:S(2)}) async-start(bf16[32,2,64,256]{3,2,1,0:T(8,128)(2,1)} %broadcast_in_dim.123), calls=%async_computation.2 | async-start | bytes 4194304 | tf_op jit(solution)/shard_map/all_to_all | solution.py:359
  88.9 18.6 %all-to-all-done.2 = bf16[32,2,64,256]{3,2,1,0:T(8,128)(2,1)} async-done(((bf16[32,2,64,256]{3,2,1,0:T(8,128)(2,1)}), bf16[32,2,64,256]{3,2,1,0:T(8,128)(2,1)}, u32[]{:S(2)}, u32[]{:S(2)}) %all-to-all-start.2) | async-done | bytes 2097184 | tf_op jit(solution)/shard_map/all_to_all | solution.py:359
  107.5 10.0 %all-gather.2.cloned.1.call-done = bf16[32,384,128]{2,1,0:T(8,128)(2,1)} async-done(((bf16[4,384,128]{2,1,0:T(8,128)(2,1)}), bf16[32,384,128]{2,1,0:T(8,128)(2,1)}) %all-gather.2.cloned.1.call-update) | async-done | bytes 3145744 | tf_op jit(solution)/shard_map/all_gather | solution.py:375
  117.5 44.6 %shard_map.139 = bf16[8,192,64]{2,1,0:T(8,128)(2,1)} custom-call(s32[8]{0:T(128)} %get-tuple-element.27.steps_ref, s32[512]{0:T(512)} %mul.189.sources_ref, s32[64]{0:T(128)} %mul.192.bases_ref, s32[16]{0:T(128)} %reshape.413.limits_ref, bf16[8,192,64]{2,1,0:T(8,128)(2,1)} %bitcast.83, s32[8,192,1]{2,1,0:T(8,128)} %copy.69.low_ref, ...), custom_call_target="tpu_custom_call" | custom-call | flops 2415919104 | bytes 12582912 | tf_op jit(solution)/shard_map/pallas_call | solution.py:304
  162.1 1.9 copy.70
  164.0 8.3 %all-to-all-start.3 = ((bf16[16,96,64]{1,2,0:T(8,128)(2,1)}), bf16[16,96,64]{1,2,0:T(8,128)(2,1)S(1)}, u32[]{:S(2)}, u32[]{:S(2)}) async-start(bf16[16,96,64]{1,2,0:T(8,128)(2,1)} %copy.70), calls=%async_computation.3 | async-start | bytes 524288 | tf_op jit(solution)/shard_map/all_to_all | solution.py:410
  172.3 1.7 copy.73
  174.0 1.7 fusion.11
  177.9 2.3 fusion.96
  181.7 3.6 %all-to-all-start.4 = ((bf16[4,96,256]{2,1,0:T(8,128)(2,1)}), bf16[4,96,256]{2,1,0:T(8,128)(2,1)S(1)}, u32[]{:S(2)}, u32[]{:S(2)}) async-start(bf16[4,96,256]{2,1,0:T(8,128)(2,1)} %bitcast.72), calls=%async_computation.4 | async-start | bytes 393216 | tf_op jit(solution)/shard_map/all_to_all | solution.py:442
  186.1 3.7 %all-to-all-done.4 = bf16[4,96,256]{2,1,0:T(8,128)(2,1)S(1)} async-done(((bf16[4,96,256]{2,1,0:T(8,128)(2,1)}), bf16[4,96,256]{2,1,0:T(8,128)(2,1)S(1)}, u32[]{:S(2)}, u32[]{:S(2)}) %all-to-all-start.4) | async-done | bytes 196640 | tf_op jit(solution)/shard_map/all_to_all | solution.py:442
  189.8 5.5 %all-to-all-start.6 = ((bf16[4,384,128]{2,1,0:T(8,128)(2,1)}), bf16[4,384,128]{2,1,0:T(8,128)(2,1)S(1)}, u32[]{:S(2)}, u32[]{:S(2)}) async-start(bf16[4,384,128]{2,1,0:T(8,128)(2,1)} %pad_maximum_fusion), calls=%async_computation.6 | async-start | bytes 786432 | tf_op jit(solution)/shard_map/all_to_all | solution.py:435
  195.2 11.5 %shard_map.140 = bf16[2,192,256]{2,1,0:T(8,128)(2,1)} custom-call(s32[2]{0:T(128)} %and_select_fusion.2.steps_ref, s32[24]{0:T(128)} %reshape.412.sources_ref, s32[12]{0:T(128)} %min.32.bases_ref, bf16[2,192,256]{2,1,0:T(8,128)(2,1)} %bitcast.85, s32[2,192,1]{2,1,0:T(8,128)} %reshape.431.low_ref, s32[2,192,1]{2,1,0:T(8,128)} %sub.88.high_ref, ...), custom_call_target="tpu_custom_call" | custom-call | flops 3623878656 | bytes 4718592 | tf_op jit(solution)/shard_map/pallas_call | solution.py:191
  206.7 4.5 %all-to-all-start.5 = ((bf16[4,96,256]{2,1,0:T(8,128)(2,1)}), bf16[4,96,256]{2,1,0:T(8,128)(2,1)S(1)}, u32[]{:S(2)}, u32[]{:S(2)}) async-start(bf16[4,96,256]{2,1,0:T(8,128)(2,1)} %bitcast.86), calls=%async_computation.5 | async-start | bytes 393216 | tf_op jit(solution)/shard_map/all_to_all | solution.py:477
  212.4 3.3 %all-to-all-done.5 = bf16[4,96,256]{2,1,0:T(8,128)(2,1)S(1)} async-done(((bf16[4,96,256]{2,1,0:T(8,128)(2,1)}), bf16[4,96,256]{2,1,0:T(8,128)(2,1)S(1)}, u32[]{:S(2)}, u32[]{:S(2)}) %all-to-all-start.5) | async-done | bytes 196640 | tf_op jit(solution)/shard_map/all_to_all | solution.py:477
  216.5 10.0 %fusion.98 = (f32[96]{0:T(128)S(1)}, f32[96,1024]{1,0:T(8,128)S(1)}) fusion(f32[96]{0:T(128)S(1)} %add_rsqrt_fusion.1, f32[96,1024]{1,0:T(8,128)S(1)} %get-tuple-element.55, f32[96]{0:T(128)S(1)} %broadcast_multiply_fusion.3, bf16[4096,1024]{1,0:T(8,128)(2,1)} %param.22, bf16[1024,4096]{1,0:T(8,128)(2,1)} %param.21), kind=kOutput, calls=%fused_computation.184 | convolution fusion | flops 1636859776 | bytes 17564800 | tf_op jit(solution)/shard_map/dot_general | solution.py:487
  227.6 8.7 %all_gather.11 = bf16[384,1024]{1,0:T(8,128)(2,1)S(1)} all-gather(bf16[96,1024]{1,0:T(8,128)(2,1)S(1)} %get-tuple-element.25), channel_id=1, replica_groups=mesh['zy'=8,'x'=4,'head'=4] {'head'}, dimensions={0}, use_global_device_ids=true | all-gather | bytes 983040 | tf_op jit(solution)/shard_map/all_gather | solution.py:489
  236.3 1.8 convolution_bitcast_fusion
  (97 shorter events, 23.6 us)
Async XLA Ops:
  7.2 208.5 %copy-start = (bf16[1024,1024]{1,0:T(8,128)(2,1)S(1)}, bf16[1024,1024]{1,0:T(8,128)(2,1)}, u32[]{:S(2)}) copy-start(bf16[1024,1024]{1,0:T(8,128)(2,1)} %param.20) | copy-start | bytes 6291460
  7.2 110.3 %all-gather.2.cloned.1.call-start = ((), (), s32[]{:S(2)}) async-start(), calls=%async_computation.7 | async-start | bytes 3538944 | tf_op jit(solution)/shard_map/all_gather | solution.py:375
  34.4 6.0 %copy-start.5 = (s32[64]{0:T(128)S(1)}, s32[64]{0:T(128)}, u32[]{:S(2)}) copy-start(s32[64]{0:T(128)} %param.13) | copy-start | bytes 772
  34.5 12.2 %copy-start.6 = (s32[9]{0:T(128)S(1)}, s32[9]{0:T(128)}, u32[]{:S(2)}) copy-start(s32[9]{0:T(128)} %param.14) | copy-start | bytes 112
  34.5 12.5 %copy-start.7 = (s32[9]{0:T(128)S(1)}, s32[9]{0:T(128)}, u32[]{:S(2)}) copy-start(s32[9]{0:T(128)} %param.15) | copy-start | bytes 112
  34.5 35.2 %copy-start.4 = (bf16[2,64,256]{2,1,0:T(8,128)(2,1)S(1)}, bf16[2,64,256]{2,1,0:T(8,128)(2,1)}, u32[]{:S(2)}) copy-start(bf16[2,64,256]{2,1,0:T(8,128)(2,1)} %param.18) | copy-start | bytes 196612
  34.5 35.1 %all-to-all-start.1 = ((bf16[4,256,1024]{2,1,0:T(8,128)(2,1)}), bf16[4,256,1024]{2,1,0:T(8,128)(2,1)}, u32[]{:S(2)}, u32[]{:S(2)}) async-start(bf16[4,256,1024]{2,1,0:T(8,128)(2,1)} %broadcast_in_dim.122), calls=%async_computation.1 | async-start | bytes 4194304 | tf_op jit(solution)/shard_map/all_to_all | solution.py:356
  71.3 36.2 %all-to-all-start.2 = ((bf16[32,2,64,256]{3,2,1,0:T(8,128)(2,1)}), bf16[32,2,64,256]{3,2,1,0:T(8,128)(2,1)}, u32[]{:S(2)}, u32[]{:S(2)}) async-start(bf16[32,2,64,256]{3,2,1,0:T(8,128)(2,1)} %broadcast_in_dim.123), calls=%async_computation.2 | async-start | bytes 4194304 | tf_op jit(solution)/shard_map/all_to_all | solution.py:359
  164.0 13.9 %all-to-all-start.3 = ((bf16[16,96,64]{1,2,0:T(8,128)(2,1)}), bf16[16,96,64]{1,2,0:T(8,128)(2,1)S(1)}, u32[]{:S(2)}, u32[]{:S(2)}) async-start(bf16[16,96,64]{1,2,0:T(8,128)(2,1)} %copy.70), calls=%async_computation.3 | async-start | bytes 524288 | tf_op jit(solution)/shard_map/all_to_all | solution.py:410
  175.7 2.2 copy-start.2
  177.9 2.6 %copy-start.1 = (bf16[1024,1024]{1,0:T(8,128)(2,1)S(1)}, bf16[1024,1024]{1,0:T(8,128)(2,1)}, u32[]{:S(2)}) copy-start(bf16[1024,1024]{1,0:T(8,128)(2,1)} %param.19) | copy-start | bytes 6291460
  181.7 8.1 %all-to-all-start.4 = ((bf16[4,96,256]{2,1,0:T(8,128)(2,1)}), bf16[4,96,256]{2,1,0:T(8,128)(2,1)S(1)}, u32[]{:S(2)}, u32[]{:S(2)}) async-start(bf16[4,96,256]{2,1,0:T(8,128)(2,1)} %bitcast.72), calls=%async_computation.4 | async-start | bytes 393216 | tf_op jit(solution)/shard_map/all_to_all | solution.py:442
  189.8 5.5 %copy-start.3 = (bf16[4,96,256]{2,1,0:T(8,128)(2,1)}, bf16[4,96,256]{2,1,0:T(8,128)(2,1)S(1)}, u32[]{:S(2)}) copy-start(bf16[4,96,256]{2,1,0:T(8,128)(2,1)S(1)} %all-to-all-done.4) | copy-start | bytes 589828
  189.8 17.0 %all-to-all-start.6 = ((bf16[4,384,128]{2,1,0:T(8,128)(2,1)}), bf16[4,384,128]{2,1,0:T(8,128)(2,1)S(1)}, u32[]{:S(2)}, u32[]{:S(2)}) async-start(bf16[4,384,128]{2,1,0:T(8,128)(2,1)} %pad_maximum_fusion), calls=%async_computation.6 | async-start | bytes 786432 | tf_op jit(solution)/shard_map/all_to_all | solution.py:435
  206.7 9.0 %all-to-all-start.5 = ((bf16[4,96,256]{2,1,0:T(8,128)(2,1)}), bf16[4,96,256]{2,1,0:T(8,128)(2,1)S(1)}, u32[]{:S(2)}, u32[]{:S(2)}) async-start(bf16[4,96,256]{2,1,0:T(8,128)(2,1)} %bitcast.86), calls=%async_computation.5 | async-start | bytes 393216 | tf_op jit(solution)/shard_map/all_to_all | solution.py:477
  226.5 9.8 %copy-start.8 = (bf16[3,1024,256]{2,1,0:T(8,128)(2,1)S(1)}, bf16[3,1024,256]{2,1,0:T(8,128)(2,1)}, u32[]{:S(2)}) copy-start(bf16[3,1024,256]{2,1,0:T(8,128)(2,1)} %param.23) | copy-start | bytes 4718596
Sparse Core Ops, SparseCore 0:
  31.9 85.5 all-gather.1

commit v10 on v8

--- a/solution.py
+++ b/solution.py
@@ -371,8 +371,7 @@
     mine = lax.all_to_all(per_head, "x", 0, 0, tiled=True)
     packed = lax.all_gather(mine[:, :, head_width:], "zy", axis=0, tiled=True)
     packed = packed.reshape(cycle_size * block_rows, 2 * head_width)
-    full_out, packed, late_kv = lax.optimization_barrier((full_out, packed, enc_kv))
-    encoder = lax.all_gather(late_kv, ("zy", "x"), axis=1, tiled=True)
+    full_out, packed = lax.optimization_barrier((full_out, packed))
     ends = jnp.cumsum(request_lengths).astype(jnp.int32)
     starts = ends - request_lengths
     halves_here = 2 * ring_size
@@ -402,6 +401,13 @@
         self_max,
         pieces,
     )
+    single_out, late_kv = lax.optimization_barrier((single_out, enc_kv))
+    enc_all = lax.all_to_all(
+        jnp.broadcast_to(late_kv[None], (cycle_size,) + enc_kv.shape), ("zy", "x"), 0, 0, tiled=True
+    )
+    encoder = enc_all.transpose(1, 0, 2, 3).reshape(
+        2, cycle_size * enc_kv.shape[1], enc_kv.shape[2]
+    )
     owners = lax.all_to_all(
         single_out.reshape(ring_size * group_size, rows_here, head_width),
         ("x", "head"),

time: 236 us -> 258 us (1.093)
  starting transfers between devices: 24.4 us -> 46.9 us
  waiting for transfers between devices: 66.2 us -> 73.6 us
  Pallas kernels: 41.6 us -> 35.1 us
    all_to_all x0 -> x1, waiting for transfers between devices: none -> 22.2 us  [on_device(): lax.all_to_all(jnp.broadcast_to(late_kv[None], (cycle_size,) + enc_kv.sha...]
    all_to_all x0 -> x1, starting transfers between devices: none -> 21.6 us  [on_device(): lax.all_to_all(jnp.broadcast_to(late_kv[None], (cycle_size,) + enc_kv.sha...]
    all_gather x1 -> x0, waiting for transfers between devices: 9.88 us -> none  [on_device(): encoder = lax.all_gather(late_kv, ('zy', 'x'), axis=1, tiled=True)]
    pallas_call x1, Pallas kernels: 33.4 us -> 23.6 us  [single(): pl.pallas_call(kernel, out_shape=jax.ShapeDtypeStruct(queries.shape, jnp....]
    all_to_all x1, waiting for transfers between devices: 18.7 us -> 12.5 us  [on_device(): lax.all_to_all(jnp.broadcast_to(w_out[None], (group_size,) + w_out.shape)...]
    pallas_call x1, Pallas kernels: 8.18 us -> 11.5 us  [flash(): pl.pallas_call(kernel, out_shape=jax.ShapeDtypeStruct(queries.shape, jnp....]
  transfers between devices with their start and end apart: 7 -> 7, of which waited for: 5 -> 6; matrix products, arithmetic and copies ran while one was open for 12% -> 10% of each run, Pallas kernels for 18% -> 4%
where the time goes in v10:
time: 258 us; the launch traced here: 255 us
  waiting for transfers between devices  73.6 us (29%)
  starting transfers between devices  46.9 us (18%)
  Pallas kernels  35.1 us (14%)
  blocking collectives  32.8 us (13%)
  local copies, waits for them, and re-layouts  21.6 us (8%)
  between operations  19.5 us (8%)
  matrix products  17.6 us (7%)
  other arithmetic  7.82 us (3%)
    all_gather x1, waiting for transfers between devices, on_device(): packed = lax.all_gather(mine[:, :, head_width:], 'zy', axis=0, tiled=True)  28.8 us
    pallas_call x1, Pallas kernels, single(): pl.pallas_call(kernel, out_shape=jax.ShapeDtypeStruct(queries.shape, jnp....  23.6 us
    all_to_all x1, waiting for transfers between devices, on_device(): lax.all_to_all(jnp.broadcast_to(late_kv[None], (cycle_size,) + enc_kv.sha...  22.2 us
    all_to_all x1, starting transfers between devices, on_device(): lax.all_to_all(jnp.broadcast_to(late_kv[None], (cycle_size,) + enc_kv.sha...  21.6 us
    all_to_all x1, blocking collectives, on_device(): mine = lax.all_to_all(per_head, 'x', 0, 0, tiled=True)  13.4 us
    all_to_all x1, waiting for transfers between devices, on_device(): lax.all_to_all(jnp.broadcast_to(w_out[None], (group_size,) + w_out.shape)...  12.5 us
    pallas_call x1, Pallas kernels, flash(): pl.pallas_call(kernel, out_shape=jax.ShapeDtypeStruct(queries.shape, jnp....  11.5 us
    all_gather x1, blocking collectives, on_device(): gathered = lax.all_gather(tokens, 'head', axis=0, tiled=True)  10.7 us
  transfers between devices with their start and end apart: 7, of which 6 were waited for; matrix products, arithmetic and copies ran while one was open for 10% of the time, Pallas kernels for 4%

profile of v10, /device:TPU:1, one launch (start us, length us, event | category | flops | bytes accessed | tf_op | source)
XLA Modules:
  0.0 254.9 jit_solution(12828505035688380692)
XLA Ops:
  7.2 10.7 %all_gather.9 = bf16[384,1024]{1,0:T(8,128)(2,1)S(1)} all-gather(bf16[96,1024]{1,0:T(8,128)(2,1)} %param.12), channel_id=1, replica_groups=mesh['zy'=8,'x'=4,'head'=4] {'head'}, dimensions={0}, use_global_device_ids=true | all-gather | bytes 983040 | tf_op jit(solution)/shard_map/all_gather | solution.py:359
  17.9 2.4 convolution_convert_fusion
  20.4 13.4 %all_to_all.35 = bf16[4,384,192]{1,2,0:T(8,128)(2,1)S(1)} all-to-all(bf16[4,384,192]{1,2,0:T(8,128)(2,1)S(1)} %bitcast.74), channel_id=1, replica_groups=mesh['zy'=8,'x'=4,'head'=4] {'x'}, dimensions={0} | all-to-all | bytes 1179648 | tf_op jit(solution)/shard_map/all_to_all | solution.py:371
  34.8 2.7 %broadcast_in_dim.122 = bf16[4,256,1024]{2,1,0:T(8,128)(2,1)} broadcast(bf16[256,1024]{1,0:T(8,128)(2,1)} %param.17), dimensions={1,2} | broadcast | bytes 2621440 | tf_op jit(solution)/shard_map/broadcast_in_dim | solution.py:357
  37.5 6.1 %all-to-all-start.1 = ((bf16[4,256,1024]{2,1,0:T(8,128)(2,1)}), bf16[4,256,1024]{2,1,0:T(8,128)(2,1)}, u32[]{:S(2)}, u32[]{:S(2)}) async-start(bf16[4,256,1024]{2,1,0:T(8,128)(2,1)} %broadcast_in_dim.122), calls=%async_computation.1 | async-start | bytes 4194304 | tf_op jit(solution)/shard_map/all_to_all | solution.py:356
  60.2 12.5 %all-to-all-done.1 = bf16[4,256,1024]{2,1,0:T(8,128)(2,1)} async-done(((bf16[4,256,1024]{2,1,0:T(8,128)(2,1)}), bf16[4,256,1024]{2,1,0:T(8,128)(2,1)}, u32[]{:S(2)}, u32[]{:S(2)}) %all-to-all-start.1) | async-done | bytes 2097184 | tf_op jit(solution)/shard_map/all_to_all | solution.py:356
  72.7 28.8 %all-gather.2.cloned.1.call-done = bf16[32,384,128]{2,1,0:T(8,128)(2,1)} async-done(((bf16[4,384,128]{2,1,0:T(8,128)(2,1)}), bf16[32,384,128]{2,1,0:T(8,128)(2,1)}) %all-gather.2.cloned.1.call-update) | async-done | bytes 3145744 | tf_op jit(solution)/shard_map/all_gather | solution.py:372
  101.5 23.6 %shard_map.139 = bf16[8,192,64]{2,1,0:T(8,128)(2,1)} custom-call(s32[8]{0:T(128)} %get-tuple-element.29.steps_ref, s32[512]{0:T(512)} %mul.189.sources_ref, s32[64]{0:T(128)} %mul.192.bases_ref, s32[16]{0:T(128)} %reshape.413.limits_ref, bf16[8,192,64]{2,1,0:T(8,128)(2,1)} %bitcast.83, s32[8,192,1]{2,1,0:T(8,128)} %copy.69.low_ref, ...), custom_call_target="tpu_custom_call" | custom-call | flops 2415919104 | bytes 12582912 | tf_op jit(solution)/shard_map/pallas_call | solution.py:304
  125.1 1.9 copy.70
  127.0 5.4 %all-to-all-start.2 = ((bf16[16,96,64]{1,2,0:T(8,128)(2,1)}), bf16[16,96,64]{1,2,0:T(8,128)(2,1)S(1)}, u32[]{:S(2)}, u32[]{:S(2)}) async-start(bf16[16,96,64]{1,2,0:T(8,128)(2,1)} %copy.70), calls=%async_computation.2 | async-start | bytes 524288 | tf_op jit(solution)/shard_map/all_to_all | solution.py:411
  134.1 5.8 %all-to-all-done.2 = bf16[16,96,64]{1,2,0:T(8,128)(2,1)S(1)} async-done(((bf16[16,96,64]{1,2,0:T(8,128)(2,1)}), bf16[16,96,64]{1,2,0:T(8,128)(2,1)S(1)}, u32[]{:S(2)}, u32[]{:S(2)}) %all-to-all-start.2) | async-done | bytes 196640 | tf_op jit(solution)/shard_map/all_to_all | solution.py:411
  139.9 1.6 broadcast_in_dim.123
  141.5 21.6 %all-to-all-start.4 = ((bf16[32,2,64,256]{3,2,1,0:T(8,128)(2,1)}), bf16[32,2,64,256]{3,2,1,0:T(8,128)(2,1)}, u32[]{:S(2)}, u32[]{:S(2)}) async-start(bf16[32,2,64,256]{3,2,1,0:T(8,128)(2,1)} %broadcast_in_dim.123), calls=%async_computation.4 | async-start | bytes 4194304 | tf_op jit(solution)/shard_map/all_to_all | solution.py:405
  165.6 2.3 fusion.96
  169.4 22.2 %all-to-all-done.4 = bf16[32,2,64,256]{3,2,1,0:T(8,128)(2,1)} async-done(((bf16[32,2,64,256]{3,2,1,0:T(8,128)(2,1)}), bf16[32,2,64,256]{3,2,1,0:T(8,128)(2,1)}, u32[]{:S(2)}, u32[]{:S(2)}) %all-to-all-start.4) | async-done | bytes 2097184 | tf_op jit(solution)/shard_map/all_to_all | solution.py:405
  191.6 5.1 %all-to-all-start.3 = ((bf16[4,96,256]{2,1,0:T(8,128)(2,1)}), bf16[4,96,256]{2,1,0:T(8,128)(2,1)S(1)}, u32[]{:S(2)}, u32[]{:S(2)}) async-start(bf16[4,96,256]{2,1,0:T(8,128)(2,1)} %bitcast.72), calls=%async_computation.3 | async-start | bytes 393216 | tf_op jit(solution)/shard_map/all_to_all | solution.py:443
  196.7 1.7 copy.73
  201.2 4.0 %all-to-all-start.6 = ((bf16[4,384,128]{2,1,0:T(8,128)(2,1)}), bf16[4,384,128]{2,1,0:T(8,128)(2,1)S(1)}, u32[]{:S(2)}, u32[]{:S(2)}) async-start(bf16[4,384,128]{2,1,0:T(8,128)(2,1)} %pad_maximum_fusion), calls=%async_computation.6 | async-start | bytes 786432 | tf_op jit(solution)/shard_map/all_to_all | solution.py:436
  205.2 11.5 %shard_map.140 = bf16[2,192,256]{2,1,0:T(8,128)(2,1)} custom-call(s32[2]{0:T(128)} %and_select_fusion.2.steps_ref, s32[24]{0:T(128)} %reshape.412.sources_ref, s32[12]{0:T(128)} %min.32.bases_ref, bf16[2,192,256]{2,1,0:T(8,128)(2,1)} %bitcast.85, s32[2,192,1]{2,1,0:T(8,128)} %reshape.431.low_ref, s32[2,192,1]{2,1,0:T(8,128)} %sub.88.high_ref, ...), custom_call_target="tpu_custom_call" | custom-call | flops 3623878656 | bytes 4718592 | tf_op jit(solution)/shard_map/pallas_call | solution.py:191
  216.7 4.5 %all-to-all-start.5 = ((bf16[4,96,256]{2,1,0:T(8,128)(2,1)}), bf16[4,96,256]{2,1,0:T(8,128)(2,1)S(1)}, u32[]{:S(2)}, u32[]{:S(2)}) async-start(bf16[4,96,256]{2,1,0:T(8,128)(2,1)} %bitcast.86), calls=%async_computation.5 | async-start | bytes 393216 | tf_op jit(solution)/shard_map/all_to_all | solution.py:478
  222.4 3.3 %all-to-all-done.5 = bf16[4,96,256]{2,1,0:T(8,128)(2,1)S(1)} async-done(((bf16[4,96,256]{2,1,0:T(8,128)(2,1)}), bf16[4,96,256]{2,1,0:T(8,128)(2,1)S(1)}, u32[]{:S(2)}, u32[]{:S(2)}) %all-to-all-start.5) | async-done | bytes 196640 | tf_op jit(solution)/shard_map/all_to_all | solution.py:478
  226.5 10.0 %fusion.98 = (f32[96]{0:T(128)S(1)}, f32[96,1024]{1,0:T(8,128)S(1)}) fusion(f32[96]{0:T(128)S(1)} %add_rsqrt_fusion.1, f32[96,1024]{1,0:T(8,128)S(1)} %get-tuple-element.57, f32[96]{0:T(128)S(1)} %broadcast_multiply_fusion.3, bf16[4096,1024]{1,0:T(8,128)(2,1)} %param.22, bf16[1024,4096]{1,0:T(8,128)(2,1)} %param.21), kind=kOutput, calls=%fused_computation.184 | convolution fusion | flops 1636859776 | bytes 17564800 | tf_op jit(solution)/shard_map/dot_general | solution.py:488
  237.6 8.7 %all_gather.11 = bf16[384,1024]{1,0:T(8,128)(2,1)S(1)} all-gather(bf16[96,1024]{1,0:T(8,128)(2,1)S(1)} %get-tuple-element.27), channel_id=1, replica_groups=mesh['zy'=8,'x'=4,'head'=4] {'head'}, dimensions={0}, use_global_device_ids=true | all-gather | bytes 983040 | tf_op jit(solution)/shard_map/all_gather | solution.py:490
  246.3 1.8 convolution_bitcast_fusion
  (97 shorter events, 23.8 us)
Async XLA Ops:
  7.2 218.5 %copy-start = (bf16[1024,1024]{1,0:T(8,128)(2,1)S(1)}, bf16[1024,1024]{1,0:T(8,128)(2,1)}, u32[]{:S(2)}) copy-start(bf16[1024,1024]{1,0:T(8,128)(2,1)} %param.20) | copy-start | bytes 6291460
  7.2 94.3 %all-gather.2.cloned.1.call-start = ((), (), s32[]{:S(2)}) async-start(), calls=%async_computation.7 | async-start | bytes 3538944 | tf_op jit(solution)/shard_map/all_gather | solution.py:372
  37.5 6.1 %copy-start.5 = (s32[64]{0:T(128)S(1)}, s32[64]{0:T(128)}, u32[]{:S(2)}) copy-start(s32[64]{0:T(128)} %param.13) | copy-start | bytes 772
  37.5 12.3 %copy-start.6 = (s32[9]{0:T(128)S(1)}, s32[9]{0:T(128)}, u32[]{:S(2)}) copy-start(s32[9]{0:T(128)} %param.14) | copy-start | bytes 112
  37.5 12.6 %copy-start.7 = (s32[9]{0:T(128)S(1)}, s32[9]{0:T(128)}, u32[]{:S(2)}) copy-start(s32[9]{0:T(128)} %param.15) | copy-start | bytes 112
  37.5 35.3 %all-to-all-start.1 = ((bf16[4,256,1024]{2,1,0:T(8,128)(2,1)}), bf16[4,256,1024]{2,1,0:T(8,128)(2,1)}, u32[]{:S(2)}, u32[]{:S(2)}) async-start(bf16[4,256,1024]{2,1,0:T(8,128)(2,1)} %broadcast_in_dim.122), calls=%async_computation.1 | async-start | bytes 4194304 | tf_op jit(solution)/shard_map/all_to_all | solution.py:356
  101.5 38.3 %copy-start.4 = (bf16[2,64,256]{2,1,0:T(8,128)(2,1)S(1)}, bf16[2,64,256]{2,1,0:T(8,128)(2,1)}, u32[]{:S(2)}) copy-start(bf16[2,64,256]{2,1,0:T(8,128)(2,1)} %param.18) | copy-start | bytes 196612
  127.0 12.8 %all-to-all-start.2 = ((bf16[16,96,64]{1,2,0:T(8,128)(2,1)}), bf16[16,96,64]{1,2,0:T(8,128)(2,1)S(1)}, u32[]{:S(2)}, u32[]{:S(2)}) async-start(bf16[16,96,64]{1,2,0:T(8,128)(2,1)} %copy.70), calls=%async_computation.2 | async-start | bytes 524288 | tf_op jit(solution)/shard_map/all_to_all | solution.py:411
  141.5 50.1 %all-to-all-start.4 = ((bf16[32,2,64,256]{3,2,1,0:T(8,128)(2,1)}), bf16[32,2,64,256]{3,2,1,0:T(8,128)(2,1)}, u32[]{:S(2)}, u32[]{:S(2)}) async-start(bf16[32,2,64,256]{3,2,1,0:T(8,128)(2,1)} %broadcast_in_dim.123), calls=%async_computation.4 | async-start | bytes 4194304 | tf_op jit(solution)/shard_map/all_to_all | solution.py:405
  163.1 2.5 copy-start.2
  165.6 2.6 %copy-start.1 = (bf16[1024,1024]{1,0:T(8,128)(2,1)S(1)}, bf16[1024,1024]{1,0:T(8,128)(2,1)}, u32[]{:S(2)}) copy-start(bf16[1024,1024]{1,0:T(8,128)(2,1)} %param.19) | copy-start | bytes 6291460
  191.6 9.6 %all-to-all-start.3 = ((bf16[4,96,256]{2,1,0:T(8,128)(2,1)}), bf16[4,96,256]{2,1,0:T(8,128)(2,1)S(1)}, u32[]{:S(2)}, u32[]{:S(2)}) async-start(bf16[4,96,256]{2,1,0:T(8,128)(2,1)} %bitcast.72), calls=%async_computation.3 | async-start | bytes 393216 | tf_op jit(solution)/shard_map/all_to_all | solution.py:443
  201.2 4.0 %copy-start.3 = (bf16[4,96,256]{2,1,0:T(8,128)(2,1)}, bf16[4,96,256]{2,1,0:T(8,128)(2,1)S(1)}, u32[]{:S(2)}) copy-start(bf16[4,96,256]{2,1,0:T(8,128)(2,1)S(1)} %all-to-all-done.3) | copy-start | bytes 589828
  201.2 15.5 %all-to-all-start.6 = ((bf16[4,384,128]{2,1,0:T(8,128)(2,1)}), bf16[4,384,128]{2,1,0:T(8,128)(2,1)S(1)}, u32[]{:S(2)}, u32[]{:S(2)}) async-start(bf16[4,384,128]{2,1,0:T(8,128)(2,1)} %pad_maximum_fusion), calls=%async_computation.6 | async-start | bytes 786432 | tf_op jit(solution)/shard_map/all_to_all | solution.py:436
  216.7 9.0 %all-to-all-start.5 = ((bf16[4,96,256]{2,1,0:T(8,128)(2,1)}), bf16[4,96,256]{2,1,0:T(8,128)(2,1)S(1)}, u32[]{:S(2)}, u32[]{:S(2)}) async-start(bf16[4,96,256]{2,1,0:T(8,128)(2,1)} %bitcast.86), calls=%async_computation.5 | async-start | bytes 393216 | tf_op jit(solution)/shard_map/all_to_all | solution.py:478
  236.5 9.8 %copy-start.8 = (bf16[3,1024,256]{2,1,0:T(8,128)(2,1)S(1)}, bf16[3,1024,256]{2,1,0:T(8,128)(2,1)}, u32[]{:S(2)}) copy-start(bf16[3,1024,256]{2,1,0:T(8,128)(2,1)} %param.23) | copy-start | bytes 4718596
Sparse Core Ops, SparseCore 0:
  34.9 66.5 all-gather.1

commit v11 on v8

--- a/solution.py
+++ b/solution.py
@@ -368,7 +368,14 @@
     holders = jnp.sum(jnp.where(block_order[:, None] == slots[None, :], slots[:, None], 0), axis=0)
     per_head = projected.reshape(3, block_rows, group_heads, head_width).transpose(2, 1, 0, 3)
     per_head = per_head.reshape(group_heads, block_rows, 3 * head_width)
-    mine = lax.all_to_all(per_head, "x", 0, 0, tiled=True)
+    lanes = 256
+    mine = lax.all_to_all(
+        per_head.reshape(group_heads, block_rows * 3 * head_width // lanes, lanes),
+        "x",
+        0,
+        0,
+        tiled=True,
+    ).reshape(group_heads, block_rows, 3 * head_width)
     packed = lax.all_gather(mine[:, :, head_width:], "zy", axis=0, tiled=True)
     packed = packed.reshape(cycle_size * block_rows, 2 * head_width)
     full_out, packed, late_kv = lax.optimization_barrier((full_out, packed, enc_kv))

time: 236 us -> 242 us (1.025)
  local copies, waits for them, and re-layouts: 21.5 us -> 25.5 us
  waiting for transfers between devices: 66.2 us -> 69.7 us
    all_gather x1, waiting for transfers between devices: 9.88 us -> 13.4 us  [on_device(): encoder = lax.all_gather(late_kv, ('zy', 'x'), axis=1, tiled=True)]
    pallas_call x1, Pallas kernels: 8.18 us -> 11.5 us  [flash(): pl.pallas_call(kernel, out_shape=jax.ShapeDtypeStruct(queries.shape, jnp....]
    another operation x0 -> x1, local copies, waits for them, and re-layouts: none -> 2.96 us  [on_device(): per_head.reshape(group_heads, block_rows * 3 * head_width // lanes, lanes)]
where the time goes in v11:
time: 242 us; the launch traced here: 239 us
  waiting for transfers between devices  69.7 us (29%)
  Pallas kernels  42.7 us (18%)
  blocking collectives  32.8 us (14%)
  local copies, waits for them, and re-layouts  25.5 us (11%)
  starting transfers between devices  23.7 us (10%)
  between operations  19.4 us (8%)
  matrix products  17.6 us (7%)
  other arithmetic  7.84 us (3%)
    pallas_call x1, Pallas kernels, single(): pl.pallas_call(kernel, out_shape=jax.ShapeDtypeStruct(queries.shape, jnp....  31.2 us
    all_gather x1, waiting for transfers between devices, on_device(): packed = lax.all_gather(mine[:, :, head_width:], 'zy', axis=0, tiled=True)  28.8 us
    all_to_all x1, waiting for transfers between devices, on_device(): lax.all_to_all(jnp.broadcast_to(w_out[None], (group_size,) + w_out.shape)...  18.7 us
    all_gather x1, waiting for transfers between devices, on_device(): encoder = lax.all_gather(late_kv, ('zy', 'x'), axis=1, tiled=True)  13.4 us
    all_to_all x1, blocking collectives, on_device(): lax.all_to_all(per_head.reshape(group_heads, block_rows * 3 * head_width...  13.4 us
    pallas_call x1, Pallas kernels, flash(): pl.pallas_call(kernel, out_shape=jax.ShapeDtypeStruct(queries.shape, jnp....  11.5 us
    all_gather x1, blocking collectives, on_device(): gathered = lax.all_gather(tokens, 'head', axis=0, tiled=True)  10.7 us
    dot_general x1, matrix products, on_device(): jnp.dot(inner, w_down, preferred_element_type=jnp.float32) + second  10 us
  transfers between devices with their start and end apart: 7, of which 5 were waited for; matrix products, arithmetic and copies ran while one was open for 12% of the time, Pallas kernels for 18%

profile of v11, /device:TPU:1, one launch (start us, length us, event | category | flops | bytes accessed | tf_op | source)
XLA Modules:
  0.0 239.2 jit_solution(13084432682422352857)
XLA Ops:
  7.2 10.7 %all_gather.12 = bf16[384,1024]{1,0:T(8,128)(2,1)S(1)} all-gather(bf16[96,1024]{1,0:T(8,128)(2,1)} %param.12), channel_id=1, replica_groups=mesh['zy'=8,'x'=4,'head'=4] {'head'}, dimensions={0}, use_global_device_ids=true | all-gather | bytes 983040 | tf_op jit(solution)/shard_map/all_gather | solution.py:359
  17.9 2.4 %convolution_convert_fusion = bf16[3,256,384]{2,1,0:T(8,128)(2,1)S(1)} fusion(bf16[3,1024,256]{2,1,0:T(8,128)(2,1)} %param.16, bf16[384,1024]{1,0:T(8,128)(2,1)S(1)} %all_gather.12), kind=kOutput, calls=%fused_computation.22 | convolution fusion | flops 604274688 | bytes 2949120 | tf_op jit(solution)/shard_map/td,cde->cte/dot_general | solution.py:360
  20.4 2.2 copy.58
  22.6 3.0 %reshape_reshape.9 = bf16[4,288,256]{2,1,0:T(8,128)(2,1)S(1)} reshape(bf16[4,384,3,64]{3,2,1,0:T(4,128)(2,1)} %bitcast.69) | data formatting | bytes 1179648 | tf_op jit(solution)/shard_map/reshape;reshape | solution.py:373
  25.6 13.4 %all_to_all.30 = bf16[4,288,256]{2,1,0:T(8,128)(2,1)S(1)} all-to-all(bf16[4,288,256]{2,1,0:T(8,128)(2,1)S(1)} %reshape_reshape.9), channel_id=1, replica_groups=mesh['zy'=8,'x'=4,'head'=4] {'x'}, dimensions={0} | all-to-all | bytes 1179648 | tf_op jit(solution)/shard_map/all_to_all | solution.py:372
  40.5 2.7 %broadcast_in_dim.116 = bf16[4,256,1024]{2,1,0:T(8,128)(2,1)} broadcast(bf16[256,1024]{1,0:T(8,128)(2,1)} %param.17), dimensions={1,2} | broadcast | bytes 2621440 | tf_op jit(solution)/shard_map/broadcast_in_dim | solution.py:357
  43.2 6.1 %all-to-all-start.1 = ((bf16[4,256,1024]{2,1,0:T(8,128)(2,1)}), bf16[4,256,1024]{2,1,0:T(8,128)(2,1)}, u32[]{:S(2)}, u32[]{:S(2)}) async-start(bf16[4,256,1024]{2,1,0:T(8,128)(2,1)} %broadcast_in_dim.116), calls=%async_computation.1 | async-start | bytes 4194304 | tf_op jit(solution)/shard_map/all_to_all | solution.py:356
  59.8 18.7 %all-to-all-done.1 = bf16[4,256,1024]{2,1,0:T(8,128)(2,1)} async-done(((bf16[4,256,1024]{2,1,0:T(8,128)(2,1)}), bf16[4,256,1024]{2,1,0:T(8,128)(2,1)}, u32[]{:S(2)}, u32[]{:S(2)}) %all-to-all-start.1) | async-done | bytes 2097184 | tf_op jit(solution)/shard_map/all_to_all | solution.py:356
  78.5 28.8 %all-gather.3.cloned.1.call-done = bf16[32,384,128]{2,1,0:T(8,128)(2,1)} async-done(((bf16[4,384,128]{2,1,0:T(8,128)(2,1)}), bf16[32,384,128]{2,1,0:T(8,128)(2,1)}) %all-gather.3.cloned.1.call-update) | async-done | bytes 3145744 | tf_op jit(solution)/shard_map/all_gather | solution.py:379
  115.6 31.2 %shard_map.139 = bf16[8,192,64]{2,1,0:T(8,128)(2,1)} custom-call(s32[8]{0:T(128)} %get-tuple-element.27.steps_ref, s32[512]{0:T(512)} %mul.189.sources_ref, s32[64]{0:T(128)} %mul.192.bases_ref, s32[16]{0:T(128)} %reshape.409.limits_ref, bf16[8,192,64]{2,1,0:T(8,128)(2,1)} %bitcast.78, s32[8,192,1]{2,1,0:T(8,128)} %copy.59.low_ref, ...), custom_call_target="tpu_custom_call" | custom-call | flops 2415919104 | bytes 12582912 | tf_op jit(solution)/shard_map/pallas_call | solution.py:304
  146.8 1.9 copy.60
  148.6 5.4 %all-to-all-start.2 = ((bf16[16,96,64]{1,2,0:T(8,128)(2,1)}), bf16[16,96,64]{1,2,0:T(8,128)(2,1)S(1)}, u32[]{:S(2)}, u32[]{:S(2)}) async-start(bf16[16,96,64]{1,2,0:T(8,128)(2,1)} %copy.60), calls=%async_computation.2 | async-start | bytes 524288 | tf_op jit(solution)/shard_map/all_to_all | solution.py:412
  156.0 5.5 %all-to-all-done.2 = bf16[16,96,64]{1,2,0:T(8,128)(2,1)S(1)} async-done(((bf16[16,96,64]{1,2,0:T(8,128)(2,1)}), bf16[16,96,64]{1,2,0:T(8,128)(2,1)S(1)}, u32[]{:S(2)}, u32[]{:S(2)}) %all-to-all-start.2) | async-done | bytes 196640 | tf_op jit(solution)/shard_map/all_to_all | solution.py:412
  161.5 2.3 fusion.96
  165.3 3.7 %all-to-all-start.3 = ((bf16[4,96,256]{2,1,0:T(8,128)(2,1)}), bf16[4,96,256]{2,1,0:T(8,128)(2,1)S(1)}, u32[]{:S(2)}, u32[]{:S(2)}) async-start(bf16[4,96,256]{2,1,0:T(8,128)(2,1)} %bitcast.68), calls=%async_computation.3 | async-start | bytes 393216 | tf_op jit(solution)/shard_map/all_to_all | solution.py:444
  169.0 13.4 %all-gather.5.cloned.1.call-done = bf16[2,2048,256]{2,1,0:T(8,128)(2,1)} async-done(((bf16[2,64,256]{2,1,0:T(8,128)(2,1)}), bf16[2,2048,256]{2,1,0:T(8,128)(2,1)}) %all-gather.5.cloned.1.call-update) | async-done | bytes 2097168 | tf_op jit(solution)/shard_map/all_gather | solution.py:382
  182.4 3.2 %fusion.11 = (bf16[2496,256]{1,0:T(8,128)(2,1)}, bf16[2496,256]{1,0:T(8,128)(2,1)}) fusion(bf16[2,2048,256]{2,1,0:T(8,128)(2,1)} %all-gather.5.cloned.1.call-done), kind=kLoop, calls=%fused_computation.24 | loop fusion | bytes 4653056 | tf_op jit(solution)/shard_map/squeeze | solution.py:472
  185.6 3.5 %all-to-all-start.5 = ((bf16[4,384,128]{2,1,0:T(8,128)(2,1)}), bf16[4,384,128]{2,1,0:T(8,128)(2,1)S(1)}, u32[]{:S(2)}, u32[]{:S(2)}) async-start(bf16[4,384,128]{2,1,0:T(8,128)(2,1)} %pad_maximum_fusion), calls=%async_computation.5 | async-start | bytes 786432 | tf_op jit(solution)/shard_map/all_to_all | solution.py:437
  189.1 11.5 %shard_map.140 = bf16[2,192,256]{2,1,0:T(8,128)(2,1)} custom-call(s32[2]{0:T(128)} %and_select_fusion.2.steps_ref, s32[24]{0:T(128)} %reshape.408.sources_ref, s32[12]{0:T(128)} %min.32.bases_ref, bf16[2,192,256]{2,1,0:T(8,128)(2,1)} %bitcast.80, s32[2,192,1]{2,1,0:T(8,128)} %reshape.426.low_ref, s32[2,192,1]{2,1,0:T(8,128)} %sub.88.high_ref, ...), custom_call_target="tpu_custom_call" | custom-call | flops 3623878656 | bytes 4718592 | tf_op jit(solution)/shard_map/pallas_call | solution.py:191
  200.6 4.9 %all-to-all-start.4 = ((bf16[4,96,256]{2,1,0:T(8,128)(2,1)}), bf16[4,96,256]{2,1,0:T(8,128)(2,1)S(1)}, u32[]{:S(2)}, u32[]{:S(2)}) async-start(bf16[4,96,256]{2,1,0:T(8,128)(2,1)} %bitcast.81), calls=%async_computation.4 | async-start | bytes 393216 | tf_op jit(solution)/shard_map/all_to_all | solution.py:479
  206.7 3.3 %all-to-all-done.4 = bf16[4,96,256]{2,1,0:T(8,128)(2,1)S(1)} async-done(((bf16[4,96,256]{2,1,0:T(8,128)(2,1)}), bf16[4,96,256]{2,1,0:T(8,128)(2,1)S(1)}, u32[]{:S(2)}, u32[]{:S(2)}) %all-to-all-start.4) | async-done | bytes 196640 | tf_op jit(solution)/shard_map/all_to_all | solution.py:479
  210.7 10.0 %fusion.98 = (f32[96]{0:T(128)S(1)}, f32[96,1024]{1,0:T(8,128)S(1)}) fusion(f32[96]{0:T(128)S(1)} %add_rsqrt_fusion.1, f32[96,1024]{1,0:T(8,128)S(1)} %get-tuple-element.55, f32[96]{0:T(128)S(1)} %broadcast_multiply_fusion.3, bf16[4096,1024]{1,0:T(8,128)(2,1)} %param.22, bf16[1024,4096]{1,0:T(8,128)(2,1)} %param.21), kind=kOutput, calls=%fused_computation.184 | convolution fusion | flops 1636859776 | bytes 17564800 | tf_op jit(solution)/shard_map/dot_general | solution.py:489
  221.9 8.7 %all_gather.15 = bf16[384,1024]{1,0:T(8,128)(2,1)S(1)} all-gather(bf16[96,1024]{1,0:T(8,128)(2,1)S(1)} %get-tuple-element.25), channel_id=1, replica_groups=mesh['zy'=8,'x'=4,'head'=4] {'head'}, dimensions={0}, use_global_device_ids=true | all-gather | bytes 983040 | tf_op jit(solution)/shard_map/all_gather | solution.py:491
  230.6 1.8 convolution_bitcast_fusion
  (94 shorter events, 21.6 us)
Async XLA Ops:
  7.2 202.8 %copy-start = (bf16[1024,1024]{1,0:T(8,128)(2,1)S(1)}, bf16[1024,1024]{1,0:T(8,128)(2,1)}, u32[]{:S(2)}) copy-start(bf16[1024,1024]{1,0:T(8,128)(2,1)} %param.20) | copy-start | bytes 6291460
  7.2 100.1 %all-gather.3.cloned.1.call-start = ((), (), s32[]{:S(2)}) async-start(), calls=%async_computation.6 | async-start | bytes 3538944 | tf_op jit(solution)/shard_map/all_gather | solution.py:379
  43.2 6.1 %copy-start.4 = (s32[64]{0:T(128)S(1)}, s32[64]{0:T(128)}, u32[]{:S(2)}) copy-start(s32[64]{0:T(128)} %param.13) | copy-start | bytes 772
  43.2 12.2 %copy-start.5 = (s32[9]{0:T(128)S(1)}, s32[9]{0:T(128)}, u32[]{:S(2)}) copy-start(s32[9]{0:T(128)} %param.14) | copy-start | bytes 112
  43.2 12.5 %copy-start.6 = (s32[9]{0:T(128)S(1)}, s32[9]{0:T(128)}, u32[]{:S(2)}) copy-start(s32[9]{0:T(128)} %param.15) | copy-start | bytes 112
  43.2 35.3 %all-to-all-start.1 = ((bf16[4,256,1024]{2,1,0:T(8,128)(2,1)}), bf16[4,256,1024]{2,1,0:T(8,128)(2,1)}, u32[]{:S(2)}, u32[]{:S(2)}) async-start(bf16[4,256,1024]{2,1,0:T(8,128)(2,1)} %broadcast_in_dim.116), calls=%async_computation.1 | async-start | bytes 4194304 | tf_op jit(solution)/shard_map/all_to_all | solution.py:356
  49.3 133.1 %all-gather.5.cloned.1.call-start = ((), (), s32[]{:S(2)}) async-start(), calls=%async_computation.7 | async-start | bytes 2162688 | tf_op jit(solution)/shard_map/all_gather | solution.py:382
  148.6 12.8 %all-to-all-start.2 = ((bf16[16,96,64]{1,2,0:T(8,128)(2,1)}), bf16[16,96,64]{1,2,0:T(8,128)(2,1)S(1)}, u32[]{:S(2)}, u32[]{:S(2)}) async-start(bf16[16,96,64]{1,2,0:T(8,128)(2,1)} %copy.60), calls=%async_computation.2 | async-start | bytes 524288 | tf_op jit(solution)/shard_map/all_to_all | solution.py:412
  154.1 7.4 %copy-start.2 = (bf16[96,1024]{1,0:T(8,128)(2,1)S(1)}, bf16[96,1024]{1,0:T(8,128)(2,1)}, u32[]{:S(2)}) copy-start(bf16[96,1024]{1,0:T(8,128)(2,1)} %param.12) | copy-start | bytes 589828
  161.5 2.6 %copy-start.1 = (bf16[1024,1024]{1,0:T(8,128)(2,1)S(1)}, bf16[1024,1024]{1,0:T(8,128)(2,1)}, u32[]{:S(2)}) copy-start(bf16[1024,1024]{1,0:T(8,128)(2,1)} %param.19) | copy-start | bytes 6291460
  165.3 20.3 %all-to-all-start.3 = ((bf16[4,96,256]{2,1,0:T(8,128)(2,1)}), bf16[4,96,256]{2,1,0:T(8,128)(2,1)S(1)}, u32[]{:S(2)}, u32[]{:S(2)}) async-start(bf16[4,96,256]{2,1,0:T(8,128)(2,1)} %bitcast.68), calls=%async_computation.3 | async-start | bytes 393216 | tf_op jit(solution)/shard_map/all_to_all | solution.py:444
  185.6 3.5 %copy-start.3 = (bf16[4,96,256]{2,1,0:T(8,128)(2,1)}, bf16[4,96,256]{2,1,0:T(8,128)(2,1)S(1)}, u32[]{:S(2)}) copy-start(bf16[4,96,256]{2,1,0:T(8,128)(2,1)S(1)} %all-to-all-done.3) | copy-start | bytes 589828
  185.6 15.0 %all-to-all-start.5 = ((bf16[4,384,128]{2,1,0:T(8,128)(2,1)}), bf16[4,384,128]{2,1,0:T(8,128)(2,1)S(1)}, u32[]{:S(2)}, u32[]{:S(2)}) async-start(bf16[4,384,128]{2,1,0:T(8,128)(2,1)} %pad_maximum_fusion), calls=%async_computation.5 | async-start | bytes 786432 | tf_op jit(solution)/shard_map/all_to_all | solution.py:437
  200.6 9.4 %all-to-all-start.4 = ((bf16[4,96,256]{2,1,0:T(8,128)(2,1)}), bf16[4,96,256]{2,1,0:T(8,128)(2,1)S(1)}, u32[]{:S(2)}, u32[]{:S(2)}) async-start(bf16[4,96,256]{2,1,0:T(8,128)(2,1)} %bitcast.81), calls=%async_computation.4 | async-start | bytes 393216 | tf_op jit(solution)/shard_map/all_to_all | solution.py:479
  220.8 9.8 %copy-start.7 = (bf16[3,1024,256]{2,1,0:T(8,128)(2,1)S(1)}, bf16[3,1024,256]{2,1,0:T(8,128)(2,1)}, u32[]{:S(2)}) copy-start(bf16[3,1024,256]{2,1,0:T(8,128)(2,1)} %param.23) | copy-start | bytes 4718596
Sparse Core Ops, SparseCore 0:
  40.7 66.5 all-gather.2
  110.3 72.1 all-gather.4

commit v12 on v8

--- a/solution.py
+++ b/solution.py
@@ -379,7 +379,7 @@
     first_half = lax.axis_index("zy") * halves_here
     pair = lax.dynamic_slice_in_dim(block_order, first_half, halves_here, 0)
     low_block = prefix_below(pair * halfway, ends, request_lengths) // halfway
-    pieces = 8
+    pieces = 16
     self_steps = (pair - low_block) // pieces + 1
     self_max = (2 * cycle_size + pieces - 1) // pieces
     firsts = low_block[:, None] + pieces * jnp.arange(self_max, dtype=jnp.int32)[None, :]

time: 236 us -> 233 us (0.987)
  waiting for transfers between devices: 66.2 us -> 63.7 us
    all_gather x1, waiting for transfers between devices: 9.88 us -> 6.87 us  [on_device(): encoder = lax.all_gather(late_kv, ('zy', 'x'), axis=1, tiled=True)]
  transfers between devices with their start and end apart: 7 -> 7, of which waited for: 5 -> 5; matrix products, arithmetic and copies ran while one was open for 12% -> 12% of each run, Pallas kernels for 18% -> 19%
where the time goes in v12:
time: 233 us; the launch traced here: 230 us
  waiting for transfers between devices  63.7 us (27%)
  Pallas kernels  42.8 us (18%)
  blocking collectives  32.8 us (14%)
  starting transfers between devices  24.5 us (11%)
  local copies, waits for them, and re-layouts  21.5 us (9%)
  between operations  19.4 us (8%)
  matrix products  17.6 us (8%)
  other arithmetic  7.34 us (3%)
    pallas_call x1, Pallas kernels, single(): pl.pallas_call(kernel, out_shape=jax.ShapeDtypeStruct(queries.shape, jnp....  34.6 us
    all_gather x1, waiting for transfers between devices, on_device(): packed = lax.all_gather(mine[:, :, head_width:], 'zy', axis=0, tiled=True)  28.8 us
    all_to_all x1, waiting for transfers between devices, on_device(): lax.all_to_all(jnp.broadcast_to(w_out[None], (group_size,) + w_out.shape)...  18.7 us
    all_to_all x1, blocking collectives, on_device(): mine = lax.all_to_all(per_head, 'x', 0, 0, tiled=True)  13.4 us
    all_gather x1, blocking collectives, on_device(): gathered = lax.all_gather(tokens, 'head', axis=0, tiled=True)  10.7 us
    dot_general x1, matrix products, on_device(): jnp.dot(inner, w_down, preferred_element_type=jnp.float32) + second  10 us
    all_gather x1, blocking collectives, on_device(): block_output = lax.all_gather(output_b, 'head', axis=0, tiled=True)  8.7 us
    pallas_call x1, Pallas kernels, flash(): pl.pallas_call(kernel, out_shape=jax.ShapeDtypeStruct(queries.shape, jnp....  8.19 us
  transfers between devices with their start and end apart: 7, of which 5 were waited for; matrix products, arithmetic and copies ran while one was open for 12% of the time, Pallas kernels for 19%

profile of v12, /device:TPU:1, one launch (start us, length us, event | category | flops | bytes accessed | tf_op | source)
XLA Modules:
  0.0 229.8 jit_solution(8919684824927606321)
XLA Ops:
  7.2 10.7 %all_gather.12 = bf16[384,1024]{1,0:T(8,128)(2,1)S(1)} all-gather(bf16[96,1024]{1,0:T(8,128)(2,1)} %param.12), channel_id=1, replica_groups=mesh['zy'=8,'x'=4,'head'=4] {'head'}, dimensions={0}, use_global_device_ids=true | all-gather | bytes 983040 | tf_op jit(solution)/shard_map/all_gather | solution.py:359
  17.9 2.4 %convolution_convert_fusion = bf16[3,256,384]{2,1,0:T(8,128)(2,1)S(1)} fusion(bf16[3,1024,256]{2,1,0:T(8,128)(2,1)} %param.16, bf16[384,1024]{1,0:T(8,128)(2,1)S(1)} %all_gather.12), kind=kOutput, calls=%fused_computation.22 | convolution fusion | flops 604274688 | bytes 2949120 | tf_op jit(solution)/shard_map/td,cde->cte/dot_general | solution.py:360
  20.4 13.4 %all_to_all.30 = bf16[4,384,192]{1,2,0:T(8,128)(2,1)S(1)} all-to-all(bf16[4,384,192]{1,2,0:T(8,128)(2,1)S(1)} %bitcast.71), channel_id=1, replica_groups=mesh['zy'=8,'x'=4,'head'=4] {'x'}, dimensions={0} | all-to-all | bytes 1179648 | tf_op jit(solution)/shard_map/all_to_all | solution.py:371
  34.8 2.7 %broadcast_in_dim.116 = bf16[4,256,1024]{2,1,0:T(8,128)(2,1)} broadcast(bf16[256,1024]{1,0:T(8,128)(2,1)} %param.17), dimensions={1,2} | broadcast | bytes 2621440 | tf_op jit(solution)/shard_map/broadcast_in_dim | solution.py:357
  37.5 6.1 %all-to-all-start.1 = ((bf16[4,256,1024]{2,1,0:T(8,128)(2,1)}), bf16[4,256,1024]{2,1,0:T(8,128)(2,1)}, u32[]{:S(2)}, u32[]{:S(2)}) async-start(bf16[4,256,1024]{2,1,0:T(8,128)(2,1)} %broadcast_in_dim.116), calls=%async_computation.1 | async-start | bytes 4194304 | tf_op jit(solution)/shard_map/all_to_all | solution.py:356
  54.0 18.7 %all-to-all-done.1 = bf16[4,256,1024]{2,1,0:T(8,128)(2,1)} async-done(((bf16[4,256,1024]{2,1,0:T(8,128)(2,1)}), bf16[4,256,1024]{2,1,0:T(8,128)(2,1)}, u32[]{:S(2)}, u32[]{:S(2)}) %all-to-all-start.1) | async-done | bytes 2097184 | tf_op jit(solution)/shard_map/all_to_all | solution.py:356
  72.7 28.8 %all-gather.3.cloned.1.call-done = bf16[32,384,128]{2,1,0:T(8,128)(2,1)} async-done(((bf16[4,384,128]{2,1,0:T(8,128)(2,1)}), bf16[32,384,128]{2,1,0:T(8,128)(2,1)}) %all-gather.3.cloned.1.call-update) | async-done | bytes 3145744 | tf_op jit(solution)/shard_map/all_gather | solution.py:372
  103.7 1.2 copy.68.low_ref
  109.5 34.6 %shard_map.139 = bf16[8,192,64]{2,1,0:T(8,128)(2,1)} custom-call(s32[8]{0:T(128)} %get-tuple-element.27.steps_ref, s32[512]{0:T(512)} %mul.189.sources_ref, s32[32]{0:T(128)} %mul.192.bases_ref, s32[16]{0:T(128)} %reshape.409.limits_ref, bf16[8,192,64]{2,1,0:T(8,128)(2,1)} %bitcast.80, s32[8,192,1]{2,1,0:T(8,128)} %copy.68.low_ref, ...), custom_call_target="tpu_custom_call" | custom-call | flops 2415919104 | bytes 12582912 | tf_op jit(solution)/shard_map/pallas_call | solution.py:304
  144.1 1.9 copy.69
  145.9 5.4 %all-to-all-start.2 = ((bf16[16,96,64]{1,2,0:T(8,128)(2,1)}), bf16[16,96,64]{1,2,0:T(8,128)(2,1)S(1)}, u32[]{:S(2)}, u32[]{:S(2)}) async-start(bf16[16,96,64]{1,2,0:T(8,128)(2,1)} %copy.69), calls=%async_computation.2 | async-start | bytes 524288 | tf_op jit(solution)/shard_map/all_to_all | solution.py:405
  151.4 1.1 constant_dynamic-slice_fusion.7
  153.3 6.1 %all-to-all-done.2 = bf16[16,96,64]{1,2,0:T(8,128)(2,1)S(1)} async-done(((bf16[16,96,64]{1,2,0:T(8,128)(2,1)}), bf16[16,96,64]{1,2,0:T(8,128)(2,1)S(1)}, u32[]{:S(2)}, u32[]{:S(2)}) %all-to-all-start.2) | async-done | bytes 196640 | tf_op jit(solution)/shard_map/all_to_all | solution.py:405
  159.4 2.3 %fusion.96 = (f32[96]{0:T(128)S(1)}, f32[96,1024]{1,0:T(8,128)S(1)}) fusion(bf16[96,1024]{1,0:T(8,128)(2,1)S(1)} %copy-done.3, bf16[96,1024]{0,1:T(8,128)(2,1)S(1)} %bitcast.74, bf16[1024,1024]{1,0:T(8,128)(2,1)} %bitcast.9), kind=kOutput, calls=%fused_computation.182 | convolution fusion | flops 201621408 | bytes 2883968 | tf_op jit(solution)/shard_map/dot_general | solution.py:433
  163.2 3.8 %all-to-all-start.3 = ((bf16[4,96,256]{2,1,0:T(8,128)(2,1)}), bf16[4,96,256]{2,1,0:T(8,128)(2,1)S(1)}, u32[]{:S(2)}, u32[]{:S(2)}) async-start(bf16[4,96,256]{2,1,0:T(8,128)(2,1)} %bitcast.70), calls=%async_computation.3 | async-start | bytes 393216 | tf_op jit(solution)/shard_map/all_to_all | solution.py:437
  167.0 6.9 %all-gather.5.cloned.1.call-done = bf16[2,2048,256]{2,1,0:T(8,128)(2,1)} async-done(((bf16[2,64,256]{2,1,0:T(8,128)(2,1)}), bf16[2,2048,256]{2,1,0:T(8,128)(2,1)}) %all-gather.5.cloned.1.call-update) | async-done | bytes 2097168 | tf_op jit(solution)/shard_map/all_gather | solution.py:375
  173.8 3.2 %fusion.11 = (bf16[2496,256]{1,0:T(8,128)(2,1)}, bf16[2496,256]{1,0:T(8,128)(2,1)}) fusion(bf16[2,2048,256]{2,1,0:T(8,128)(2,1)} %all-gather.5.cloned.1.call-done), kind=kLoop, calls=%fused_computation.24 | loop fusion | bytes 4653056 | tf_op jit(solution)/shard_map/squeeze | solution.py:465
  177.0 3.5 %all-to-all-start.5 = ((bf16[4,384,128]{2,1,0:T(8,128)(2,1)}), bf16[4,384,128]{2,1,0:T(8,128)(2,1)S(1)}, u32[]{:S(2)}, u32[]{:S(2)}) async-start(bf16[4,384,128]{2,1,0:T(8,128)(2,1)} %pad_maximum_fusion), calls=%async_computation.5 | async-start | bytes 786432 | tf_op jit(solution)/shard_map/all_to_all | solution.py:430
  180.5 8.2 %shard_map.140 = bf16[2,192,256]{2,1,0:T(8,128)(2,1)} custom-call(s32[2]{0:T(128)} %and_select_fusion.2.steps_ref, s32[24]{0:T(128)} %reshape.408.sources_ref, s32[12]{0:T(128)} %min.32.bases_ref, bf16[2,192,256]{2,1,0:T(8,128)(2,1)} %bitcast.82, s32[2,192,1]{2,1,0:T(8,128)} %reshape.426.low_ref, s32[2,192,1]{2,1,0:T(8,128)} %sub.88.high_ref, ...), custom_call_target="tpu_custom_call" | custom-call | flops 3623878656 | bytes 4718592 | tf_op jit(solution)/shard_map/pallas_call | solution.py:191
  188.7 5.7 %all-to-all-start.4 = ((bf16[4,96,256]{2,1,0:T(8,128)(2,1)}), bf16[4,96,256]{2,1,0:T(8,128)(2,1)S(1)}, u32[]{:S(2)}, u32[]{:S(2)}) async-start(bf16[4,96,256]{2,1,0:T(8,128)(2,1)} %bitcast.83), calls=%async_computation.4 | async-start | bytes 393216 | tf_op jit(solution)/shard_map/all_to_all | solution.py:472
  195.6 3.3 %all-to-all-done.4 = bf16[4,96,256]{2,1,0:T(8,128)(2,1)S(1)} async-done(((bf16[4,96,256]{2,1,0:T(8,128)(2,1)}), bf16[4,96,256]{2,1,0:T(8,128)(2,1)S(1)}, u32[]{:S(2)}, u32[]{:S(2)}) %all-to-all-start.4) | async-done | bytes 196640 | tf_op jit(solution)/shard_map/all_to_all | solution.py:472
  201.3 10.0 %fusion.98 = (f32[96]{0:T(128)S(1)}, f32[96,1024]{1,0:T(8,128)S(1)}) fusion(f32[96]{0:T(128)S(1)} %add_rsqrt_fusion.1, f32[96,1024]{1,0:T(8,128)S(1)} %get-tuple-element.55, f32[96]{0:T(128)S(1)} %broadcast_multiply_fusion.3, bf16[4096,1024]{1,0:T(8,128)(2,1)} %param.22, bf16[1024,4096]{1,0:T(8,128)(2,1)} %param.21), kind=kOutput, calls=%fused_computation.184 | convolution fusion | flops 1636859776 | bytes 17564800 | tf_op jit(solution)/shard_map/dot_general | solution.py:482
  212.4 8.7 %all_gather.15 = bf16[384,1024]{1,0:T(8,128)(2,1)S(1)} all-gather(bf16[96,1024]{1,0:T(8,128)(2,1)S(1)} %get-tuple-element.25), channel_id=1, replica_groups=mesh['zy'=8,'x'=4,'head'=4] {'head'}, dimensions={0}, use_global_device_ids=true | all-gather | bytes 983040 | tf_op jit(solution)/shard_map/all_gather | solution.py:484
  221.1 1.8 convolution_bitcast_fusion
  (96 shorter events, 20.1 us)
Async XLA Ops:
  7.2 193.4 %copy-start = (bf16[1024,1024]{1,0:T(8,128)(2,1)S(1)}, bf16[1024,1024]{1,0:T(8,128)(2,1)}, u32[]{:S(2)}) copy-start(bf16[1024,1024]{1,0:T(8,128)(2,1)} %param.20) | copy-start | bytes 6291460
  7.2 94.3 %all-gather.3.cloned.1.call-start = ((), (), s32[]{:S(2)}) async-start(), calls=%async_computation.6 | async-start | bytes 3538944 | tf_op jit(solution)/shard_map/all_gather | solution.py:372
  37.5 6.1 %copy-start.5 = (s32[64]{0:T(128)S(1)}, s32[64]{0:T(128)}, u32[]{:S(2)}) copy-start(s32[64]{0:T(128)} %param.13) | copy-start | bytes 772
  37.5 12.2 %copy-start.6 = (s32[9]{0:T(128)S(1)}, s32[9]{0:T(128)}, u32[]{:S(2)}) copy-start(s32[9]{0:T(128)} %param.14) | copy-start | bytes 112
  37.5 12.5 %copy-start.7 = (s32[9]{0:T(128)S(1)}, s32[9]{0:T(128)}, u32[]{:S(2)}) copy-start(s32[9]{0:T(128)} %param.15) | copy-start | bytes 112
  37.5 35.3 %all-to-all-start.1 = ((bf16[4,256,1024]{2,1,0:T(8,128)(2,1)}), bf16[4,256,1024]{2,1,0:T(8,128)(2,1)}, u32[]{:S(2)}, u32[]{:S(2)}) async-start(bf16[4,256,1024]{2,1,0:T(8,128)(2,1)} %broadcast_in_dim.116), calls=%async_computation.1 | async-start | bytes 4194304 | tf_op jit(solution)/shard_map/all_to_all | solution.py:356
  43.6 130.2 %all-gather.5.cloned.1.call-start = ((), (), s32[]{:S(2)}) async-start(), calls=%async_computation.7 | async-start | bytes 2162688 | tf_op jit(solution)/shard_map/all_gather | solution.py:375
  145.9 13.4 %all-to-all-start.2 = ((bf16[16,96,64]{1,2,0:T(8,128)(2,1)}), bf16[16,96,64]{1,2,0:T(8,128)(2,1)S(1)}, u32[]{:S(2)}, u32[]{:S(2)}) async-start(bf16[16,96,64]{1,2,0:T(8,128)(2,1)} %copy.69), calls=%async_computation.2 | async-start | bytes 524288 | tf_op jit(solution)/shard_map/all_to_all | solution.py:405
  151.4 8.0 %copy-start.3 = (bf16[96,1024]{1,0:T(8,128)(2,1)S(1)}, bf16[96,1024]{1,0:T(8,128)(2,1)}, u32[]{:S(2)}) copy-start(bf16[96,1024]{1,0:T(8,128)(2,1)} %param.12) | copy-start | bytes 589828
  159.4 2.6 %copy-start.1 = (bf16[1024,1024]{1,0:T(8,128)(2,1)S(1)}, bf16[1024,1024]{1,0:T(8,128)(2,1)}, u32[]{:S(2)}) copy-start(bf16[1024,1024]{1,0:T(8,128)(2,1)} %param.19) | copy-start | bytes 6291460
  163.2 13.8 %all-to-all-start.3 = ((bf16[4,96,256]{2,1,0:T(8,128)(2,1)}), bf16[4,96,256]{2,1,0:T(8,128)(2,1)S(1)}, u32[]{:S(2)}, u32[]{:S(2)}) async-start(bf16[4,96,256]{2,1,0:T(8,128)(2,1)} %bitcast.70), calls=%async_computation.3 | async-start | bytes 393216 | tf_op jit(solution)/shard_map/all_to_all | solution.py:437
  177.0 3.5 %copy-start.4 = (bf16[4,96,256]{2,1,0:T(8,128)(2,1)}, bf16[4,96,256]{2,1,0:T(8,128)(2,1)S(1)}, u32[]{:S(2)}) copy-start(bf16[4,96,256]{2,1,0:T(8,128)(2,1)S(1)} %all-to-all-done.3) | copy-start | bytes 589828
  177.0 11.7 %all-to-all-start.5 = ((bf16[4,384,128]{2,1,0:T(8,128)(2,1)}), bf16[4,384,128]{2,1,0:T(8,128)(2,1)S(1)}, u32[]{:S(2)}, u32[]{:S(2)}) async-start(bf16[4,384,128]{2,1,0:T(8,128)(2,1)} %pad_maximum_fusion), calls=%async_computation.5 | async-start | bytes 786432 | tf_op jit(solution)/shard_map/all_to_all | solution.py:430
  188.7 10.2 %all-to-all-start.4 = ((bf16[4,96,256]{2,1,0:T(8,128)(2,1)}), bf16[4,96,256]{2,1,0:T(8,128)(2,1)S(1)}, u32[]{:S(2)}, u32[]{:S(2)}) async-start(bf16[4,96,256]{2,1,0:T(8,128)(2,1)} %bitcast.83), calls=%async_computation.4 | async-start | bytes 393216 | tf_op jit(solution)/shard_map/all_to_all | solution.py:472
  198.9 0.7 copy-start.2
  211.3 9.8 %copy-start.8 = (bf16[3,1024,256]{2,1,0:T(8,128)(2,1)S(1)}, bf16[3,1024,256]{2,1,0:T(8,128)(2,1)}, u32[]{:S(2)}) copy-start(bf16[3,1024,256]{2,1,0:T(8,128)(2,1)} %param.23) | copy-start | bytes 4718596
Sparse Core Ops, SparseCore 0:
  34.9 66.5 all-gather.2
  104.5 69.2 all-gather.4

commit v13 on v8

--- a/solution.py
+++ b/solution.py
@@ -368,10 +368,14 @@
     holders = jnp.sum(jnp.where(block_order[:, None] == slots[None, :], slots[:, None], 0), axis=0)
     per_head = projected.reshape(3, block_rows, group_heads, head_width).transpose(2, 1, 0, 3)
     per_head = per_head.reshape(group_heads, block_rows, 3 * head_width)
-    mine = lax.all_to_all(per_head, "x", 0, 0, tiled=True)
-    packed = lax.all_gather(mine[:, :, head_width:], "zy", axis=0, tiled=True)
+    mine_kv = lax.all_to_all(per_head[:, :, head_width:], "x", 0, 0, tiled=True)
+    packed = lax.all_gather(mine_kv, "zy", axis=0, tiled=True)
+    own_queries, mine_kv = lax.optimization_barrier((per_head[:, :, :head_width], mine_kv))
+    mine_q = lax.all_to_all(own_queries, "x", 0, 0, tiled=True)
     packed = packed.reshape(cycle_size * block_rows, 2 * head_width)
-    full_out, packed, late_kv = lax.optimization_barrier((full_out, packed, enc_kv))
+    full_out, packed, late_kv, mine_q = lax.optimization_barrier(
+        (full_out, packed, enc_kv, mine_q)
+    )
     encoder = lax.all_gather(late_kv, ("zy", "x"), axis=1, tiled=True)
     ends = jnp.cumsum(request_lengths).astype(jnp.int32)
     starts = ends - request_lengths
@@ -391,7 +395,7 @@
     self_low = prefix_below(places_here, ends, request_lengths).reshape(halves_here, halfway)
     limits = jnp.stack([self_low[:, -1], places_here[:, 0]], axis=1).reshape(-1)
     single_out = single(
-        mine[:, :, :head_width].reshape(halves_here, halfway, head_width),
+        mine_q.reshape(halves_here, halfway, head_width),
         self_low.reshape(halves_here, halfway, 1),
         places_here.reshape(halves_here, halfway, 1),
         packed,

time: 236 us -> 239 us (1.013)
  waiting for transfers between devices: 66.2 us -> 70.7 us
  starting transfers between devices: 24.4 us -> 27 us
    all_to_all x1, waiting for transfers between devices: 18.7 us -> 33.5 us  [on_device(): lax.all_to_all(jnp.broadcast_to(w_out[None], (group_size,) + w_out.shape)...]
    all_gather x1, waiting for transfers between devices: 28.8 us -> 16.3 us  [on_device(): packed = lax.all_gather(mine_kv, 'zy', axis=0, tiled=True)]
    all_to_all x0 -> x1, waiting for transfers between devices: none -> 5.13 us  [on_device(): mine_q = lax.all_to_all(own_queries, 'x', 0, 0, tiled=True)]
    all_gather x1, waiting for transfers between devices: 9.88 us -> 5.38 us  [on_device(): encoder = lax.all_gather(late_kv, ('zy', 'x'), axis=1, tiled=True)]
    all_to_all x0 -> x1, starting transfers between devices: none -> 3.38 us  [on_device(): mine_q = lax.all_to_all(own_queries, 'x', 0, 0, tiled=True)]
  transfers between devices with their start and end apart: 7 -> 8, of which waited for: 5 -> 6; matrix products, arithmetic and copies ran while one was open for 12% -> 12% of each run, Pallas kernels for 18% -> 18%
where the time goes in v13:
time: 239 us; the launch traced here: 235 us
  waiting for transfers between devices  70.7 us (30%)
  Pallas kernels  42.3 us (18%)
  blocking collectives  31 us (13%)
  starting transfers between devices  27 us (11%)
  local copies, waits for them, and re-layouts  19.6 us (8%)
  between operations  19.3 us (8%)
  matrix products  17.6 us (7%)
  other arithmetic  7.82 us (3%)
    pallas_call x1, Pallas kernels, single(): pl.pallas_call(kernel, out_shape=jax.ShapeDtypeStruct(queries.shape, jnp....  34.1 us
    all_to_all x1, waiting for transfers between devices, on_device(): lax.all_to_all(jnp.broadcast_to(w_out[None], (group_size,) + w_out.shape)...  33.5 us
    all_gather x1, waiting for transfers between devices, on_device(): packed = lax.all_gather(mine_kv, 'zy', axis=0, tiled=True)  16.3 us
    all_to_all x1, blocking collectives, on_device(): mine_kv = lax.all_to_all(per_head[:, :, head_width:], 'x', 0, 0, tiled=True)  11.6 us
    all_gather x1, blocking collectives, on_device(): gathered = lax.all_gather(tokens, 'head', axis=0, tiled=True)  10.7 us
    dot_general x1, matrix products, on_device(): jnp.dot(inner, w_down, preferred_element_type=jnp.float32) + second  10 us
    all_gather x1, blocking collectives, on_device(): block_output = lax.all_gather(output_b, 'head', axis=0, tiled=True)  8.7 us
    pallas_call x1, Pallas kernels, flash(): pl.pallas_call(kernel, out_shape=jax.ShapeDtypeStruct(queries.shape, jnp....  8.18 us
  transfers between devices with their start and end apart: 8, of which 6 were waited for; matrix products, arithmetic and copies ran while one was open for 12% of the time, Pallas kernels for 18%

profile of v13, /device:TPU:1, one launch (start us, length us, event | category | flops | bytes accessed | tf_op | source)
XLA Modules:
  0.0 235.3 jit_solution(4042234324062550830)
XLA Ops:
  7.2 10.7 %all_gather.12 = bf16[384,1024]{1,0:T(8,128)(2,1)S(1)} all-gather(bf16[96,1024]{1,0:T(8,128)(2,1)} %param.12), channel_id=1, replica_groups=mesh['zy'=8,'x'=4,'head'=4] {'head'}, dimensions={0}, use_global_device_ids=true | all-gather | bytes 983040 | tf_op jit(solution)/shard_map/all_gather | solution.py:359
  17.9 2.4 %convolution_convert_fusion = bf16[3,256,384]{2,1,0:T(8,128)(2,1)S(1)} fusion(bf16[3,1024,256]{2,1,0:T(8,128)(2,1)} %param.16, bf16[384,1024]{1,0:T(8,128)(2,1)S(1)} %all_gather.12), kind=kOutput, calls=%fused_computation.22 | convolution fusion | flops 604274688 | bytes 2949120 | tf_op jit(solution)/shard_map/td,cde->cte/dot_general | solution.py:360
  20.5 11.6 %all_to_all.35 = bf16[4,384,128]{1,2,0:T(8,128)(2,1)S(1)} all-to-all(bf16[4,384,128]{1,2,0:T(8,128)(2,1)S(1)} %slice.68), channel_id=1, replica_groups=mesh['zy'=8,'x'=4,'head'=4] {'x'}, dimensions={0} | all-to-all | bytes 786432 | tf_op jit(solution)/shard_map/all_to_all | solution.py:371
  40.0 3.4 %all-to-all-start.2 = ((bf16[4,384,64]{1,2,0:T(8,128)(2,1)}), bf16[4,384,64]{1,2,0:T(8,128)(2,1)S(1)}, u32[]{:S(2)}, u32[]{:S(2)}) async-start(bf16[4,384,64]{1,2,0:T(8,128)(2,1)} %slice.69), calls=%async_computation.2 | async-start | bytes 393216 | tf_op jit(solution)/shard_map/all_to_all | solution.py:374
  43.4 5.1 %all-to-all-done.2 = bf16[4,384,64]{1,2,0:T(8,128)(2,1)S(1)} async-done(((bf16[4,384,64]{1,2,0:T(8,128)(2,1)}), bf16[4,384,64]{1,2,0:T(8,128)(2,1)S(1)}, u32[]{:S(2)}, u32[]{:S(2)}) %all-to-all-start.2) | async-done | bytes 196640 | tf_op jit(solution)/shard_map/all_to_all | solution.py:374
  48.6 1.6 broadcast_in_dim.116
  50.2 7.0 %all-to-all-start = ((bf16[4,256,1024]{2,1,0:T(8,128)(2,1)}), bf16[4,256,1024]{2,1,0:T(8,128)(2,1)}, u32[]{:S(2)}, u32[]{:S(2)}) async-start(bf16[4,256,1024]{2,1,0:T(8,128)(2,1)} %broadcast_in_dim.116), calls=%async_computation | async-start | bytes 4194304 | tf_op jit(solution)/shard_map/all_to_all | solution.py:356
  61.2 33.5 %all-to-all-done = bf16[4,256,1024]{2,1,0:T(8,128)(2,1)} async-done(((bf16[4,256,1024]{2,1,0:T(8,128)(2,1)}), bf16[4,256,1024]{2,1,0:T(8,128)(2,1)}, u32[]{:S(2)}, u32[]{:S(2)}) %all-to-all-start) | async-done | bytes 2097184 | tf_op jit(solution)/shard_map/all_to_all | solution.py:356
  94.7 16.3 %all-gather.3.cloned.1.call-done = bf16[32,384,128]{2,1,0:T(8,128)(2,1)} async-done(((bf16[4,384,128]{2,1,0:T(8,128)(2,1)}), bf16[32,384,128]{2,1,0:T(8,128)(2,1)}) %all-gather.3.cloned.1.call-update) | async-done | bytes 3145744 | tf_op jit(solution)/shard_map/all_gather | solution.py:372
  119.4 34.1 %shard_map.139 = bf16[8,192,64]{2,1,0:T(8,128)(2,1)} custom-call(s32[8]{0:T(128)} %get-tuple-element.31.steps_ref, s32[512]{0:T(512)} %mul.189.sources_ref, s32[64]{0:T(128)} %mul.192.bases_ref, s32[16]{0:T(128)} %reshape.409.limits_ref, bf16[8,192,64]{2,1,0:T(8,128)(2,1)} %bitcast.81, s32[8,192,1]{2,1,0:T(8,128)} %copy.68.low_ref, ...), custom_call_target="tpu_custom_call" | custom-call | flops 2415919104 | bytes 12582912 | tf_op jit(solution)/shard_map/pallas_call | solution.py:304
  153.5 1.9 copy.69
  155.3 4.1 %all-to-all-start.3 = ((bf16[16,96,64]{1,2,0:T(8,128)(2,1)}), bf16[16,96,64]{1,2,0:T(8,128)(2,1)S(1)}, u32[]{:S(2)}, u32[]{:S(2)}) async-start(bf16[16,96,64]{1,2,0:T(8,128)(2,1)} %copy.69), calls=%async_computation.3 | async-start | bytes 524288 | tf_op jit(solution)/shard_map/all_to_all | solution.py:409
  161.4 7.1 %all-to-all-done.3 = bf16[16,96,64]{1,2,0:T(8,128)(2,1)S(1)} async-done(((bf16[16,96,64]{1,2,0:T(8,128)(2,1)}), bf16[16,96,64]{1,2,0:T(8,128)(2,1)S(1)}, u32[]{:S(2)}, u32[]{:S(2)}) %all-to-all-start.3) | async-done | bytes 196640 | tf_op jit(solution)/shard_map/all_to_all | solution.py:409
  168.6 2.3 fusion.96
  172.4 3.4 %all-to-all-start.4 = ((bf16[4,96,256]{2,1,0:T(8,128)(2,1)}), bf16[4,96,256]{2,1,0:T(8,128)(2,1)S(1)}, u32[]{:S(2)}, u32[]{:S(2)}) async-start(bf16[4,96,256]{2,1,0:T(8,128)(2,1)} %bitcast.70), calls=%async_computation.4 | async-start | bytes 393216 | tf_op jit(solution)/shard_map/all_to_all | solution.py:441
  175.8 5.4 %all-gather.5.cloned.1.call-done = bf16[2,2048,256]{2,1,0:T(8,128)(2,1)} async-done(((bf16[2,64,256]{2,1,0:T(8,128)(2,1)}), bf16[2,2048,256]{2,1,0:T(8,128)(2,1)}) %all-gather.5.cloned.1.call-update) | async-done | bytes 2097168 | tf_op jit(solution)/shard_map/all_gather | solution.py:379
  181.2 3.2 %fusion.11 = (bf16[2496,256]{1,0:T(8,128)(2,1)}, bf16[2496,256]{1,0:T(8,128)(2,1)}) fusion(bf16[2,2048,256]{2,1,0:T(8,128)(2,1)} %all-gather.5.cloned.1.call-done), kind=kLoop, calls=%fused_computation.24 | loop fusion | bytes 4653056 | tf_op jit(solution)/shard_map/squeeze | solution.py:469
  184.4 3.5 %all-to-all-start.6 = ((bf16[4,384,128]{2,1,0:T(8,128)(2,1)}), bf16[4,384,128]{2,1,0:T(8,128)(2,1)S(1)}, u32[]{:S(2)}, u32[]{:S(2)}) async-start(bf16[4,384,128]{2,1,0:T(8,128)(2,1)} %pad_maximum_fusion), calls=%async_computation.6 | async-start | bytes 786432 | tf_op jit(solution)/shard_map/all_to_all | solution.py:434
  187.9 8.2 %shard_map.140 = bf16[2,192,256]{2,1,0:T(8,128)(2,1)} custom-call(s32[2]{0:T(128)} %and_select_fusion.2.steps_ref, s32[24]{0:T(128)} %reshape.408.sources_ref, s32[12]{0:T(128)} %min.32.bases_ref, bf16[2,192,256]{2,1,0:T(8,128)(2,1)} %bitcast.83, s32[2,192,1]{2,1,0:T(8,128)} %reshape.426.low_ref, s32[2,192,1]{2,1,0:T(8,128)} %sub.88.high_ref, ...), custom_call_target="tpu_custom_call" | custom-call | flops 3623878656 | bytes 4718592 | tf_op jit(solution)/shard_map/pallas_call | solution.py:191
  196.1 5.5 %all-to-all-start.5 = ((bf16[4,96,256]{2,1,0:T(8,128)(2,1)}), bf16[4,96,256]{2,1,0:T(8,128)(2,1)S(1)}, u32[]{:S(2)}, u32[]{:S(2)}) async-start(bf16[4,96,256]{2,1,0:T(8,128)(2,1)} %bitcast.84), calls=%async_computation.5 | async-start | bytes 393216 | tf_op jit(solution)/shard_map/all_to_all | solution.py:476
  202.8 3.3 %all-to-all-done.5 = bf16[4,96,256]{2,1,0:T(8,128)(2,1)S(1)} async-done(((bf16[4,96,256]{2,1,0:T(8,128)(2,1)}), bf16[4,96,256]{2,1,0:T(8,128)(2,1)S(1)}, u32[]{:S(2)}, u32[]{:S(2)}) %all-to-all-start.5) | async-done | bytes 196640 | tf_op jit(solution)/shard_map/all_to_all | solution.py:476
  206.9 10.0 %fusion.98 = (f32[96]{0:T(128)S(1)}, f32[96,1024]{1,0:T(8,128)S(1)}) fusion(f32[96]{0:T(128)S(1)} %add_rsqrt_fusion.1, f32[96,1024]{1,0:T(8,128)S(1)} %get-tuple-element.59, f32[96]{0:T(128)S(1)} %broadcast_multiply_fusion.3, bf16[4096,1024]{1,0:T(8,128)(2,1)} %param.22, bf16[1024,4096]{1,0:T(8,128)(2,1)} %param.21), kind=kOutput, calls=%fused_computation.184 | convolution fusion | flops 1636859776 | bytes 17564800 | tf_op jit(solution)/shard_map/dot_general | solution.py:486
  218.0 8.7 %all_gather.15 = bf16[384,1024]{1,0:T(8,128)(2,1)S(1)} all-gather(bf16[96,1024]{1,0:T(8,128)(2,1)S(1)} %get-tuple-element.29), channel_id=1, replica_groups=mesh['zy'=8,'x'=4,'head'=4] {'head'}, dimensions={0}, use_global_device_ids=true | all-gather | bytes 983040 | tf_op jit(solution)/shard_map/all_gather | solution.py:488
  226.7 1.8 convolution_bitcast_fusion
  (98 shorter events, 21.9 us)
Async XLA Ops:
  7.2 198.9 %copy-start = (bf16[1024,1024]{1,0:T(8,128)(2,1)S(1)}, bf16[1024,1024]{1,0:T(8,128)(2,1)}, u32[]{:S(2)}) copy-start(bf16[1024,1024]{1,0:T(8,128)(2,1)} %param.20) | copy-start | bytes 6291460
  7.2 103.8 %all-gather.3.cloned.1.call-start = ((), (), s32[]{:S(2)}) async-start(), calls=%async_computation.7 | async-start | bytes 3538944 | tf_op jit(solution)/shard_map/all_gather | solution.py:372
  20.4 12.6 %copy-start.5 = (s32[64]{0:T(128)S(1)}, s32[64]{0:T(128)}, u32[]{:S(2)}) copy-start(s32[64]{0:T(128)} %param.13) | copy-start | bytes 772
  20.5 19.3 %copy-start.6 = (s32[9]{0:T(128)S(1)}, s32[9]{0:T(128)}, u32[]{:S(2)}) copy-start(s32[9]{0:T(128)} %param.14) | copy-start | bytes 112
  33.0 15.6 %copy-start.3 = (bf16[256,1024]{1,0:T(8,128)(2,1)S(1)}, bf16[256,1024]{1,0:T(8,128)(2,1)}, u32[]{:S(2)}) copy-start(bf16[256,1024]{1,0:T(8,128)(2,1)} %param.17) | copy-start | bytes 1572868
  40.0 8.5 %all-to-all-start.2 = ((bf16[4,384,64]{1,2,0:T(8,128)(2,1)}), bf16[4,384,64]{1,2,0:T(8,128)(2,1)S(1)}, u32[]{:S(2)}, u32[]{:S(2)}) async-start(bf16[4,384,64]{1,2,0:T(8,128)(2,1)} %slice.69), calls=%async_computation.2 | async-start | bytes 393216 | tf_op jit(solution)/shard_map/all_to_all | solution.py:374
  50.2 7.0 %copy-start.7 = (s32[9]{0:T(128)S(1)}, s32[9]{0:T(128)}, u32[]{:S(2)}) copy-start(s32[9]{0:T(128)} %param.15) | copy-start | bytes 112
  50.2 44.5 %all-to-all-start = ((bf16[4,256,1024]{2,1,0:T(8,128)(2,1)}), bf16[4,256,1024]{2,1,0:T(8,128)(2,1)}, u32[]{:S(2)}, u32[]{:S(2)}) async-start(bf16[4,256,1024]{2,1,0:T(8,128)(2,1)} %broadcast_in_dim.116), calls=%async_computation | async-start | bytes 4194304 | tf_op jit(solution)/shard_map/all_to_all | solution.py:356
  57.2 124.0 %all-gather.5.cloned.1.call-start = ((), (), s32[]{:S(2)}) async-start(), calls=%async_computation.8 | async-start | bytes 2162688 | tf_op jit(solution)/shard_map/all_gather | solution.py:379
  155.3 13.2 %all-to-all-start.3 = ((bf16[16,96,64]{1,2,0:T(8,128)(2,1)}), bf16[16,96,64]{1,2,0:T(8,128)(2,1)S(1)}, u32[]{:S(2)}, u32[]{:S(2)}) async-start(bf16[16,96,64]{1,2,0:T(8,128)(2,1)} %copy.69), calls=%async_computation.3 | async-start | bytes 524288 | tf_op jit(solution)/shard_map/all_to_all | solution.py:409
  159.5 9.1 %copy-start.2 = (bf16[96,1024]{1,0:T(8,128)(2,1)S(1)}, bf16[96,1024]{1,0:T(8,128)(2,1)}, u32[]{:S(2)}) copy-start(bf16[96,1024]{1,0:T(8,128)(2,1)} %param.12) | copy-start | bytes 589828
  168.6 2.6 %copy-start.1 = (bf16[1024,1024]{1,0:T(8,128)(2,1)S(1)}, bf16[1024,1024]{1,0:T(8,128)(2,1)}, u32[]{:S(2)}) copy-start(bf16[1024,1024]{1,0:T(8,128)(2,1)} %param.19) | copy-start | bytes 6291460
  172.4 12.0 %all-to-all-start.4 = ((bf16[4,96,256]{2,1,0:T(8,128)(2,1)}), bf16[4,96,256]{2,1,0:T(8,128)(2,1)S(1)}, u32[]{:S(2)}, u32[]{:S(2)}) async-start(bf16[4,96,256]{2,1,0:T(8,128)(2,1)} %bitcast.70), calls=%async_computation.4 | async-start | bytes 393216 | tf_op jit(solution)/shard_map/all_to_all | solution.py:441
  184.4 3.5 %copy-start.4 = (bf16[4,96,256]{2,1,0:T(8,128)(2,1)}, bf16[4,96,256]{2,1,0:T(8,128)(2,1)S(1)}, u32[]{:S(2)}) copy-start(bf16[4,96,256]{2,1,0:T(8,128)(2,1)S(1)} %all-to-all-done.4) | copy-start | bytes 589828
  184.4 11.7 %all-to-all-start.6 = ((bf16[4,384,128]{2,1,0:T(8,128)(2,1)}), bf16[4,384,128]{2,1,0:T(8,128)(2,1)S(1)}, u32[]{:S(2)}, u32[]{:S(2)}) async-start(bf16[4,384,128]{2,1,0:T(8,128)(2,1)} %pad_maximum_fusion), calls=%async_computation.6 | async-start | bytes 786432 | tf_op jit(solution)/shard_map/all_to_all | solution.py:434
  196.1 10.0 %all-to-all-start.5 = ((bf16[4,96,256]{2,1,0:T(8,128)(2,1)}), bf16[4,96,256]{2,1,0:T(8,128)(2,1)S(1)}, u32[]{:S(2)}, u32[]{:S(2)}) async-start(bf16[4,96,256]{2,1,0:T(8,128)(2,1)} %bitcast.84), calls=%async_computation.5 | async-start | bytes 393216 | tf_op jit(solution)/shard_map/all_to_all | solution.py:476
  216.9 9.8 %copy-start.8 = (bf16[3,1024,256]{2,1,0:T(8,128)(2,1)S(1)}, bf16[3,1024,256]{2,1,0:T(8,128)(2,1)}, u32[]{:S(2)}) copy-start(bf16[3,1024,256]{2,1,0:T(8,128)(2,1)} %param.23) | copy-start | bytes 4718596
Sparse Core Ops, SparseCore 0:
  33.1 77.7 all-gather.2
  114.0 67.1 all-gather.4

commit v14 on v8

--- a/solution.py
+++ b/solution.py
@@ -371,8 +371,14 @@
     mine = lax.all_to_all(per_head, "x", 0, 0, tiled=True)
     packed = lax.all_gather(mine[:, :, head_width:], "zy", axis=0, tiled=True)
     packed = packed.reshape(cycle_size * block_rows, 2 * head_width)
-    full_out, packed, late_kv = lax.optimization_barrier((full_out, packed, enc_kv))
-    encoder = lax.all_gather(late_kv, ("zy", "x"), axis=1, tiled=True)
+    enc_ring = lax.all_to_all(
+        jnp.broadcast_to(enc_kv[None], (ring_size,) + enc_kv.shape), "x", 0, 0, tiled=True
+    )
+    enc_ring = enc_ring.transpose(1, 0, 2, 3).reshape(
+        2, ring_size * enc_kv.shape[1], enc_kv.shape[2]
+    )
+    full_out, packed, late_kv = lax.optimization_barrier((full_out, packed, enc_ring))
+    encoder = lax.all_gather(late_kv, "zy", axis=1, tiled=True)
     ends = jnp.cumsum(request_lengths).astype(jnp.int32)
     starts = ends - request_lengths
     halves_here = 2 * ring_size

time: 236 us -> 237 us (level)
  waiting for transfers between devices: 66.2 us -> 60.6 us
  Pallas kernels: 41.6 us -> 46.3 us
  starting transfers between devices: 24.4 us -> 26.8 us
    all_to_all x1, waiting for transfers between devices: 18.7 us -> 30.1 us  [on_device(): lax.all_to_all(jnp.broadcast_to(w_out[None], (group_size,) + w_out.shape)...]
    all_gather x1, waiting for transfers between devices: 9.88 us -> 0.01 us  [on_device(): encoder = lax.all_gather(late_kv, 'zy', axis=1, tiled=True)]
    all_gather x1, waiting for transfers between devices: 28.8 us -> 20.4 us  [on_device(): packed = lax.all_gather(mine[:, :, head_width:], 'zy', axis=0, tiled=True)]
    pallas_call x1, Pallas kernels: 33.4 us -> 38.1 us  [single(): pl.pallas_call(kernel, out_shape=jax.ShapeDtypeStruct(queries.shape, jnp....]
    all_to_all x0 -> x1, starting transfers between devices: none -> 3.41 us  [on_device(): lax.all_to_all(jnp.broadcast_to(enc_kv[None], (ring_size,) + enc_kv.shape...]
  transfers between devices with their start and end apart: 7 -> 8, of which waited for: 5 -> 5; matrix products, arithmetic and copies ran while one was open for 12% -> 12% of each run, Pallas kernels for 18% -> 20%
where the time goes in v14:
time: 237 us; the launch traced here: 233 us
  waiting for transfers between devices  60.6 us (26%)
  Pallas kernels  46.3 us (20%)
  blocking collectives  32.9 us (14%)
  starting transfers between devices  26.8 us (11%)
  local copies, waits for them, and re-layouts  22 us (9%)
  between operations  19.4 us (8%)
  matrix products  17.6 us (7%)
  other arithmetic  7.86 us (3%)
    pallas_call x1, Pallas kernels, single(): pl.pallas_call(kernel, out_shape=jax.ShapeDtypeStruct(queries.shape, jnp....  38.1 us
    all_to_all x1, waiting for transfers between devices, on_device(): lax.all_to_all(jnp.broadcast_to(w_out[None], (group_size,) + w_out.shape)...  30.1 us
    all_gather x1, waiting for transfers between devices, on_device(): packed = lax.all_gather(mine[:, :, head_width:], 'zy', axis=0, tiled=True)  20.4 us
    all_to_all x1, blocking collectives, on_device(): mine = lax.all_to_all(per_head, 'x', 0, 0, tiled=True)  13.5 us
    all_gather x1, blocking collectives, on_device(): gathered = lax.all_gather(tokens, 'head', axis=0, tiled=True)  10.7 us
    dot_general x1, matrix products, on_device(): jnp.dot(inner, w_down, preferred_element_type=jnp.float32) + second  10 us
    all_gather x1, blocking collectives, on_device(): block_output = lax.all_gather(output_b, 'head', axis=0, tiled=True)  8.7 us
    pallas_call x1, Pallas kernels, flash(): pl.pallas_call(kernel, out_shape=jax.ShapeDtypeStruct(queries.shape, jnp....  8.19 us
  transfers between devices with their start and end apart: 8, of which 5 were waited for; matrix products, arithmetic and copies ran while one was open for 12% of the time, Pallas kernels for 20%

profile of v14, /device:TPU:1, one launch (start us, length us, event | category | flops | bytes accessed | tf_op | source)
XLA Modules:
  0.0 233.4 jit_solution(1081138130792821913)
XLA Ops:
  7.2 10.7 %all_gather.12 = bf16[384,1024]{1,0:T(8,128)(2,1)S(1)} all-gather(bf16[96,1024]{1,0:T(8,128)(2,1)} %param.12), channel_id=1, replica_groups=mesh['zy'=8,'x'=4,'head'=4] {'head'}, dimensions={0}, use_global_device_ids=true | all-gather | bytes 983040 | tf_op jit(solution)/shard_map/all_gather | solution.py:359
  17.9 2.4 %convolution_convert_fusion = bf16[3,256,384]{2,1,0:T(8,128)(2,1)S(1)} fusion(bf16[3,1024,256]{2,1,0:T(8,128)(2,1)} %param.16, bf16[384,1024]{1,0:T(8,128)(2,1)S(1)} %all_gather.12), kind=kOutput, calls=%fused_computation.22 | convolution fusion | flops 604274688 | bytes 2949120 | tf_op jit(solution)/shard_map/td,cde->cte/dot_general | solution.py:360
  20.5 13.5 %all_to_all.35 = bf16[4,384,192]{1,2,0:T(8,128)(2,1)S(1)} all-to-all(bf16[4,384,192]{1,2,0:T(8,128)(2,1)S(1)} %bitcast.73), channel_id=1, replica_groups=mesh['zy'=8,'x'=4,'head'=4] {'x'}, dimensions={0} | all-to-all | bytes 1179648 | tf_op jit(solution)/shard_map/all_to_all | solution.py:371
  35.7 3.4 %all-to-all-start.2 = ((bf16[4,2,64,256]{3,2,1,0:T(8,128)(2,1)}), bf16[4,2,64,256]{3,2,1,0:T(8,128)(2,1)S(1)}, u32[]{:S(2)}, u32[]{:S(2)}) async-start(bf16[4,2,64,256]{3,2,1,0:T(8,128)(2,1)} %broadcast_in_dim.123), calls=%async_computation.2 | async-start | bytes 524288 | tf_op jit(solution)/shard_map/all_to_all | solution.py:374
  47.6 1.6 broadcast_in_dim.122
  49.3 6.0 %all-to-all-start.1 = ((bf16[4,256,1024]{2,1,0:T(8,128)(2,1)}), bf16[4,256,1024]{2,1,0:T(8,128)(2,1)}, u32[]{:S(2)}, u32[]{:S(2)}) async-start(bf16[4,256,1024]{2,1,0:T(8,128)(2,1)} %broadcast_in_dim.122), calls=%async_computation.1 | async-start | bytes 4194304 | tf_op jit(solution)/shard_map/all_to_all | solution.py:356
  56.5 1.2 select_reduce_fusion
  58.5 30.1 %all-to-all-done.1 = bf16[4,256,1024]{2,1,0:T(8,128)(2,1)} async-done(((bf16[4,256,1024]{2,1,0:T(8,128)(2,1)}), bf16[4,256,1024]{2,1,0:T(8,128)(2,1)}, u32[]{:S(2)}, u32[]{:S(2)}) %all-to-all-start.1) | async-done | bytes 2097184 | tf_op jit(solution)/shard_map/all_to_all | solution.py:356
  88.6 20.4 %all-gather.3.cloned.1.call-done = bf16[32,384,128]{2,1,0:T(8,128)(2,1)} async-done(((bf16[4,384,128]{2,1,0:T(8,128)(2,1)}), bf16[32,384,128]{2,1,0:T(8,128)(2,1)}) %all-gather.3.cloned.1.call-update) | async-done | bytes 3145744 | tf_op jit(solution)/shard_map/all_gather | solution.py:372
  116.8 38.1 %shard_map.139 = bf16[8,192,64]{2,1,0:T(8,128)(2,1)} custom-call(s32[8]{0:T(128)} %get-tuple-element.27.steps_ref, s32[512]{0:T(512)} %mul.189.sources_ref, s32[64]{0:T(128)} %mul.192.bases_ref, s32[16]{0:T(128)} %reshape.413.limits_ref, bf16[8,192,64]{2,1,0:T(8,128)(2,1)} %bitcast.84, s32[8,192,1]{2,1,0:T(8,128)} %copy.70.low_ref, ...), custom_call_target="tpu_custom_call" | custom-call | flops 2415919104 | bytes 12582912 | tf_op jit(solution)/shard_map/pallas_call | solution.py:304
  154.9 1.9 copy.71
  156.8 6.0 %all-to-all-start.3 = ((bf16[16,96,64]{1,2,0:T(8,128)(2,1)}), bf16[16,96,64]{1,2,0:T(8,128)(2,1)S(1)}, u32[]{:S(2)}, u32[]{:S(2)}) async-start(bf16[16,96,64]{1,2,0:T(8,128)(2,1)} %copy.71), calls=%async_computation.3 | async-start | bytes 524288 | tf_op jit(solution)/shard_map/all_to_all | solution.py:411
  164.7 5.5 %all-to-all-done.3 = bf16[16,96,64]{1,2,0:T(8,128)(2,1)S(1)} async-done(((bf16[16,96,64]{1,2,0:T(8,128)(2,1)}), bf16[16,96,64]{1,2,0:T(8,128)(2,1)S(1)}, u32[]{:S(2)}, u32[]{:S(2)}) %all-to-all-start.3) | async-done | bytes 196640 | tf_op jit(solution)/shard_map/all_to_all | solution.py:411
  170.2 2.3 %fusion.96 = (f32[96]{0:T(128)S(1)}, f32[96,1024]{1,0:T(8,128)S(1)}) fusion(bf16[96,1024]{1,0:T(8,128)(2,1)S(1)} %copy-done.3, bf16[96,1024]{0,1:T(8,128)(2,1)S(1)} %bitcast.76, bf16[1024,1024]{1,0:T(8,128)(2,1)} %bitcast.9), kind=kOutput, calls=%fused_computation.182 | convolution fusion | flops 201621408 | bytes 2883968 | tf_op jit(solution)/shard_map/dot_general | solution.py:439
  174.0 3.7 %all-to-all-start.4 = ((bf16[4,96,256]{2,1,0:T(8,128)(2,1)}), bf16[4,96,256]{2,1,0:T(8,128)(2,1)S(1)}, u32[]{:S(2)}, u32[]{:S(2)}) async-start(bf16[4,96,256]{2,1,0:T(8,128)(2,1)} %bitcast.72), calls=%async_computation.4 | async-start | bytes 393216 | tf_op jit(solution)/shard_map/all_to_all | solution.py:443
  177.7 3.2 %fusion.11 = (bf16[2496,256]{1,0:T(8,128)(2,1)}, bf16[2496,256]{1,0:T(8,128)(2,1)}) fusion(bf16[2,2048,256]{2,1,0:T(8,128)(2,1)} %all-gather.5.cloned.1.call-done), kind=kLoop, calls=%fused_computation.24 | loop fusion | bytes 4653056 | tf_op jit(solution)/shard_map/squeeze | solution.py:471
  180.9 1.3 all-to-all-done.4
  182.2 3.5 %all-to-all-start.6 = ((bf16[4,384,128]{2,1,0:T(8,128)(2,1)}), bf16[4,384,128]{2,1,0:T(8,128)(2,1)S(1)}, u32[]{:S(2)}, u32[]{:S(2)}) async-start(bf16[4,384,128]{2,1,0:T(8,128)(2,1)} %pad_maximum_fusion), calls=%async_computation.6 | async-start | bytes 786432 | tf_op jit(solution)/shard_map/all_to_all | solution.py:436
  185.7 8.2 %shard_map.140 = bf16[2,192,256]{2,1,0:T(8,128)(2,1)} custom-call(s32[2]{0:T(128)} %and_select_fusion.2.steps_ref, s32[24]{0:T(128)} %reshape.412.sources_ref, s32[12]{0:T(128)} %min.32.bases_ref, bf16[2,192,256]{2,1,0:T(8,128)(2,1)} %bitcast.86, s32[2,192,1]{2,1,0:T(8,128)} %reshape.431.low_ref, s32[2,192,1]{2,1,0:T(8,128)} %sub.88.high_ref, ...), custom_call_target="tpu_custom_call" | custom-call | flops 3623878656 | bytes 4718592 | tf_op jit(solution)/shard_map/pallas_call | solution.py:191
  193.9 4.2 %all-to-all-start.5 = ((bf16[4,96,256]{2,1,0:T(8,128)(2,1)}), bf16[4,96,256]{2,1,0:T(8,128)(2,1)S(1)}, u32[]{:S(2)}, u32[]{:S(2)}) async-start(bf16[4,96,256]{2,1,0:T(8,128)(2,1)} %bitcast.87), calls=%async_computation.5 | async-start | bytes 393216 | tf_op jit(solution)/shard_map/all_to_all | solution.py:478
  199.3 3.3 %all-to-all-done.5 = bf16[4,96,256]{2,1,0:T(8,128)(2,1)S(1)} async-done(((bf16[4,96,256]{2,1,0:T(8,128)(2,1)}), bf16[4,96,256]{2,1,0:T(8,128)(2,1)S(1)}, u32[]{:S(2)}, u32[]{:S(2)}) %all-to-all-start.5) | async-done | bytes 196640 | tf_op jit(solution)/shard_map/all_to_all | solution.py:478
  205.0 10.0 %fusion.98 = (f32[96]{0:T(128)S(1)}, f32[96,1024]{1,0:T(8,128)S(1)}) fusion(f32[96]{0:T(128)S(1)} %add_rsqrt_fusion.1, f32[96,1024]{1,0:T(8,128)S(1)} %get-tuple-element.55, f32[96]{0:T(128)S(1)} %broadcast_multiply_fusion.3, bf16[4096,1024]{1,0:T(8,128)(2,1)} %param.22, bf16[1024,4096]{1,0:T(8,128)(2,1)} %param.21), kind=kOutput, calls=%fused_computation.184 | convolution fusion | flops 1636859776 | bytes 17564800 | tf_op jit(solution)/shard_map/dot_general | solution.py:488
  216.1 8.7 %all_gather.15 = bf16[384,1024]{1,0:T(8,128)(2,1)S(1)} all-gather(bf16[96,1024]{1,0:T(8,128)(2,1)S(1)} %get-tuple-element.25), channel_id=1, replica_groups=mesh['zy'=8,'x'=4,'head'=4] {'head'}, dimensions={0}, use_global_device_ids=true | all-gather | bytes 983040 | tf_op jit(solution)/shard_map/all_gather | solution.py:490
  224.8 1.8 convolution_bitcast_fusion
  (104 shorter events, 23.1 us)
Async XLA Ops:
  7.2 197.0 %copy-start = (bf16[1024,1024]{1,0:T(8,128)(2,1)S(1)}, bf16[1024,1024]{1,0:T(8,128)(2,1)}, u32[]{:S(2)}) copy-start(bf16[1024,1024]{1,0:T(8,128)(2,1)} %param.20) | copy-start | bytes 6291460
  7.2 101.8 %all-gather.3.cloned.1.call-start = ((), (), s32[]{:S(2)}) async-start(), calls=%async_computation.7 | async-start | bytes 3538944 | tf_op jit(solution)/shard_map/all_gather | solution.py:372
  20.4 14.5 %copy-start.6 = (bf16[2,64,256]{2,1,0:T(8,128)(2,1)S(1)}, bf16[2,64,256]{2,1,0:T(8,128)(2,1)}, u32[]{:S(2)}) copy-start(bf16[2,64,256]{2,1,0:T(8,128)(2,1)} %param.18) | copy-start | bytes 196612
  34.0 5.2 %copy-start.8 = (s32[9]{0:T(128)S(1)}, s32[9]{0:T(128)}, u32[]{:S(2)}) copy-start(s32[9]{0:T(128)} %param.14) | copy-start | bytes 112
  34.0 5.4 %copy-start.7 = (s32[64]{0:T(128)S(1)}, s32[64]{0:T(128)}, u32[]{:S(2)}) copy-start(s32[64]{0:T(128)} %param.13) | copy-start | bytes 772
  34.0 5.8 %copy-start.9 = (s32[9]{0:T(128)S(1)}, s32[9]{0:T(128)}, u32[]{:S(2)}) copy-start(s32[9]{0:T(128)} %param.15) | copy-start | bytes 112
  34.9 12.7 %copy-start.4 = (bf16[256,1024]{1,0:T(8,128)(2,1)S(1)}, bf16[256,1024]{1,0:T(8,128)(2,1)}, u32[]{:S(2)}) copy-start(bf16[256,1024]{1,0:T(8,128)(2,1)} %param.17) | copy-start | bytes 1572868
  35.7 11.9 %all-to-all-start.2 = ((bf16[4,2,64,256]{3,2,1,0:T(8,128)(2,1)}), bf16[4,2,64,256]{3,2,1,0:T(8,128)(2,1)S(1)}, u32[]{:S(2)}, u32[]{:S(2)}) async-start(bf16[4,2,64,256]{3,2,1,0:T(8,128)(2,1)} %broadcast_in_dim.123), calls=%async_computation.2 | async-start | bytes 524288 | tf_op jit(solution)/shard_map/all_to_all | solution.py:374
  49.3 39.3 %all-to-all-start.1 = ((bf16[4,256,1024]{2,1,0:T(8,128)(2,1)}), bf16[4,256,1024]{2,1,0:T(8,128)(2,1)}, u32[]{:S(2)}, u32[]{:S(2)}) async-start(bf16[4,256,1024]{2,1,0:T(8,128)(2,1)} %broadcast_in_dim.122), calls=%async_computation.1 | async-start | bytes 4194304 | tf_op jit(solution)/shard_map/all_to_all | solution.py:356
  55.2 122.5 %all-gather.5.cloned.1.call-start = ((), (), s32[]{:S(2)}) async-start(), calls=%async_computation.8 | async-start | bytes 2359296 | tf_op jit(solution)/shard_map/all_gather | solution.py:381
  156.8 13.4 %all-to-all-start.3 = ((bf16[16,96,64]{1,2,0:T(8,128)(2,1)}), bf16[16,96,64]{1,2,0:T(8,128)(2,1)S(1)}, u32[]{:S(2)}, u32[]{:S(2)}) async-start(bf16[16,96,64]{1,2,0:T(8,128)(2,1)} %copy.71), calls=%async_computation.3 | async-start | bytes 524288 | tf_op jit(solution)/shard_map/all_to_all | solution.py:411
  162.8 7.4 %copy-start.3 = (bf16[96,1024]{1,0:T(8,128)(2,1)S(1)}, bf16[96,1024]{1,0:T(8,128)(2,1)}, u32[]{:S(2)}) copy-start(bf16[96,1024]{1,0:T(8,128)(2,1)} %param.12) | copy-start | bytes 589828
  170.2 2.6 %copy-start.1 = (bf16[1024,1024]{1,0:T(8,128)(2,1)S(1)}, bf16[1024,1024]{1,0:T(8,128)(2,1)}, u32[]{:S(2)}) copy-start(bf16[1024,1024]{1,0:T(8,128)(2,1)} %param.19) | copy-start | bytes 6291460
  174.0 8.2 %all-to-all-start.4 = ((bf16[4,96,256]{2,1,0:T(8,128)(2,1)}), bf16[4,96,256]{2,1,0:T(8,128)(2,1)S(1)}, u32[]{:S(2)}, u32[]{:S(2)}) async-start(bf16[4,96,256]{2,1,0:T(8,128)(2,1)} %bitcast.72), calls=%async_computation.4 | async-start | bytes 393216 | tf_op jit(solution)/shard_map/all_to_all | solution.py:443
  182.2 3.5 %copy-start.5 = (bf16[4,96,256]{2,1,0:T(8,128)(2,1)}, bf16[4,96,256]{2,1,0:T(8,128)(2,1)S(1)}, u32[]{:S(2)}) copy-start(bf16[4,96,256]{2,1,0:T(8,128)(2,1)S(1)} %all-to-all-done.4) | copy-start | bytes 589828
  182.2 11.7 %all-to-all-start.6 = ((bf16[4,384,128]{2,1,0:T(8,128)(2,1)}), bf16[4,384,128]{2,1,0:T(8,128)(2,1)S(1)}, u32[]{:S(2)}, u32[]{:S(2)}) async-start(bf16[4,384,128]{2,1,0:T(8,128)(2,1)} %pad_maximum_fusion), calls=%async_computation.6 | async-start | bytes 786432 | tf_op jit(solution)/shard_map/all_to_all | solution.py:436
  193.9 8.7 %all-to-all-start.5 = ((bf16[4,96,256]{2,1,0:T(8,128)(2,1)}), bf16[4,96,256]{2,1,0:T(8,128)(2,1)S(1)}, u32[]{:S(2)}, u32[]{:S(2)}) async-start(bf16[4,96,256]{2,1,0:T(8,128)(2,1)} %bitcast.87), calls=%async_computation.5 | async-start | bytes 393216 | tf_op jit(solution)/shard_map/all_to_all | solution.py:478
  202.6 0.7 copy-start.2
  215.0 9.8 %copy-start.10 = (bf16[3,1024,256]{2,1,0:T(8,128)(2,1)S(1)}, bf16[3,1024,256]{2,1,0:T(8,128)(2,1)}, u32[]{:S(2)}) copy-start(bf16[3,1024,256]{2,1,0:T(8,128)(2,1)} %param.23) | copy-start | bytes 4718596
Sparse Core Ops, SparseCore 0:
  35.1 73.8 all-gather.2
  111.3 52.5 all-gather.4
